TPU v7x, 128 devices: a whole 4x4x4 slice. The times are simulated.
128 devices in a mesh: dp: 16 (over z, y), cent: 8 (over x, core).
Axes of the slice: x: 4, y: 4, z: 4, core: 2. Of those that a mesh axis runs over, the one named last changes fastest.
Arguments:
- clip_data: bfloat16 [16384, 4, 16, 192], P(('dp', 'cent')), may hold values from -6 to 6
- frame_counts: int32 [128, 128], P(('dp', 'cent')), may hold values from 1 to 4, 320 in all within a row
- send_list: int32 [128, 128], P(('dp', 'cent')), may hold values from 0 to 127, each once within a row
- cluster_ids: int32 [128, 128], P(('dp', 'cent')), may hold values from 0 to 43813, as said below
- expand_weight: bfloat16 [2, 192, 432], replicated, may hold values from -0.4375 to 0.4375
- depth_kernel: bfloat16 [2, 27, 432], replicated, may hold values from -1.25 to 1.25
- reduce_weight: bfloat16 [2, 432, 192], replicated, may hold values from -0.3125 to 0.3125
- head_weight: bfloat16 [192, 1024], replicated, may hold values from -0.4375 to 0.4375
- centroids: bfloat16 [50000, 1024], P('cent'), may hold values from -6 to 6
Outputs:
- embeddings: bfloat16 [16384, 1024], P(('dp', 'cent'))
- nearest: float32 [16384], P(('dp', 'cent'))
- own_sim: float32 [16384], P(('dp', 'cent'))
- peer_sim: float32 [16384], P(('dp', 'cent'))
Inputs may be any that keep to these rules, and one draw needn't show every extreme that they name: `cluster_ids`: cluster id q is owned by the device with dp index (q % 6250) % 16 and cent index q // 6250. The clips of one device name at most 4 clusters of one owner, and in every draw one owner gets exactly 4 from every device. Only ids with q % 6250 < 64 occur.
All inputs are finite; a program needn't handle non-finite values.
Results may differ from a plain program's by a relative error of at most 0.014.
Values may be sent and summed in bfloat16 or wider, within the bound.
No kernel may reach another device: no remote copies, remote signals or barrier semaphores. Data moves between devices by JAX's collectives and lax.ppermute only.
A program may use at most 128 MiB of HBM per device.

v0:
```python
import jax
import jax.numpy as jnp
from jax import lax
from jax.sharding import PartitionSpec as P

SIDE = 4


def depthwise(hidden, kernel):
    frame_count = hidden.shape[1]
    padded = jnp.pad(hidden, ((0, 0), (1, 1), (1, 1), (1, 1), (0, 0)))
    accumulated = jnp.zeros_like(hidden)
    for shift_t in range(3):
        for shift_y in range(3):
            for shift_x in range(3):
                accumulated = (
                    accumulated
                    + kernel[9 * shift_t + 3 * shift_y + shift_x]
                    * padded[
                        :,
                        shift_t : shift_t + frame_count,
                        shift_y : shift_y + SIDE,
                        shift_x : shift_x + SIDE,
                        :,
                    ]
                )
    return accumulated


def embed_clips(clip_block, length_values, expand_weight, depth_kernel, reduce_weight, head_weight):
    clip_count, frame_count, positions, channels = clip_block.shape
    frame_mask = (
        jnp.arange(frame_count, dtype=jnp.float32)[None, :] < length_values[:, None]
    ).astype(jnp.float32)
    mask_four = frame_mask[:, :, None, None]
    features = clip_block * mask_four.astype(jnp.bfloat16)
    for layer_index in range(expand_weight.shape[0]):
        hidden = jax.nn.relu(
            jnp.dot(
                features.reshape(-1, channels),
                expand_weight[layer_index],
                preferred_element_type=jnp.float32,
            )
        )
        expanded = hidden.shape[-1]
        hidden = (
            hidden.reshape(clip_count, frame_count, SIDE, SIDE, expanded)
            * frame_mask[:, :, None, None, None]
        )
        mixed = depthwise(hidden, depth_kernel[layer_index].astype(jnp.float32))
        activated = (mixed * jax.nn.sigmoid(mixed)).astype(jnp.bfloat16)
        branch = jnp.dot(
            activated.reshape(-1, expanded),
            reduce_weight[layer_index],
            preferred_element_type=jnp.float32,
        )
        branch = branch.reshape(clip_count, frame_count, positions, channels)
        features = (features.astype(jnp.float32) + branch * mask_four).astype(jnp.bfloat16)
    pooled = (
        jnp.sum(features.astype(jnp.float32), axis=(1, 2)) / (length_values * positions)[:, None]
    ).astype(jnp.bfloat16)
    projected = jnp.dot(pooled, head_weight, preferred_element_type=jnp.float32)
    return (
        projected * lax.rsqrt(jnp.sum(projected * projected, axis=1, keepdims=True) + 1e-06)
    ).astype(jnp.bfloat16)


def local(
    clip_data,
    frame_counts,
    send_list,
    cluster_ids,
    expand_weight,
    depth_kernel,
    reduce_weight,
    head_weight,
    centroids,
):
    n_dp = lax.axis_size("dp")
    n_cent = lax.axis_size("cent")
    clip_count = clip_data.shape[0]
    per_peer = clip_count // n_dp
    destination = send_list[0]
    length_list = frame_counts[0]
    rest_shape = clip_data.shape[1:]

    def embed_pair(group_pair):
        return embed_clips(
            group_pair[0],
            group_pair[1].astype(jnp.float32),
            expand_weight,
            depth_kernel,
            reduce_weight,
            head_weight,
        )

    clip_buffer = (
        jnp.zeros_like(clip_data)
        .at[destination]
        .set(clip_data)
        .reshape((per_peer, n_dp) + rest_shape)
    )
    length_buffer = (
        jnp.zeros((clip_count,), jnp.bfloat16)
        .at[destination]
        .set(length_list.astype(jnp.bfloat16))
        .reshape(per_peer, n_dp)
    )
    vectors = lax.map(
        embed_pair,
        (
            lax.all_to_all(clip_buffer, "dp", split_axis=1, concat_axis=1, tiled=True),
            lax.all_to_all(length_buffer, "dp", split_axis=1, concat_axis=1, tiled=True),
        ),
    )
    vectors = vectors.reshape(clip_count, -1)
    panel_size = centroids.shape[0]
    panel_blocks = centroids.reshape(5, panel_size // 5, -1)
    block_rows = lax.all_gather(vectors, "cent", axis=0, tiled=True)

    def visit(running, panel_block):
        scores = jnp.einsum(
            "rd,kd->rk", block_rows, panel_block, preferred_element_type=jnp.float32
        )
        return (jnp.maximum(running, jnp.max(scores, axis=1)), None)

    result, unused = lax.scan(
        visit, jnp.full((block_rows.shape[0],), -jnp.inf, jnp.float32), panel_blocks
    )
    all_best = lax.pmax(result, "cent")
    nearest = lax.dynamic_slice_in_dim(all_best, lax.axis_index("cent") * clip_count, clip_count)
    owner_total = n_dp * n_cent
    capacity = max(2, 4 * clip_count // owner_total)
    given = cluster_ids[0]
    panel_index = given % panel_size
    target = panel_index % n_dp * n_cent + given // panel_size
    slot_list = jnp.arange(clip_count, dtype=jnp.int32)
    earlier = (target[:, None] == target[None, :]) & (slot_list[None, :] < slot_list[:, None])
    position = jnp.sum(earlier.astype(jnp.int32), axis=1)
    width_d = vectors.shape[1]
    send_vectors = (
        jnp.zeros((owner_total, capacity, width_d), jnp.bfloat16).at[target, position].set(vectors)
    )
    label_rows = jnp.stack(
        [panel_index // 64, panel_index % 64, jnp.ones_like(panel_index)], axis=1
    ).astype(jnp.bfloat16)
    labels = (
        jnp.zeros((owner_total, capacity, 3), jnp.bfloat16).at[target, position].set(label_rows)
    )
    arrived_vectors, arrived_labels = (
        lax.all_to_all(send_vectors, ("dp", "cent"), split_axis=0, concat_axis=0, tiled=True),
        lax.all_to_all(labels, ("dp", "cent"), split_axis=0, concat_axis=0, tiled=True),
    )
    slot_total = owner_total * capacity
    member_vectors = arrived_vectors.reshape(slot_total, width_d)
    label_values = arrived_labels.reshape(slot_total, 3).astype(jnp.float32)
    row_index = (label_values[:, 0] * 64.0 + label_values[:, 1]).astype(jnp.int32)
    filled = label_values[:, 2] > 0.5
    centre_rows = centroids[row_index]
    own_values = jnp.sum(
        member_vectors.astype(jnp.float32) * centre_rows.astype(jnp.float32), axis=1
    )
    own_values = jnp.where(filled, own_values, 0.0)
    similarity = jnp.einsum(
        "rd,td->rt", member_vectors, member_vectors, preferred_element_type=jnp.float32
    )
    slots = jnp.arange(slot_total, dtype=jnp.int32)
    same_cluster = (
        (row_index[:, None] == row_index[None, :])
        & filled[:, None]
        & filled[None, :]
        & (slots[:, None] != slots[None, :])
    )
    peer_values = jnp.max(jnp.where(same_cluster, similarity, -1.0), axis=1)
    own_values, peer_values = (
        own_values.reshape(owner_total, capacity),
        peer_values.reshape(owner_total, capacity),
    )
    back_own, back_peer = (
        lax.all_to_all(own_values, ("dp", "cent"), split_axis=0, concat_axis=0, tiled=True),
        lax.all_to_all(peer_values, ("dp", "cent"), split_axis=0, concat_axis=0, tiled=True),
    )
    own_sim = back_own[target, position]
    peer_sim = back_peer[target, position]
    return (vectors, nearest, own_sim, peer_sim)


def solution(mesh):
    placed = (
        P(("dp", "cent"), None, None, None),
        P(("dp", "cent"), None),
        P(("dp", "cent"), None),
        P(("dp", "cent"), None),
        P(),
        P(),
        P(),
        P(),
        P("cent", None),
    )
    return jax.shard_map(
        local,
        mesh=mesh,
        in_specs=placed,
        out_specs=(
            P(("dp", "cent"), None),
            P(("dp", "cent")),
            P(("dp", "cent")),
            P(("dp", "cent")),
        ),
        check_vma=False,
    )
```

profile of v0, /device:TPU:1, one launch (start us, length us, event | category | flops | bytes accessed | tf_op | source)
XLA Modules:
  0.0 623.9 jit_solution(5597285684266068169)
XLA Ops:
  10.6 8.6 %all-to-all-start.1 = ((bf16[8,16,1]{0,2,1:T(2,128)(2,1)}), bf16[8,16,1]{0,2,1:T(2,128)(2,1)S(1)}, u32[]{:S(2)}, u32[]{:S(2)}) async-start(bf16[8,16,1]{0,2,1:T(2,128)(2,1)} %copy.43), calls=%async_computation.1 | async-start | bytes 16384 | tf_op jit(solution)/shard_map/all_to_all | solution.py:113
  19.2 7.7 %copy.41 = bf16[128,4,16,192]{3,2,1,0:T(8,128)(2,1)} copy(bf16[128,4,16,192]{0,3,2,1:T(8,128)(2,1)} %param.13) | data formatting | bytes 6291456 | tf_op args[0]
  29.4 19.6 %scatter_fusion = bf16[128,4,16,192]{3,2,1,0:T(8,128)(2,1)} fusion(bf16[128,4,16,192]{3,2,1,0:T(8,128)(2,1)} %broadcast_in_dim.33, s32[128]{0:T(128)S(1)} %fusion.149, bf16[128,4,16,192]{3,2,1,0:T(8,128)(2,1)} %copy.41), kind=kCustom, calls=%fused_computation.3 | custom fusion | bytes 9437696 | tf_op jit(solution)/shard_map/scatter | solution.py:100
  53.7 6.8 %all-to-all-start = ((bf16[8,16,4,16,192]{4,3,2,0,1:T(8,128)(2,1)}), bf16[8,16,4,16,192]{4,3,2,0,1:T(8,128)(2,1)}, u32[]{:S(2)}, u32[]{:S(2)}) async-start(bf16[8,16,4,16,192]{4,3,2,0,1:T(8,128)(2,1)} %copy.42), calls=%async_computation | async-start | bytes 8388608 | tf_op jit(solution)/shard_map/all_to_all | solution.py:112
  61.4 59.7 %all-to-all-done = bf16[8,16,4,16,192]{4,3,2,0,1:T(8,128)(2,1)} async-done(((bf16[8,16,4,16,192]{4,3,2,0,1:T(8,128)(2,1)}), bf16[8,16,4,16,192]{4,3,2,0,1:T(8,128)(2,1)}, u32[]{:S(2)}, u32[]{:S(2)}) %all-to-all-start) | async-done | bytes 3145760 | tf_op jit(solution)/shard_map/all_to_all | solution.py:112
  121.2 343.8 %while.23 = (s32[]{:T(128)}, bf16[8,16,1024]{2,1,0:T(8,128)(2,1)}, bf16[8,16,4,16,192]{4,3,2,0,1:T(8,128)(2,1)}, bf16[8,16]{1,0:T(8,128)(2,1)}, bf16[2,27,432]{2...) while((s32[]{:T(128)}, bf16[8,16,1024]{2,1,0:T(8,128)(2,1)}, ...), condition=%wide.region_5.6_spmd, body=%wide.region_2.5_spmd.sunk | while | flops 741304320 | bytes 41976544 | solution.py:109
  129.0 12.5 %fusion.202 = bf16[16,4,4,4,432]{4,3,2,1,0:T(4,128)(2,1)S(1)} fusion(f32[16,4,4,4,432]{4,3,2,1,0:T(4,128)S(1)} %broadcast_multiply_fusion.7, f32[432]{0:T(512)S(1)} %bitcast.332, f32[432]{0:T(512)S(1)} %bitcast.333, f32[432]{0:T(512)S(1)} %bitcast.334, f32[432]{0:T(512)S(1)} %bitcast.335, f32[432]{0:T(512)S(1)} %bitcast.336, f32[432]{0:T(512)S(1)} %bitcast.337, ...), kind=kLoop, calls=%fused_computation.165.clone.1 | loop fusion | flops 25657344 | bytes 2700864 | tf_op jit(solution)/shard_map/while/body/eval_jaxpr/convert_element_type | solution.py:51
  148.7 12.5 %fusion.205 = bf16[16,4,4,4,432]{4,3,2,1,0:T(4,128)(2,1)S(1)} fusion(f32[16,4,4,4,432]{4,3,2,1,0:T(4,128)S(1)} %broadcast_multiply_fusion.8, f32[432]{0:T(512)S(1)} %bitcast.359, f32[432]{0:T(512)S(1)} %bitcast.360, f32[432]{0:T(512)S(1)} %bitcast.361, f32[432]{0:T(512)S(1)} %bitcast.362, f32[432]{0:T(512)S(1)} %bitcast.363, f32[432]{0:T(512)S(1)} %bitcast.364, ...), kind=kLoop, calls=%fused_computation.166.clone.1 | loop fusion | flops 25657344 | bytes 2700864 | tf_op jit(solution)/shard_map/while/body/eval_jaxpr/convert_element_type | solution.py:51
  172.0 12.5 %fusion.202 = bf16[16,4,4,4,432]{4,3,2,1,0:T(4,128)(2,1)S(1)} fusion(f32[16,4,4,4,432]{4,3,2,1,0:T(4,128)S(1)} %broadcast_multiply_fusion.7, f32[432]{0:T(512)S(1)} %bitcast.332, f32[432]{0:T(512)S(1)} %bitcast.333, f32[432]{0:T(512)S(1)} %bitcast.334, f32[432]{0:T(512)S(1)} %bitcast.335, f32[432]{0:T(512)S(1)} %bitcast.336, f32[432]{0:T(512)S(1)} %bitcast.337, ...), kind=kLoop, calls=%fused_computation.165.clone.1 | loop fusion | flops 25657344 | bytes 2700864 | tf_op jit(solution)/shard_map/while/body/eval_jaxpr/convert_element_type | solution.py:51
  191.7 12.5 %fusion.205 = bf16[16,4,4,4,432]{4,3,2,1,0:T(4,128)(2,1)S(1)} fusion(f32[16,4,4,4,432]{4,3,2,1,0:T(4,128)S(1)} %broadcast_multiply_fusion.8, f32[432]{0:T(512)S(1)} %bitcast.359, f32[432]{0:T(512)S(1)} %bitcast.360, f32[432]{0:T(512)S(1)} %bitcast.361, f32[432]{0:T(512)S(1)} %bitcast.362, f32[432]{0:T(512)S(1)} %bitcast.363, f32[432]{0:T(512)S(1)} %bitcast.364, ...), kind=kLoop, calls=%fused_computation.166.clone.1 | loop fusion | flops 25657344 | bytes 2700864 | tf_op jit(solution)/shard_map/while/body/eval_jaxpr/convert_element_type | solution.py:51
  215.0 12.5 %fusion.202 = bf16[16,4,4,4,432]{4,3,2,1,0:T(4,128)(2,1)S(1)} fusion(f32[16,4,4,4,432]{4,3,2,1,0:T(4,128)S(1)} %broadcast_multiply_fusion.7, f32[432]{0:T(512)S(1)} %bitcast.332, f32[432]{0:T(512)S(1)} %bitcast.333, f32[432]{0:T(512)S(1)} %bitcast.334, f32[432]{0:T(512)S(1)} %bitcast.335, f32[432]{0:T(512)S(1)} %bitcast.336, f32[432]{0:T(512)S(1)} %bitcast.337, ...), kind=kLoop, calls=%fused_computation.165.clone.1 | loop fusion | flops 25657344 | bytes 2700864 | tf_op jit(solution)/shard_map/while/body/eval_jaxpr/convert_element_type | solution.py:51
  234.7 12.5 %fusion.205 = bf16[16,4,4,4,432]{4,3,2,1,0:T(4,128)(2,1)S(1)} fusion(f32[16,4,4,4,432]{4,3,2,1,0:T(4,128)S(1)} %broadcast_multiply_fusion.8, f32[432]{0:T(512)S(1)} %bitcast.359, f32[432]{0:T(512)S(1)} %bitcast.360, f32[432]{0:T(512)S(1)} %bitcast.361, f32[432]{0:T(512)S(1)} %bitcast.362, f32[432]{0:T(512)S(1)} %bitcast.363, f32[432]{0:T(512)S(1)} %bitcast.364, ...), kind=kLoop, calls=%fused_computation.166.clone.1 | loop fusion | flops 25657344 | bytes 2700864 | tf_op jit(solution)/shard_map/while/body/eval_jaxpr/convert_element_type | solution.py:51
  258.0 12.5 %fusion.202 = bf16[16,4,4,4,432]{4,3,2,1,0:T(4,128)(2,1)S(1)} fusion(f32[16,4,4,4,432]{4,3,2,1,0:T(4,128)S(1)} %broadcast_multiply_fusion.7, f32[432]{0:T(512)S(1)} %bitcast.332, f32[432]{0:T(512)S(1)} %bitcast.333, f32[432]{0:T(512)S(1)} %bitcast.334, f32[432]{0:T(512)S(1)} %bitcast.335, f32[432]{0:T(512)S(1)} %bitcast.336, f32[432]{0:T(512)S(1)} %bitcast.337, ...), kind=kLoop, calls=%fused_computation.165.clone.1 | loop fusion | flops 25657344 | bytes 2700864 | tf_op jit(solution)/shard_map/while/body/eval_jaxpr/convert_element_type | solution.py:51
  277.6 12.5 %fusion.205 = bf16[16,4,4,4,432]{4,3,2,1,0:T(4,128)(2,1)S(1)} fusion(f32[16,4,4,4,432]{4,3,2,1,0:T(4,128)S(1)} %broadcast_multiply_fusion.8, f32[432]{0:T(512)S(1)} %bitcast.359, f32[432]{0:T(512)S(1)} %bitcast.360, f32[432]{0:T(512)S(1)} %bitcast.361, f32[432]{0:T(512)S(1)} %bitcast.362, f32[432]{0:T(512)S(1)} %bitcast.363, f32[432]{0:T(512)S(1)} %bitcast.364, ...), kind=kLoop, calls=%fused_computation.166.clone.1 | loop fusion | flops 25657344 | bytes 2700864 | tf_op jit(solution)/shard_map/while/body/eval_jaxpr/convert_element_type | solution.py:51
  300.9 12.5 %fusion.202 = bf16[16,4,4,4,432]{4,3,2,1,0:T(4,128)(2,1)S(1)} fusion(f32[16,4,4,4,432]{4,3,2,1,0:T(4,128)S(1)} %broadcast_multiply_fusion.7, f32[432]{0:T(512)S(1)} %bitcast.332, f32[432]{0:T(512)S(1)} %bitcast.333, f32[432]{0:T(512)S(1)} %bitcast.334, f32[432]{0:T(512)S(1)} %bitcast.335, f32[432]{0:T(512)S(1)} %bitcast.336, f32[432]{0:T(512)S(1)} %bitcast.337, ...), kind=kLoop, calls=%fused_computation.165.clone.1 | loop fusion | flops 25657344 | bytes 2700864 | tf_op jit(solution)/shard_map/while/body/eval_jaxpr/convert_element_type | solution.py:51
  320.6 12.5 %fusion.205 = bf16[16,4,4,4,432]{4,3,2,1,0:T(4,128)(2,1)S(1)} fusion(f32[16,4,4,4,432]{4,3,2,1,0:T(4,128)S(1)} %broadcast_multiply_fusion.8, f32[432]{0:T(512)S(1)} %bitcast.359, f32[432]{0:T(512)S(1)} %bitcast.360, f32[432]{0:T(512)S(1)} %bitcast.361, f32[432]{0:T(512)S(1)} %bitcast.362, f32[432]{0:T(512)S(1)} %bitcast.363, f32[432]{0:T(512)S(1)} %bitcast.364, ...), kind=kLoop, calls=%fused_computation.166.clone.1 | loop fusion | flops 25657344 | bytes 2700864 | tf_op jit(solution)/shard_map/while/body/eval_jaxpr/convert_element_type | solution.py:51
  343.9 12.5 %fusion.202 = bf16[16,4,4,4,432]{4,3,2,1,0:T(4,128)(2,1)S(1)} fusion(f32[16,4,4,4,432]{4,3,2,1,0:T(4,128)S(1)} %broadcast_multiply_fusion.7, f32[432]{0:T(512)S(1)} %bitcast.332, f32[432]{0:T(512)S(1)} %bitcast.333, f32[432]{0:T(512)S(1)} %bitcast.334, f32[432]{0:T(512)S(1)} %bitcast.335, f32[432]{0:T(512)S(1)} %bitcast.336, f32[432]{0:T(512)S(1)} %bitcast.337, ...), kind=kLoop, calls=%fused_computation.165.clone.1 | loop fusion | flops 25657344 | bytes 2700864 | tf_op jit(solution)/shard_map/while/body/eval_jaxpr/convert_element_type | solution.py:51
  363.6 12.5 %fusion.205 = bf16[16,4,4,4,432]{4,3,2,1,0:T(4,128)(2,1)S(1)} fusion(f32[16,4,4,4,432]{4,3,2,1,0:T(4,128)S(1)} %broadcast_multiply_fusion.8, f32[432]{0:T(512)S(1)} %bitcast.359, f32[432]{0:T(512)S(1)} %bitcast.360, f32[432]{0:T(512)S(1)} %bitcast.361, f32[432]{0:T(512)S(1)} %bitcast.362, f32[432]{0:T(512)S(1)} %bitcast.363, f32[432]{0:T(512)S(1)} %bitcast.364, ...), kind=kLoop, calls=%fused_computation.166.clone.1 | loop fusion | flops 25657344 | bytes 2700864 | tf_op jit(solution)/shard_map/while/body/eval_jaxpr/convert_element_type | solution.py:51
  386.9 12.5 %fusion.202 = bf16[16,4,4,4,432]{4,3,2,1,0:T(4,128)(2,1)S(1)} fusion(f32[16,4,4,4,432]{4,3,2,1,0:T(4,128)S(1)} %broadcast_multiply_fusion.7, f32[432]{0:T(512)S(1)} %bitcast.332, f32[432]{0:T(512)S(1)} %bitcast.333, f32[432]{0:T(512)S(1)} %bitcast.334, f32[432]{0:T(512)S(1)} %bitcast.335, f32[432]{0:T(512)S(1)} %bitcast.336, f32[432]{0:T(512)S(1)} %bitcast.337, ...), kind=kLoop, calls=%fused_computation.165.clone.1 | loop fusion | flops 25657344 | bytes 2700864 | tf_op jit(solution)/shard_map/while/body/eval_jaxpr/convert_element_type | solution.py:51
  406.5 12.5 %fusion.205 = bf16[16,4,4,4,432]{4,3,2,1,0:T(4,128)(2,1)S(1)} fusion(f32[16,4,4,4,432]{4,3,2,1,0:T(4,128)S(1)} %broadcast_multiply_fusion.8, f32[432]{0:T(512)S(1)} %bitcast.359, f32[432]{0:T(512)S(1)} %bitcast.360, f32[432]{0:T(512)S(1)} %bitcast.361, f32[432]{0:T(512)S(1)} %bitcast.362, f32[432]{0:T(512)S(1)} %bitcast.363, f32[432]{0:T(512)S(1)} %bitcast.364, ...), kind=kLoop, calls=%fused_computation.166.clone.1 | loop fusion | flops 25657344 | bytes 2700864 | tf_op jit(solution)/shard_map/while/body/eval_jaxpr/convert_element_type | solution.py:51
  429.8 12.5 %fusion.202 = bf16[16,4,4,4,432]{4,3,2,1,0:T(4,128)(2,1)S(1)} fusion(f32[16,4,4,4,432]{4,3,2,1,0:T(4,128)S(1)} %broadcast_multiply_fusion.7, f32[432]{0:T(512)S(1)} %bitcast.332, f32[432]{0:T(512)S(1)} %bitcast.333, f32[432]{0:T(512)S(1)} %bitcast.334, f32[432]{0:T(512)S(1)} %bitcast.335, f32[432]{0:T(512)S(1)} %bitcast.336, f32[432]{0:T(512)S(1)} %bitcast.337, ...), kind=kLoop, calls=%fused_computation.165.clone.1 | loop fusion | flops 25657344 | bytes 2700864 | tf_op jit(solution)/shard_map/while/body/eval_jaxpr/convert_element_type | solution.py:51
  449.5 12.5 %fusion.205 = bf16[16,4,4,4,432]{4,3,2,1,0:T(4,128)(2,1)S(1)} fusion(f32[16,4,4,4,432]{4,3,2,1,0:T(4,128)S(1)} %broadcast_multiply_fusion.8, f32[432]{0:T(512)S(1)} %bitcast.359, f32[432]{0:T(512)S(1)} %bitcast.360, f32[432]{0:T(512)S(1)} %bitcast.361, f32[432]{0:T(512)S(1)} %bitcast.362, f32[432]{0:T(512)S(1)} %bitcast.363, f32[432]{0:T(512)S(1)} %bitcast.364, ...), kind=kLoop, calls=%fused_computation.166.clone.1 | loop fusion | flops 25657344 | bytes 2700864 | tf_op jit(solution)/shard_map/while/body/eval_jaxpr/convert_element_type | solution.py:51
  468.2 13.4 %scatter_fusion.1 = bf16[128,4,3]{2,1,0:T(4,128)(2,1)} fusion(bf16[128,4,3]{2,1,0:T(4,128)(2,1)} %broadcast_in_dim.37, s32[128]{0:T(128)S(1)} %fusion.151, bf16[128,3]{1,0:T(8,128)(2,1)S(1)} %copy.46), kind=kCustom, calls=%fused_computation.5 | custom fusion | bytes 3328 | tf_op jit(solution)/shard_map/scatter | solution.py:148
  481.6 9.5 %all-to-all-start.2 = ((bf16[128,4,3]{2,1,0:T(4,128)(2,1)}), bf16[128,4,3]{2,1,0:T(4,128)(2,1)S(1)}, u32[]{:S(2)}, u32[]{:S(2)}) async-start(bf16[128,4,3]{2,1,0:T(4,128)(2,1)} %scatter_fusion.1), calls=%async_computation.2 | async-start | bytes 262144 | tf_op jit(solution)/shard_map/all_to_all | solution.py:152
  492.3 18.2 %scatter_fusion.2 = bf16[128,4,1024]{2,1,0:T(4,128)(2,1)} fusion(bf16[128,4,1024]{2,1,0:T(4,128)(2,1)} %broadcast_in_dim.38, s32[128]{0:T(128)S(1)} %fusion.151, bf16[128,1024]{1,0:T(8,128)(2,1)S(1)} %bitcast.322), kind=kCustom, calls=%fused_computation.6 | custom fusion | bytes 787456 | tf_op jit(solution)/shard_map/scatter | solution.py:142
  510.5 9.8 %all-to-all-start.3 = ((bf16[128,4,1024]{2,1,0:T(4,128)(2,1)}), bf16[128,4,1024]{2,1,0:T(4,128)(2,1)S(1)}, u32[]{:S(2)}, u32[]{:S(2)}) async-start(bf16[128,4,1024]{2,1,0:T(4,128)(2,1)} %scatter_fusion.2), calls=%async_computation.3 | async-start | bytes 2097152 | tf_op jit(solution)/shard_map/all_to_all | solution.py:151
  521.0 9.8 %gather_fusion = bf16[512,1024]{1,0:T(8,128)(2,1)} fusion(bf16[6250,1024]{1,0:T(8,128)(2,1)} %param.21, s32[1024]{0:T(1024)S(1)} %pad_clamp_fusion), kind=kCustom, calls=%fused_computation | custom fusion | bytes 2099200 | tf_op jit(solution)/shard_map/gather | solution.py:159
  532.5 7.0 %all-to-all-done.3 = bf16[128,4,1024]{2,1,0:T(4,128)(2,1)S(1)} async-done(((bf16[128,4,1024]{2,1,0:T(4,128)(2,1)}), bf16[128,4,1024]{2,1,0:T(4,128)(2,1)S(1)}, u32[]{:S(2)}, u32[]{:S(2)}) %all-to-all-start.3) | async-done | bytes 1048608 | tf_op jit(solution)/shard_map/all_to_all | solution.py:151
  547.1 7.8 %all-to-all-done.4 = f32[128,1,4]{2,1,0:T(1,128)S(1)} async-done(((f32[128,1,4]{2,1,0:T(1,128)}), f32[128,1,4]{2,1,0:T(1,128)S(1)}, u32[]{:S(2)}, u32[]{:S(2)}) %all-to-all-start.4) | async-done | bytes 2080 | tf_op jit(solution)/shard_map/all_to_all | solution.py:180
  559.5 13.8 %reshape.613 = bf16[5,1250,1024]{2,1,0:T(8,128)(2,1)} reshape(bf16[6250,1024]{1,0:T(8,128)(2,1)} %param.21) | data formatting | bytes 25600000 | tf_op jit(solution)/shard_map/reshape | solution.py:118
  576.9 26.5 %while.24 = (s32[]{:T(128)}, f32[1024]{0:T(1024)S(1)}, bf16[5,1250,1024]{2,1,0:T(8,128)(2,1)}, bf16[1024,1024]{1,0:T(8,128)(2,1)}, s32[]{:T(128)}, /*index=5*/s32[]{:T(128)}) while((s32[]{:T(128)}, f32[1024]{0:T(1024)S(1)}, bf16[5,1250,1024]{2,1,0:T(8,128)(2,1)}, bf16[1024,1024]{1,0:T(8,128)(2,1)}, s32[]{:T(128)}, ...), condition=%wide.region_8.9_spmd.clone, body=%wide.region_6.8_spmd.clone.sunk | while | flops 2622721024 | bytes 4685915 | solution.py:127
  603.4 13.1 %pmax.7 = f32[1024]{0:T(1024)S(1)} all-reduce(f32[1024]{0:T(1024)S(1)} %get-tuple-element.128), channel_id=1, replica_groups=mesh['dp'=16,'cent'=8] {'cent'}, use_global_device_ids=true, to_apply=%region_9.10 | all-reduce | flops 1024 | bytes 8192 | tf_op jit(solution)/shard_map/pmax | solution.py:130
  (320 shorter events, 203.1 us)
Async XLA Ops:
  10.6 43.1 %all-to-all-start.1 = ((bf16[8,16,1]{0,2,1:T(2,128)(2,1)}), bf16[8,16,1]{0,2,1:T(2,128)(2,1)S(1)}, u32[]{:S(2)}, u32[]{:S(2)}) async-start(bf16[8,16,1]{0,2,1:T(2,128)(2,1)} %copy.43), calls=%async_computation.1 | async-start | bytes 16384 | tf_op jit(solution)/shard_map/all_to_all | solution.py:113
  53.7 67.4 %copy-start = (bf16[2,192,432]{2,1,0:T(8,128)(2,1)S(1)}, bf16[2,192,432]{2,1,0:T(8,128)(2,1)}, u32[]{:S(2)}) copy-start(bf16[2,192,432]{2,1,0:T(8,128)(2,1)} %param.17) | copy-start | bytes 995332
  53.7 67.4 %copy-start.1 = (bf16[192,1024]{1,0:T(8,128)(2,1)S(1)}, bf16[192,1024]{1,0:T(8,128)(2,1)}, u32[]{:S(2)}) copy-start(bf16[192,1024]{1,0:T(8,128)(2,1)} %param.20) | copy-start | bytes 1179652
  53.7 67.4 %copy-start.2 = (bf16[2,27,432]{2,0,1:T(2,128)(2,1)S(1)}, bf16[2,27,432]{2,0,1:T(2,128)(2,1)}, u32[]{:S(2)}) copy-start(bf16[2,27,432]{2,0,1:T(2,128)(2,1)} %param.18) | copy-start | bytes 139972
  53.7 67.4 %all-to-all-start = ((bf16[8,16,4,16,192]{4,3,2,0,1:T(8,128)(2,1)}), bf16[8,16,4,16,192]{4,3,2,0,1:T(8,128)(2,1)}, u32[]{:S(2)}, u32[]{:S(2)}) async-start(bf16[8,16,4,16,192]{4,3,2,0,1:T(8,128)(2,1)} %copy.42), calls=%async_computation | async-start | bytes 8388608 | tf_op jit(solution)/shard_map/all_to_all | solution.py:112
  60.5 516.4 %all-gather.2.cloned.1.call-start = ((), (), s32[]{:S(2)}) async-start(), calls=%async_computation.6 | async-start | bytes 2359296 | tf_op jit(solution)/shard_map/all_gather | solution.py:119
  148.0 0.7 copy-start.6
  148.7 13.1 %copy-start.8 = (bf16[2,432,192]{1,2,0:T(8,128)(2,1)S(1)}, bf16[2,432,192]{1,2,0:T(8,128)(2,1)}, u32[]{:S(2)}) copy-start(bf16[2,432,192]{1,2,0:T(8,128)(2,1)} %get-tuple-element.488) | copy-start | bytes 995332 | tf_op jit(solution)/shard_map/while
  161.2 1.9 copy-start.7
  191.0 0.7 copy-start.6
  191.7 13.1 %copy-start.8 = (bf16[2,432,192]{1,2,0:T(8,128)(2,1)S(1)}, bf16[2,432,192]{1,2,0:T(8,128)(2,1)}, u32[]{:S(2)}) copy-start(bf16[2,432,192]{1,2,0:T(8,128)(2,1)} %get-tuple-element.488) | copy-start | bytes 995332 | tf_op jit(solution)/shard_map/while
  204.2 1.9 copy-start.7
  234.0 0.7 copy-start.6
  234.7 13.1 %copy-start.8 = (bf16[2,432,192]{1,2,0:T(8,128)(2,1)S(1)}, bf16[2,432,192]{1,2,0:T(8,128)(2,1)}, u32[]{:S(2)}) copy-start(bf16[2,432,192]{1,2,0:T(8,128)(2,1)} %get-tuple-element.488) | copy-start | bytes 995332 | tf_op jit(solution)/shard_map/while
  247.2 1.9 copy-start.7
  276.9 0.7 copy-start.6
  277.6 13.1 %copy-start.8 = (bf16[2,432,192]{1,2,0:T(8,128)(2,1)S(1)}, bf16[2,432,192]{1,2,0:T(8,128)(2,1)}, u32[]{:S(2)}) copy-start(bf16[2,432,192]{1,2,0:T(8,128)(2,1)} %get-tuple-element.488) | copy-start | bytes 995332 | tf_op jit(solution)/shard_map/while
  290.1 1.9 copy-start.7
  319.9 0.7 copy-start.6
  320.6 13.1 %copy-start.8 = (bf16[2,432,192]{1,2,0:T(8,128)(2,1)S(1)}, bf16[2,432,192]{1,2,0:T(8,128)(2,1)}, u32[]{:S(2)}) copy-start(bf16[2,432,192]{1,2,0:T(8,128)(2,1)} %get-tuple-element.488) | copy-start | bytes 995332 | tf_op jit(solution)/shard_map/while
  333.1 1.9 copy-start.7
  363.6 13.1 %copy-start.8 = (bf16[2,432,192]{1,2,0:T(8,128)(2,1)S(1)}, bf16[2,432,192]{1,2,0:T(8,128)(2,1)}, u32[]{:S(2)}) copy-start(bf16[2,432,192]{1,2,0:T(8,128)(2,1)} %get-tuple-element.488) | copy-start | bytes 995332 | tf_op jit(solution)/shard_map/while
  376.1 1.9 copy-start.7
  406.5 13.1 %copy-start.8 = (bf16[2,432,192]{1,2,0:T(8,128)(2,1)S(1)}, bf16[2,432,192]{1,2,0:T(8,128)(2,1)}, u32[]{:S(2)}) copy-start(bf16[2,432,192]{1,2,0:T(8,128)(2,1)} %get-tuple-element.488) | copy-start | bytes 995332 | tf_op jit(solution)/shard_map/while
  419.1 1.9 copy-start.7
  449.5 13.1 %copy-start.8 = (bf16[2,432,192]{1,2,0:T(8,128)(2,1)S(1)}, bf16[2,432,192]{1,2,0:T(8,128)(2,1)}, u32[]{:S(2)}) copy-start(bf16[2,432,192]{1,2,0:T(8,128)(2,1)} %get-tuple-element.488) | copy-start | bytes 995332 | tf_op jit(solution)/shard_map/while
  462.0 1.9 copy-start.7
  465.0 27.3 %copy-start.3 = (bf16[8,16,1024]{2,1,0:T(8,128)(2,1)S(1)}, bf16[8,16,1024]{2,1,0:T(8,128)(2,1)}, u32[]{:S(2)}) copy-start(bf16[8,16,1024]{2,1,0:T(8,128)(2,1)} %get-tuple-element.127) | copy-start | bytes 786436
  481.6 28.9 %all-to-all-start.2 = ((bf16[128,4,3]{2,1,0:T(4,128)(2,1)}), bf16[128,4,3]{2,1,0:T(4,128)(2,1)S(1)}, u32[]{:S(2)}, u32[]{:S(2)}) async-start(bf16[128,4,3]{2,1,0:T(4,128)(2,1)} %scatter_fusion.1), calls=%async_computation.2 | async-start | bytes 262144 | tf_op jit(solution)/shard_map/all_to_all | solution.py:152
  510.5 29.0 %all-to-all-start.3 = ((bf16[128,4,1024]{2,1,0:T(4,128)(2,1)}), bf16[128,4,1024]{2,1,0:T(4,128)(2,1)S(1)}, u32[]{:S(2)}, u32[]{:S(2)}) async-start(bf16[128,4,1024]{2,1,0:T(4,128)(2,1)} %scatter_fusion.2), calls=%async_computation.3 | async-start | bytes 2097152 | tf_op jit(solution)/shard_map/all_to_all | solution.py:151
  540.8 14.2 %all-to-all-start.4 = ((f32[128,1,4]{2,1,0:T(1,128)}), f32[128,1,4]{2,1,0:T(1,128)S(1)}, u32[]{:S(2)}, u32[]{:S(2)}) async-start(f32[128,1,4]{2,1,0:T(1,128)} %bitcast.88), calls=%async_computation.4 | async-start | bytes 131072 | tf_op jit(solution)/shard_map/all_to_all | solution.py:180
  555.0 20.2 %all-to-all-start.5 = ((f32[128,1,4]{2,1,0:T(1,128)}), f32[128,1,4]{2,1,0:T(1,128)S(1)}, u32[]{:S(2)}, u32[]{:S(2)}) async-start(f32[128,1,4]{2,1,0:T(1,128)} %bitcast.92), calls=%async_computation.5 | async-start | bytes 131072 | tf_op jit(solution)/shard_map/all_to_all | solution.py:181
  (19 other events, 12.5 us)
Sparse Core Ops, SparseCore 0:
  465.1 26.9 all-gather.1
where the time goes:
time: 628 us; the launch traced here: 624 us
  other arithmetic  238 us (38%)
  local copies, waits for them, and re-layouts  179 us (29%)
  waiting for transfers between devices  74.6 us (12%)
  matrix products  60.1 us (10%)
  starting transfers between devices  43.8 us (7%)
  between operations  14.2 us (2%)
  blocking collectives  13.1 us (2%)
    convert_element_type x16, other arithmetic, embed_clips(): activated = (mixed * jax.nn.sigmoid(mixed)).astype(jnp.bfloat16)  200 us
    all_to_all x1, waiting for transfers between devices, local(): lax.all_to_all(clip_buffer, 'dp', split_axis=1, concat_axis=1, tiled=True)  59.7 us
    reshape x16, local copies, waits for them, and re-layouts, embed_clips(): hidden.reshape(clip_count, frame_count, SIDE, SIDE, expanded)  31.2 us
    max x16, local copies, waits for them, and re-layouts, embed_clips(): jax.nn.relu(jnp.dot(features.reshape(-1, channels), expand_weight[layer_i...  29.2 us
    dot_general x5, matrix products, visit(): jnp.einsum('rd,kd->rk', block_rows, panel_block, preferred_element_type=j...  26.3 us
    dot_general x16, matrix products, embed_clips(): jnp.dot(activated.reshape(-1, expanded), reduce_weight[layer_index], pref...  23.3 us
    scatter x1, local copies, waits for them, and re-layouts, local(): clip_buffer = jnp.zeros_like(clip_data).at[destination].set(clip_data).re...  19.6 us
    scatter x1, local copies, waits for them, and re-layouts, local(): jnp.zeros((owner_total, capacity, width_d), jnp.bfloat16)  18.2 us
  transfers between devices with their start and end apart: 7, of which 3 were waited for; matrix products, arithmetic and copies ran while one was open for 17% of the time, Pallas kernels for 0%

commit v1 on v0

v1 whole, which is shorter than its diff:
```python
import functools

import jax
import jax.numpy as jnp
from jax import lax
from jax.experimental import pallas as pl
from jax.experimental.pallas import tpu as pltpu
from jax.sharding import PartitionSpec as P

SIDE = 4
FRAMES = 4
SPOTS = SIDE * SIDE
BF = jnp.bfloat16
F32 = jnp.float32


def neighbours(at, extent):
    return [(at + shift - 1, shift) for shift in range(3) if 0 <= at + shift - 1 < extent]


def embed_kernel(
    clip_ref, count_ref, send_ref, expand_ref, depth_ref, reduce_ref, out_ref, x_ref, hidden_ref, act_ref, pool_ref
):
    channels, clips = clip_ref.shape[2], clip_ref.shape[3]
    expanded = expand_ref.shape[1]
    counts = count_ref[...]
    zero = jnp.zeros((channels, clips), BF)

    @pl.loop(0, FRAMES)
    def _(frame):
        kept = jnp.broadcast_to((counts > frame).astype(F32), (channels, clips)) > 0.5

        @pl.loop(0, SPOTS)
        def _(spot):
            x_ref[frame * SPOTS + spot] = jnp.where(
                kept, clip_ref[frame, spot].astype(F32), 0.0
            ).astype(BF)

    pool_ref[...] = jnp.zeros_like(pool_ref)
    for layer in range(2):

        @pl.loop(0, FRAMES * SPOTS // 2)
        def _(pair):
            both = jnp.concatenate([x_ref[2 * pair], x_ref[2 * pair + 1]], axis=1)
            hidden = jnp.dot(expand_ref[layer], both, preferred_element_type=F32)
            hidden = jnp.maximum(hidden, 0.0).astype(BF)
            hidden_ref[2 * pair] = hidden[:, :clips]
            hidden_ref[2 * pair + 1] = hidden[:, clips:]

        @pl.loop(0, expanded // 16)
        def _(tile):
            rows = pl.ds(pl.multiple_of(tile * 16, 16), 16)
            taps = depth_ref[layer, rows, :]
            weight = [
                jnp.broadcast_to(taps[:, tap : tap + 1], (16, clips)).astype(BF) for tap in range(27)
            ]
            for frame in range(FRAMES):
                for y in range(SIDE):
                    mixed = [None] * SIDE
                    for from_t, shift_t in neighbours(frame, FRAMES):
                        for from_y, shift_y in neighbours(y, SIDE):
                            base = from_t * SPOTS + from_y * SIDE
                            line = [hidden_ref[base + z, rows, :] for z in range(SIDE)]
                            for z in range(SIDE):
                                for from_z, shift_z in neighbours(z, SIDE):
                                    term = line[from_z] * weight[9 * shift_t + 3 * shift_y + shift_z]
                                    mixed[z] = term if mixed[z] is None else mixed[z] + term
                    for z in range(SIDE):
                        half = mixed[z] * BF(0.5)
                        act_ref[frame * SPOTS + y * SIDE + z, rows, :] = half + half * jnp.tanh(half)

        @pl.loop(0, FRAMES * SPOTS // 2)
        def _(pair):
            both = jnp.concatenate([act_ref[2 * pair], act_ref[2 * pair + 1]], axis=1)
            branch = jnp.dot(reduce_ref[layer], both, preferred_element_type=F32)
            kept = jnp.broadcast_to((counts > pair // (SPOTS // 2)).astype(F32), (channels, clips))
            for side in range(2):
                spot = 2 * pair + side
                x = x_ref[spot].astype(F32) + branch[:, side * clips : (side + 1) * clips] * kept
                x = x.astype(BF)
                if layer == 0:
                    x_ref[spot] = x
                else:
                    pool_ref[...] += x.astype(F32)

    pooled = (pool_ref[...] / (counts * SPOTS).astype(F32)).astype(BF)
    per_peer = out_ref.shape[1]
    n_dp = out_ref.shape[0]
    row = lax.broadcasted_iota(jnp.int32, (clips, clips), 0)
    slot = (row % per_peer) * n_dp + row // per_peer
    pick = (jnp.broadcast_to(send_ref[...], (clips, clips)) == slot).astype(F32).astype(BF)
    rows = lax.dot_general(pick, pooled, (((1,), (1,)), ((), ())), preferred_element_type=F32)
    rows = rows.astype(BF).reshape(n_dp, per_peer, channels)
    out_ref[:, :, :channels] = rows
    out_ref[:, :, channels:] = jnp.zeros((n_dp, per_peer, out_ref.shape[2] - channels), BF)


def embed(clip_data, frame_counts, send_list, expand_weight, depth_kernel, reduce_weight, n_dp):
    clips, frames, spots, channels = clip_data.shape
    expanded = expand_weight.shape[2]
    return pl.pallas_call(
        embed_kernel,
        out_shape=jax.ShapeDtypeStruct((n_dp, clips // n_dp, 256), BF),
        in_specs=[pl.BlockSpec(memory_space=pltpu.VMEM)] * 6,
        out_specs=pl.BlockSpec(memory_space=pltpu.VMEM),
        scratch_shapes=[
            pltpu.VMEM((frames * spots, channels, clips), BF),
            pltpu.VMEM((frames * spots, expanded, clips), BF),
            pltpu.VMEM((frames * spots, expanded, clips), BF),
            pltpu.VMEM((channels, clips), F32),
        ],
        compiler_params=pltpu.CompilerParams(vmem_limit_bytes=60 << 20),
        name="embed",
    )(
        jnp.transpose(clip_data, (1, 2, 3, 0)),
        frame_counts,
        send_list,
        jnp.swapaxes(expand_weight, 1, 2),
        jnp.swapaxes(depth_kernel, 1, 2).astype(F32),
        jnp.swapaxes(reduce_weight, 1, 2),
    )


def unit(projected, axis):
    square = jnp.sum(projected * projected, axis=axis, keepdims=True)
    return (projected * lax.rsqrt(square + 1e-06)).astype(BF)


LABEL_ROWS = 16


def own_kernel(arrived_ref, ids_ref, head_ref, payload_ref, vectors_ref):
    n_dp, per_peer, width = arrived_ref.shape
    clips = n_dp * per_peer
    channels = head_ref.shape[0]
    arrived = arrived_ref[...].reshape(clips, width)[:, :channels]
    row = lax.broadcasted_iota(jnp.int32, (clips, clips), 0)
    lane = lax.broadcasted_iota(jnp.int32, (clips, clips), 1)
    pick = (lane == (row % n_dp) * per_peer + row // n_dp).astype(F32).astype(BF)
    rows = jnp.dot(pick, arrived, preferred_element_type=F32).astype(BF)
    projected = jnp.dot(rows, head_ref[...], preferred_element_type=F32)
    vectors_ref[...] = unit(projected, 1)
    payload_ref[0:channels, :] = jnp.transpose(rows.astype(F32)).astype(BF)
    ids = ids_ref[...]
    which = lax.broadcasted_iota(jnp.int32, (LABEL_ROWS, clips), 0)
    high, low = ids // 256, ids % 256
    label = jnp.where(which == 0, high, jnp.where(which == 1, low, 0))
    payload_ref[channels:, :] = label.astype(F32).astype(BF)


def own(arrived, cluster_ids, head_weight):
    n_dp, per_peer, width = arrived.shape
    channels, dims = head_weight.shape
    clips = n_dp * per_peer
    return pl.pallas_call(
        own_kernel,
        out_shape=(
            jax.ShapeDtypeStruct((channels + LABEL_ROWS, clips), BF),
            jax.ShapeDtypeStruct((clips, dims), BF),
        ),
        in_specs=[pl.BlockSpec(memory_space=pltpu.VMEM)] * 3,
        out_specs=(pl.BlockSpec(memory_space=pltpu.VMEM),) * 2,
        name="own",
    )(arrived, cluster_ids, head_weight)


PANEL_ROWS = 784
OCCUR = 64


def nearest_kernel(panel_rows, base_ref, rows_ref, head_ref, panel_ref, turned_ref, near_ref, own_ref, best_ref):
    n_cent, height, clips = rows_ref.shape
    dims, channels = head_ref.shape
    total = n_cent * clips
    step = pl.program_id(0)
    last = pl.num_programs(0) - 1

    @pl.when(step == 0)
    def _():
        @pl.loop(0, n_cent // 2)
        def _(pair):
            both = jnp.concatenate([rows_ref[2 * pair], rows_ref[2 * pair + 1]], axis=1)
            projected = jnp.dot(head_ref[...], both[:channels], preferred_element_type=F32)
            cols = pl.ds(pl.multiple_of(pair * 2 * clips, 2 * clips), 2 * clips)
            turned_ref[:, cols] = unit(projected, 0)

        best_ref[...] = jnp.full_like(best_ref, -jnp.inf)

    def score(cols):
        return jnp.dot(panel_ref[...], turned_ref[:, cols], preferred_element_type=F32)

    def keep(scores, cols):
        rows = scores.shape[0]
        best_ref[:, cols] = jnp.maximum(
            best_ref[:, cols], jnp.max(scores.reshape(rows // 8, 8, scores.shape[1]), axis=0)
        )

    for block in range(total // 256):
        cols = pl.ds(block * 256, 256)

        @pl.when(step < last)
        def _():
            scores = score(cols)
            keep(scores, cols)

            @pl.when(step == 0)
            def _():
                label = jnp.concatenate(
                    [rows_ref[2 * block, channels:, :], rows_ref[2 * block + 1, channels:, :]], axis=1
                ).astype(F32)
                local_id = (label[0:1] * 256.0 + label[1:2]).astype(jnp.int32) - base_ref[0]
                index = lax.broadcasted_iota(jnp.int32, (OCCUR, 256), 0)
                own_ref[:, cols] = jnp.max(
                    jnp.where(index == local_id, scores[:OCCUR], -jnp.inf), axis=0, keepdims=True
                )

        @pl.when(step == last)
        def _():
            scores = score(cols)
            index = lax.broadcasted_iota(jnp.int32, scores.shape, 0) + last * panel_ref.shape[0]
            keep(jnp.where(index < panel_rows, scores, -jnp.inf), cols)
            near_ref[:, cols] = jnp.max(best_ref[:, cols], axis=0, keepdims=True)


def nearest_of(rows, head_turned, centroids, base):
    n_cent, height, clips = rows.shape
    dims, channels = head_turned.shape
    total = n_cent * clips
    panel_rows = centroids.shape[0]
    whole = lambda shape: pl.BlockSpec(shape, lambda step: (0,) * len(shape))
    return pl.pallas_call(
        functools.partial(nearest_kernel, panel_rows),
        grid=(pl.cdiv(panel_rows, PANEL_ROWS),),
        out_shape=(
            jax.ShapeDtypeStruct((dims, total), BF),
            jax.ShapeDtypeStruct((1, total), F32),
            jax.ShapeDtypeStruct((1, total), F32),
        ),
        in_specs=[
            pl.BlockSpec(memory_space=pltpu.SMEM),
            whole(rows.shape),
            whole(head_turned.shape),
            pl.BlockSpec((PANEL_ROWS, dims), lambda step: (step, 0)),
        ],
        out_specs=(whole((dims, total)), whole((1, total)), whole((1, total))),
        scratch_shapes=[pltpu.VMEM((8, total), F32)],
        compiler_params=pltpu.CompilerParams(vmem_limit_bytes=60 << 20),
        name="nearest",
    )(base, rows, head_turned, centroids)


GROUP = 4


def peer_kernel(place_ref, cols_ref, rows_ref, turned_ref, head_ref, near_ref, own_ref, out_ref, best_ref):
    n_dp, height, clips = cols_ref.shape
    n_cent = rows_ref.shape[0]
    channels = head_ref.shape[0]
    total = n_cent * clips
    eye = (
        lax.broadcasted_iota(jnp.int32, (clips, clips), 0)
        == lax.broadcasted_iota(jnp.int32, (clips, clips), 1)
    ).astype(F32).astype(BF)
    best_ref[...] = jnp.full_like(best_ref, -1.0)
    mine_dp, mine_cent = place_ref[0], place_ref[1]

    @pl.loop(0, n_dp // GROUP)
    def _(group):
        flipped = jnp.concatenate(
            [
                lax.dot_general(
                    eye, cols_ref[group * GROUP + at], (((1,), (1,)), ((), ())), preferred_element_type=F32
                )
                for at in range(GROUP)
            ],
            axis=0,
        )
        projected = jnp.dot(flipped[:, :channels].astype(BF), head_ref[...], preferred_element_type=F32)
        vectors = unit(projected, 1)
        ids = flipped[:, channels : channels + 1] * 256.0 + flipped[:, channels + 1 : channels + 2]
        wide = jnp.broadcast_to(ids, (GROUP * clips, 256))
        line = lax.broadcasted_iota(jnp.int32, (GROUP * clips, 256), 0)
        lane = lax.broadcasted_iota(jnp.int32, (GROUP * clips, 256), 1)
        for block in range(total // 256):
            cols = pl.ds(block * 256, 256)
            scores = jnp.dot(vectors, turned_ref[:, cols], preferred_element_type=F32)
            label = jnp.concatenate(
                [rows_ref[2 * block, channels:, :], rows_ref[2 * block + 1, channels:, :]], axis=1
            ).astype(F32)
            row_ids = label[0:1] * 256.0 + label[1:2]
            self_line = lane + (mine_dp - group * GROUP) * clips - (mine_cent - 2 * block) * clips
            inside = (lane // clips) == (mine_cent - 2 * block)
            same = (wide == row_ids) & jnp.logical_not(inside & (line == self_line))
            found = jnp.where(same, scores, -1.0)
            best_ref[:, cols] = jnp.maximum(
                best_ref[:, cols], jnp.max(found.reshape(GROUP * clips // 8, 8, 256), axis=0)
            )

    best = jnp.max(best_ref[...], axis=0, keepdims=True)
    for cent in range(n_cent):
        cols = slice(cent * clips, (cent + 1) * clips)
        out_ref[cent, 0:1, :] = near_ref[:, cols]
        out_ref[cent, 1:2, :] = own_ref[:, cols]
        out_ref[cent, 2:3, :] = best[:, cols]
        out_ref[cent, 3:4, :] = best[:, cols]


def peers_of(cols, rows, turned, head_weight, near, own_best, place):
    n_cent, height, clips = rows.shape
    total = n_cent * clips
    return pl.pallas_call(
        peer_kernel,
        out_shape=jax.ShapeDtypeStruct((n_cent, 4, clips), F32),
        in_specs=[pl.BlockSpec(memory_space=pltpu.SMEM)] + [pl.BlockSpec(memory_space=pltpu.VMEM)] * 6,
        out_specs=pl.BlockSpec(memory_space=pltpu.VMEM),
        scratch_shapes=[pltpu.VMEM((8, total), F32)],
        compiler_params=pltpu.CompilerParams(vmem_limit_bytes=60 << 20),
        name="peers",
    )(place, cols, rows, turned, head_weight, near, own_best)


def local(
    clip_data,
    frame_counts,
    send_list,
    cluster_ids,
    expand_weight,
    depth_kernel,
    reduce_weight,
    head_weight,
    centroids,
):
    n_dp = lax.axis_size("dp")
    n_cent = lax.axis_size("cent")
    panel_rows = centroids.shape[0]
    mine_dp, mine_cent = lax.axis_index("dp"), lax.axis_index("cent")
    base = (mine_cent * panel_rows).astype(jnp.int32)[None]
    place = jnp.stack([mine_dp, mine_cent]).astype(jnp.int32)
    pooled = embed(
        clip_data, frame_counts, send_list, expand_weight, depth_kernel, reduce_weight, n_dp
    )
    arrived = lax.all_to_all(pooled, "dp", split_axis=0, concat_axis=0, tiled=True)
    payload, vectors = own(arrived, cluster_ids, head_weight)
    rows = lax.all_gather(payload, "cent", axis=0)
    spread = jnp.broadcast_to(payload, (n_dp,) + payload.shape)
    cols = lax.all_to_all(spread, "dp", split_axis=0, concat_axis=0, tiled=True)
    turned, near, own_best = nearest_of(rows, jnp.swapaxes(head_weight, 0, 1), centroids, base)
    partial = peers_of(cols, rows, turned, head_weight, near, own_best, place)
    parts = lax.all_to_all(partial, "cent", split_axis=0, concat_axis=0, tiled=True)
    final = jnp.max(parts, axis=0)
    return (vectors, final[0], final[1], final[2])


def solution(mesh):
    placed = (
        P(("dp", "cent"), None, None, None),
        P(("dp", "cent"), None),
        P(("dp", "cent"), None),
        P(("dp", "cent"), None),
        P(),
        P(),
        P(),
        P(),
        P("cent", None),
    )
    return jax.shard_map(
        local,
        mesh=mesh,
        in_specs=placed,
        out_specs=(
            P(("dp", "cent"), None),
            P(("dp", "cent")),
            P(("dp", "cent")),
            P(("dp", "cent")),
        ),
        check_vma=False,
    )
```

time: 628 us -> 171 us (0.27)
  other arithmetic: 238 us -> 1.41 us
  local copies, waits for them, and re-layouts: 179 us -> 7.31 us
  Pallas kernels: 0 us -> 117 us
  waiting for transfers between devices: 74.6 us -> 0.01 us
  matrix products: 60.1 us -> 0 us
  starting transfers between devices: 43.8 us -> 3.62 us
  blocking collectives: 13.1 us -> 40 us
  between operations: 14.2 us -> 0.67 us
    convert_element_type x33 -> x1, other arithmetic: 202 us -> 0.81 us  [embed(): jnp.swapaxes(depth_kernel, 1, 2).astype(F32)]
    pallas_call x0 -> x4, Pallas kernels: none -> 117 us  [the longest x1 79.5 us: embed(): pl.pallas_call(embed_kernel, out_shape=jax.ShapeDtypeStruct((n_dp, clips...]
    all_to_all x6 -> x1, waiting for transfers between devices: 74.6 us -> 0.01 us  [local(): cols = lax.all_to_all(spread, 'dp', split_axis=0, concat_axis=0, tiled=True)]
    dot_general x46 -> x0, matrix products: 60.1 us -> none  [the longest x5 26.3 us: visit(): jnp.einsum('rd,kd->rk', block_rows, panel_block, preferred_element_type=j...]
    scatter x4 -> x0, local copies, waits for them, and re-layouts: 52.5 us -> none  [the longest x1 19.6 us: local(): clip_buffer = jnp.zeros_like(clip_data).at[destination].set(clip_data).re...]
    reshape x19 -> x0, local copies, waits for them, and re-layouts: 50.1 us -> none  [the longest x16 31.2 us: embed_clips(): hidden.reshape(clip_count, frame_count, SIDE, SIDE, expanded)]
    all_to_all x6 -> x1, starting transfers between devices: 43.5 us -> 3.62 us  [local(): cols = lax.all_to_all(spread, 'dp', split_axis=0, concat_axis=0, tiled=True)]
    max x16 -> x0, local copies, waits for them, and re-layouts: 29.2 us -> none  [embed_clips(): jax.nn.relu(jnp.dot(features.reshape(-1, channels), expand_weight[layer_i...]
  transfers between devices with their start and end apart: 7 -> 1, of which waited for: 3 -> 0; matrix products, arithmetic and copies ran while one was open for 17% -> 1% of each run, Pallas kernels for 0% -> 14%
where the time goes in v1:
time: 171 us; the launch traced here: 170 us
  Pallas kernels  117 us (68%)
  blocking collectives  40 us (23%)
  local copies, waits for them, and re-layouts  7.31 us (4%)
  starting transfers between devices  3.62 us (2%)
    pallas_call x1, Pallas kernels, embed(): pl.pallas_call(embed_kernel, out_shape=jax.ShapeDtypeStruct((n_dp, clips...  79.5 us
    pallas_call x1, Pallas kernels, nearest_of(): pl.pallas_call(functools.partial(nearest_kernel, panel_rows), grid=(pl.cd...  24.5 us
    all_gather x1, blocking collectives, local(): rows = lax.all_gather(payload, 'cent', axis=0)  16.3 us
    all_to_all x1, blocking collectives, local(): lax.all_to_all(pooled, 'dp', split_axis=0, concat_axis=0, tiled=True)  15.2 us
    pallas_call x1, Pallas kernels, peers_of(): pl.pallas_call(peer_kernel, out_shape=jax.ShapeDtypeStruct((n_cent, 4, cl...  11 us
    all_to_all x1, blocking collectives, local(): lax.all_to_all(partial, 'cent', split_axis=0, concat_axis=0, tiled=True)  8.51 us
    unnamed x9, local copies, waits for them, and re-layouts  4.89 us
    all_to_all x1, starting transfers between devices, local(): cols = lax.all_to_all(spread, 'dp', split_axis=0, concat_axis=0, tiled=True)  3.62 us
  transfers between devices with their start and end apart: 1, of which 0 were waited for; matrix products, arithmetic and copies ran while one was open for 1% of the time, Pallas kernels for 14%

profile of v1, /device:TPU:1, one launch (start us, length us, event | category | flops | bytes accessed | tf_op | source)
XLA Modules:
  0.0 170.3 jit_solution(7857997891428858227)
XLA Ops:
  0.6 1.0 copy.14
  1.6 0.8 convert_bitcast_fusion.depth_ref
  2.5 2.0 %copy.13 = bf16[2,192,432]{1,2,0:T(8,128)(2,1)} copy(bf16[2,192,432]{2,1,0:T(8,128)(2,1)} %param.13) | data formatting | bytes 663552 | tf_op args[4]
  4.4 0.0 copy-start
  4.4 79.5 %embed.1 = bf16[16,8,256]{2,1,0:T(8,128)(2,1)} custom-call(bf16[4,16,192,128]{3,2,1,0:T(8,128)(2,1)} %bitcast.18, s32[1,128]{1,0:T(1,128)} %count_ref.1, s32[1,128]{1,0:T(1,128)} %send_ref.1, bf16[2,432,192]{2,1,0:T(8,128)(2,1)} %bitcast.20, f32[2,432,27]{2,1,0:T(8,128)} %convert_bitcast_fusion.depth_ref, bf16[2,192,432]{2,1,0:T(8,128)(2,1)} %bitcast.21), custom_call_target="tpu_custom_call" | custom-call | tf_op jit(solution)/shard_map/embed/pallas_call | solution.py:101
  83.9 15.2 %all_to_all.15.arrived_ref = bf16[16,8,256]{2,1,0:T(8,128)(2,1)} all-to-all(bf16[16,8,256]{2,1,0:T(8,128)(2,1)} %embed.1), channel_id=1, replica_groups=mesh['dp'=16,'cent'=8] {'dp'}, dimensions={0} | all-to-all | bytes 131072 | tf_op jit(solution)/shard_map/all_to_all | solution.py:342
  99.2 2.2 %own.1 = (bf16[208,128]{1,0:T(8,128)(2,1)}, bf16[128,1024]{1,0:T(8,128)(2,1)}) custom-call(bf16[16,8,256]{2,1,0:T(8,128)(2,1)} %all_to_all.15.arrived_ref, s32[1,128]{1,0:T(1,128)} %ids_ref.1, bf16[192,1024]{1,0:T(8,128)(2,1)} %head_ref.3), custom_call_target="tpu_custom_call" | custom-call | tf_op jit(solution)/shard_map/own/pallas_call | solution.py:155
  101.4 0.0 copy-start.2
  101.4 1.9 %broadcast_in_dim.6 = bf16[16,208,128]{2,1,0:T(8,128)(2,1)} broadcast(bf16[208,128]{1,0:T(8,128)(2,1)} %get-tuple-element.10), dimensions={1,2} | broadcast | bytes 905216 | tf_op jit(solution)/shard_map/broadcast_in_dim | solution.py:345
  103.3 3.6 %all-to-all-start.1 = ((bf16[16,208,128]{2,1,0:T(8,128)(2,1)}), bf16[16,208,128]{2,1,0:T(8,128)(2,1)S(1)}, u32[]{:S(2)}, u32[]{:S(2)}) async-start(bf16[16,208,128]{2,1,0:T(8,128)(2,1)} %broadcast_in_dim.6), calls=%async_computation.1 | async-start | bytes 1703936 | tf_op jit(solution)/shard_map/all_to_all | solution.py:346
  106.9 0.0 copy-done
  106.9 1.0 copy.15
  107.9 0.6 pad_add_fusion.place_ref
  108.5 0.0 copy-done.2
  108.5 16.3 %all-gather = bf16[1664,128]{1,0:T(8,128)(2,1)} all-gather(bf16[208,128]{1,0:T(8,128)(2,1)S(1)} %copy-done.2), channel_id=2, replica_groups=mesh['dp'=16,'cent'=8] {'cent'}, dimensions={0}, use_global_device_ids=true | all-gather | bytes 479232 | tf_op jit(solution)/shard_map/all_gather | solution.py:344
  124.8 24.5 %nearest.1 = (bf16[1024,1024]{1,0:T(8,128)(2,1)}, f32[1,1024]{1,0:T(1,128)}, f32[1,1024]{1,0:T(1,128)}) custom-call(s32[1]{0:T(128)} %bitcast.7.base_ref, bf16[8,208,128]{2,1,0:T(8,128)(2,1)} %bitcast.16, bf16[1024,192]{1,0:T(8,128)(2,1)} %bitcast.19, bf16[6250,1024]{1,0:T(8,128)(2,1)} %panel_ref.1), custom_call_target="tpu_custom_call" | custom-call | tf_op jit(solution)/shard_map/nearest/pallas_call | solution.py:231
  149.3 0.0 all-to-all-done.1.cols_ref
  149.3 0.0 copy-start.1
  149.3 0.9 copy-done.1
  150.2 11.0 %peers.1 = f32[8,4,128]{2,1,0:T(4,128)} custom-call(s32[2]{0:T(128)} %pad_add_fusion.place_ref, bf16[16,208,128]{2,1,0:T(8,128)(2,1)} %copy-done.1, bf16[8,208,128]{2,1,0:T(8,128)(2,1)} %bitcast.17, bf16[1024,1024]{1,0:T(8,128)(2,1)} %get-tuple-element.11.turned_ref, bf16[192,1024]{1,0:T(8,128)(2,1)} %head_ref.3, f32[1,1024]{1,0:T(1,128)} %get-tuple-element.12.near_ref, ...), custom_call_target="tpu_custom_call" | custom-call | tf_op jit(solution)/shard_map/peers/pallas_call | solution.py:311
  161.2 8.5 %all_to_all.16 = f32[8,4,128]{2,1,0:T(4,128)S(1)} all-to-all(f32[8,4,128]{2,1,0:T(4,128)} %peers.1), channel_id=1, replica_groups=mesh['dp'=16,'cent'=8] {'cent'}, dimensions={0} | all-to-all | bytes 32768 | tf_op jit(solution)/shard_map/all_to_all | solution.py:349
  169.8 0.5 slice_bitcast_fusion
  (1 shorter events, 0.0 us)
Async XLA Ops:
  4.4 102.5 %copy-start = (bf16[192,1024]{1,0:T(8,128)(2,1)S(1)}, bf16[192,1024]{1,0:T(8,128)(2,1)}, u32[]{:S(2)}) copy-start(bf16[192,1024]{1,0:T(8,128)(2,1)} %head_ref.3) | copy-start | bytes 1179652
  101.4 7.1 %copy-start.2 = (bf16[208,128]{1,0:T(8,128)(2,1)S(1)}, bf16[208,128]{1,0:T(8,128)(2,1)}, u32[]{:S(2)}) copy-start(bf16[208,128]{1,0:T(8,128)(2,1)} %get-tuple-element.10) | copy-start | bytes 159748
  103.3 46.1 %all-to-all-start.1 = ((bf16[16,208,128]{2,1,0:T(8,128)(2,1)}), bf16[16,208,128]{2,1,0:T(8,128)(2,1)S(1)}, u32[]{:S(2)}, u32[]{:S(2)}) async-start(bf16[16,208,128]{2,1,0:T(8,128)(2,1)} %broadcast_in_dim.6), calls=%async_computation.1 | async-start | bytes 1703936 | tf_op jit(solution)/shard_map/all_to_all | solution.py:346
  149.3 0.9 copy-start.1

commit v2 on v1

--- a/solution.py
+++ b/solution.py
@@ -43,7 +43,6 @@
         def _(pair):
             both = jnp.concatenate([x_ref[2 * pair], x_ref[2 * pair + 1]], axis=1)
             hidden = jnp.dot(expand_ref[layer], both, preferred_element_type=F32)
-            hidden = jnp.maximum(hidden, 0.0).astype(BF)
             hidden_ref[2 * pair] = hidden[:, :clips]
             hidden_ref[2 * pair + 1] = hidden[:, clips:]
 
@@ -54,13 +53,16 @@
             weight = [
                 jnp.broadcast_to(taps[:, tap : tap + 1], (16, clips)).astype(BF) for tap in range(27)
             ]
+            hidden = [
+                jnp.maximum(hidden_ref[spot, rows, :], 0.0).astype(BF) for spot in range(FRAMES * SPOTS)
+            ]
             for frame in range(FRAMES):
                 for y in range(SIDE):
                     mixed = [None] * SIDE
                     for from_t, shift_t in neighbours(frame, FRAMES):
                         for from_y, shift_y in neighbours(y, SIDE):
                             base = from_t * SPOTS + from_y * SIDE
-                            line = [hidden_ref[base + z, rows, :] for z in range(SIDE)]
+                            line = hidden[base : base + SIDE]
                             for z in range(SIDE):
                                 for from_z, shift_z in neighbours(z, SIDE):
                                     term = line[from_z] * weight[9 * shift_t + 3 * shift_y + shift_z]
@@ -105,7 +107,7 @@
         out_specs=pl.BlockSpec(memory_space=pltpu.VMEM),
         scratch_shapes=[
             pltpu.VMEM((frames * spots, channels, clips), BF),
-            pltpu.VMEM((frames * spots, expanded, clips), BF),
+            pltpu.VMEM((frames * spots, expanded, clips), F32),
             pltpu.VMEM((frames * spots, expanded, clips), BF),
             pltpu.VMEM((channels, clips), F32),
         ],

time: 171 us -> 146 us (0.85)
  Pallas kernels: 117 us -> 92.4 us
    pallas_call x1, Pallas kernels: 79.5 us -> 54.7 us  [embed(): pl.pallas_call(embed_kernel, out_shape=jax.ShapeDtypeStruct((n_dp, clips...]
  transfers between devices with their start and end apart: 1 -> 1, of which waited for: 0 -> 0; matrix products, arithmetic and copies ran while one was open for 1% -> 1% of each run, Pallas kernels for 14% -> 17%
where the time goes in v2:
time: 146 us; the launch traced here: 145 us
  Pallas kernels  92.4 us (63%)
  blocking collectives  40 us (27%)
  local copies, waits for them, and re-layouts  7.31 us (5%)
  starting transfers between devices  3.62 us (2%)
    pallas_call x1, Pallas kernels, embed(): pl.pallas_call(embed_kernel, out_shape=jax.ShapeDtypeStruct((n_dp, clips...  54.7 us
    pallas_call x1, Pallas kernels, nearest_of(): pl.pallas_call(functools.partial(nearest_kernel, panel_rows), grid=(pl.cd...  24.5 us
    all_gather x1, blocking collectives, local(): rows = lax.all_gather(payload, 'cent', axis=0)  16.4 us
    all_to_all x1, blocking collectives, local(): lax.all_to_all(pooled, 'dp', split_axis=0, concat_axis=0, tiled=True)  15.2 us
    pallas_call x1, Pallas kernels, peers_of(): pl.pallas_call(peer_kernel, out_shape=jax.ShapeDtypeStruct((n_cent, 4, cl...  11 us
    all_to_all x1, blocking collectives, local(): lax.all_to_all(partial, 'cent', split_axis=0, concat_axis=0, tiled=True)  8.48 us
    unnamed x9, local copies, waits for them, and re-layouts  4.89 us
    all_to_all x1, starting transfers between devices, local(): cols = lax.all_to_all(spread, 'dp', split_axis=0, concat_axis=0, tiled=True)  3.62 us
  transfers between devices with their start and end apart: 1, of which 0 were waited for; matrix products, arithmetic and copies ran while one was open for 1% of the time, Pallas kernels for 17%

profile of v2, /device:TPU:1, one launch (start us, length us, event | category | flops | bytes accessed | tf_op | source)
XLA Modules:
  0.0 145.4 jit_solution(7506048060127377655)
XLA Ops:
  0.6 1.0 copy.14
  1.6 0.8 convert_bitcast_fusion.depth_ref
  2.5 2.0 %copy.13 = bf16[2,192,432]{1,2,0:T(8,128)(2,1)} copy(bf16[2,192,432]{2,1,0:T(8,128)(2,1)} %param.13) | data formatting | bytes 663552 | tf_op args[4]
  4.4 0.0 copy-start
  4.4 54.7 %embed.1 = bf16[16,8,256]{2,1,0:T(8,128)(2,1)} custom-call(bf16[4,16,192,128]{3,2,1,0:T(8,128)(2,1)} %bitcast.18, s32[1,128]{1,0:T(1,128)} %count_ref.1, s32[1,128]{1,0:T(1,128)} %send_ref.1, bf16[2,432,192]{2,1,0:T(8,128)(2,1)} %bitcast.20, f32[2,432,27]{2,1,0:T(8,128)} %convert_bitcast_fusion.depth_ref, bf16[2,192,432]{2,1,0:T(8,128)(2,1)} %bitcast.21), custom_call_target="tpu_custom_call" | custom-call | tf_op jit(solution)/shard_map/embed/pallas_call | solution.py:103
  59.1 15.2 %all_to_all.15.arrived_ref = bf16[16,8,256]{2,1,0:T(8,128)(2,1)} all-to-all(bf16[16,8,256]{2,1,0:T(8,128)(2,1)} %embed.1), channel_id=1, replica_groups=mesh['dp'=16,'cent'=8] {'dp'}, dimensions={0} | all-to-all | bytes 131072 | tf_op jit(solution)/shard_map/all_to_all | solution.py:344
  74.3 2.2 %own.1 = (bf16[208,128]{1,0:T(8,128)(2,1)}, bf16[128,1024]{1,0:T(8,128)(2,1)}) custom-call(bf16[16,8,256]{2,1,0:T(8,128)(2,1)} %all_to_all.15.arrived_ref, s32[1,128]{1,0:T(1,128)} %ids_ref.1, bf16[192,1024]{1,0:T(8,128)(2,1)} %head_ref.3), custom_call_target="tpu_custom_call" | custom-call | tf_op jit(solution)/shard_map/own/pallas_call | solution.py:157
  76.5 0.0 copy-start.2
  76.5 1.9 %broadcast_in_dim.6 = bf16[16,208,128]{2,1,0:T(8,128)(2,1)} broadcast(bf16[208,128]{1,0:T(8,128)(2,1)} %get-tuple-element.10), dimensions={1,2} | broadcast | bytes 905216 | tf_op jit(solution)/shard_map/broadcast_in_dim | solution.py:347
  78.4 3.6 %all-to-all-start.1 = ((bf16[16,208,128]{2,1,0:T(8,128)(2,1)}), bf16[16,208,128]{2,1,0:T(8,128)(2,1)S(1)}, u32[]{:S(2)}, u32[]{:S(2)}) async-start(bf16[16,208,128]{2,1,0:T(8,128)(2,1)} %broadcast_in_dim.6), calls=%async_computation.1 | async-start | bytes 1703936 | tf_op jit(solution)/shard_map/all_to_all | solution.py:348
  82.0 0.0 copy-done
  82.0 1.0 copy.15
  83.0 0.6 pad_add_fusion.place_ref
  83.6 0.0 copy-done.2
  83.6 16.4 %all-gather = bf16[1664,128]{1,0:T(8,128)(2,1)} all-gather(bf16[208,128]{1,0:T(8,128)(2,1)S(1)} %copy-done.2), channel_id=2, replica_groups=mesh['dp'=16,'cent'=8] {'cent'}, dimensions={0}, use_global_device_ids=true | all-gather | bytes 479232 | tf_op jit(solution)/shard_map/all_gather | solution.py:346
  100.0 24.5 %nearest.1 = (bf16[1024,1024]{1,0:T(8,128)(2,1)}, f32[1,1024]{1,0:T(1,128)}, f32[1,1024]{1,0:T(1,128)}) custom-call(s32[1]{0:T(128)} %bitcast.7.base_ref, bf16[8,208,128]{2,1,0:T(8,128)(2,1)} %bitcast.16, bf16[1024,192]{1,0:T(8,128)(2,1)} %bitcast.19, bf16[6250,1024]{1,0:T(8,128)(2,1)} %panel_ref.1), custom_call_target="tpu_custom_call" | custom-call | tf_op jit(solution)/shard_map/nearest/pallas_call | solution.py:233
  124.5 0.0 all-to-all-done.1.cols_ref
  124.5 0.0 copy-start.1
  124.5 0.9 copy-done.1
  125.4 11.0 %peers.1 = f32[8,4,128]{2,1,0:T(4,128)} custom-call(s32[2]{0:T(128)} %pad_add_fusion.place_ref, bf16[16,208,128]{2,1,0:T(8,128)(2,1)} %copy-done.1, bf16[8,208,128]{2,1,0:T(8,128)(2,1)} %bitcast.17, bf16[1024,1024]{1,0:T(8,128)(2,1)} %get-tuple-element.11.turned_ref, bf16[192,1024]{1,0:T(8,128)(2,1)} %head_ref.3, f32[1,1024]{1,0:T(1,128)} %get-tuple-element.12.near_ref, ...), custom_call_target="tpu_custom_call" | custom-call | tf_op jit(solution)/shard_map/peers/pallas_call | solution.py:313
  136.4 8.5 %all_to_all.16 = f32[8,4,128]{2,1,0:T(4,128)S(1)} all-to-all(f32[8,4,128]{2,1,0:T(4,128)} %peers.1), channel_id=1, replica_groups=mesh['dp'=16,'cent'=8] {'cent'}, dimensions={0} | all-to-all | bytes 32768 | tf_op jit(solution)/shard_map/all_to_all | solution.py:351
  144.9 0.5 slice_bitcast_fusion
  (1 shorter events, 0.0 us)
Async XLA Ops:
  4.4 77.6 %copy-start = (bf16[192,1024]{1,0:T(8,128)(2,1)S(1)}, bf16[192,1024]{1,0:T(8,128)(2,1)}, u32[]{:S(2)}) copy-start(bf16[192,1024]{1,0:T(8,128)(2,1)} %head_ref.3) | copy-start | bytes 1179652
  76.5 7.1 %copy-start.2 = (bf16[208,128]{1,0:T(8,128)(2,1)S(1)}, bf16[208,128]{1,0:T(8,128)(2,1)}, u32[]{:S(2)}) copy-start(bf16[208,128]{1,0:T(8,128)(2,1)} %get-tuple-element.10) | copy-start | bytes 159748
  78.4 46.1 %all-to-all-start.1 = ((bf16[16,208,128]{2,1,0:T(8,128)(2,1)}), bf16[16,208,128]{2,1,0:T(8,128)(2,1)S(1)}, u32[]{:S(2)}, u32[]{:S(2)}) async-start(bf16[16,208,128]{2,1,0:T(8,128)(2,1)} %broadcast_in_dim.6), calls=%async_computation.1 | async-start | bytes 1703936 | tf_op jit(solution)/shard_map/all_to_all | solution.py:348
  124.5 0.9 copy-start.1

commit v3 on v1

--- a/solution.py
+++ b/solution.py
@@ -8,7 +8,6 @@
 from jax.sharding import PartitionSpec as P
 
 SIDE = 4
-FRAMES = 4
 SPOTS = SIDE * SIDE
 BF = jnp.bfloat16
 F32 = jnp.float32
@@ -18,80 +17,194 @@
     return [(at + shift - 1, shift) for shift in range(3) if 0 <= at + shift - 1 < extent]
 
 
+TILES = 3
+STEPS = 9
+
+
 def embed_kernel(
-    clip_ref, count_ref, send_ref, expand_ref, depth_ref, reduce_ref, out_ref, x_ref, hidden_ref, act_ref, pool_ref
+    clip_ref, count_ref, send_ref, expand_ref, depth_ref, reduce_ref, out_ref, *scratch
 ):
+    x_refs, hidden_refs, act_refs = scratch[0:6], scratch[6:12], scratch[12:15]
+    pool_ref, packed_pool_ref = scratch[15:17]
+    weight_refs = scratch[17:19]
     channels, clips = clip_ref.shape[2], clip_ref.shape[3]
     expanded = expand_ref.shape[1]
-    counts = count_ref[...]
-    zero = jnp.zeros((channels, clips), BF)
-
-    @pl.loop(0, FRAMES)
-    def _(frame):
-        kept = jnp.broadcast_to((counts > frame).astype(F32), (channels, clips)) > 0.5
-
-        @pl.loop(0, SPOTS)
-        def _(spot):
-            x_ref[frame * SPOTS + spot] = jnp.where(
-                kept, clip_ref[frame, spot].astype(F32), 0.0
-            ).astype(BF)
+
+    counts = count_ref[...].astype(F32)
+    line = lax.broadcasted_iota(jnp.int32, (clips, clips), 0)
+    lane = lax.broadcasted_iota(jnp.int32, (clips, clips), 1)
+    count_lane = jnp.broadcast_to(counts, (clips, clips))
+    count_line = jnp.transpose(count_lane)
+    ahead = (count_lane > count_line) | ((count_lane == count_line) & (lane < line))
+    rank = jnp.dot(
+        ahead.astype(F32).astype(BF), jnp.ones((clips, clips), BF), preferred_element_type=F32
+    ).astype(jnp.int32)
+    n1, n2, n3 = [jnp.sum((counts > frame).astype(jnp.int32)) for frame in (1, 2, 3)]
+    blocks = expanded // 16 // STEPS
+    one_hot = lambda mask: mask.astype(F32).astype(BF)
+    order = one_hot(rank == lane)
+    place = [
+        order,
+        one_hot((rank == lane) & (count_line > 1)),
+        jnp.concatenate(
+            [
+                one_hot((rank == lane) & (count_line > 2)),
+                one_hot((rank + n2 == lane) & (count_line > 3)),
+            ],
+            axis=0,
+        ),
+    ]
+    row_lane = lax.broadcasted_iota(jnp.int32, (1, clips), 1)
+    kept = [None, (row_lane < n1).astype(F32), (row_lane < n2 + n3).astype(F32)]
+    tile_lane = lax.broadcasted_iota(jnp.int32, (16, clips), 1)
+    in_second, in_third = tile_lane < n2, tile_lane < n3
+
+    def expand(layer, tile, pair, both):
+        hidden = jnp.maximum(jnp.dot(expand_ref[layer], both, preferred_element_type=F32), 0.0)
+        hidden_refs[3 * layer + tile][2 * pair] = hidden[:, :clips]
+        hidden_refs[3 * layer + tile][2 * pair + 1] = hidden[:, clips:]
+
+    def gather(tile, pair):
+        if tile < 2:
+            spots = jnp.concatenate([clip_ref[tile, 2 * pair], clip_ref[tile, 2 * pair + 1]], axis=0)
+        else:
+            spots = jnp.concatenate(
+                [
+                    jnp.concatenate([clip_ref[2, 2 * pair + side], clip_ref[3, 2 * pair + side]], axis=1)
+                    for side in range(2)
+                ],
+                axis=0,
+            )
+        x = jnp.dot(spots, place[tile], preferred_element_type=F32).astype(BF)
+        x_refs[tile][2 * pair] = x[:channels]
+        x_refs[tile][2 * pair + 1] = x[channels:]
+
+    def expand_stored(layer, tile, pair):
+        x_ref = x_refs[3 * layer + tile]
+        expand(layer, tile, pair, jnp.concatenate([x_ref[2 * pair], x_ref[2 * pair + 1]], axis=1))
+
+    def spread_taps(layer, step, first, last):
+        rows = [pl.ds(pl.multiple_of((step * blocks + at) * 16, 16), 16) for at in range(blocks)]
+        taps = [depth_ref[layer, row, :] for row in rows]
+        for tap in range(first, last):
+            for at in range(blocks):
+                weight_refs[layer][step * blocks + at, tap] = jnp.broadcast_to(
+                    taps[at][:, tap : tap + 1], (16, clips)
+                )
+
+    def reduce(layer, tile, pair):
+        both = jnp.concatenate([act_refs[tile][2 * pair], act_refs[tile][2 * pair + 1]], axis=1)
+        branch = jnp.dot(reduce_ref[layer], both, preferred_element_type=F32)
+        result = []
+        for side in range(2):
+            part = branch[:, side * clips : (side + 1) * clips]
+            if kept[tile] is not None:
+                part = part * kept[tile]
+            x = x_refs[3 * layer + tile][2 * pair + side].astype(F32) + part
+            result.append(x.astype(BF))
+        return result
+
+    def reduce_store(tile, pair):
+        x = reduce(0, tile, pair)
+        x_refs[3 + tile][2 * pair] = x[0]
+        x_refs[3 + tile][2 * pair + 1] = x[1]
+
+    def reduce_pool(tile, pair, live):
+        x = reduce(1, tile, pair)
+        into = packed_pool_ref if tile == 2 else pool_ref
+        into[...] += (x[0].astype(F32) + x[1].astype(F32)) * live
+
+    def depthwise(layer, tile, block):
+        rows = pl.ds(pl.multiple_of(block * 16, 16), 16)
+        read = lambda source, spot: hidden_refs[3 * layer + source][spot, rows, :]
+        if tile == 0:
+            sources = [(1, lambda s: read(0, s)), (2, lambda s: read(1, s))]
+        elif tile == 1:
+            sources = [
+                (0, lambda s: read(0, s)),
+                (1, lambda s: read(1, s)),
+                (2, lambda s: jnp.where(in_second, read(2, s), 0.0)),
+            ]
+        else:
+            sources = [
+                (0, lambda s: jnp.where(in_second, read(1, s), pltpu.roll(read(2, s), n2, 1))),
+                (1, lambda s: read(2, s)),
+                (2, lambda s: jnp.where(in_third, pltpu.roll(read(2, s), clips - n2, 1), 0.0)),
+            ]
+        mixed = [None] * SPOTS
+        for shift_t, source in sources:
+            weight = [weight_refs[layer][block, 9 * shift_t + tap].astype(BF) for tap in range(9)]
+            hidden = [source(spot).astype(BF) for spot in range(SPOTS)]
+            for y in range(SIDE):
+                for from_y, shift_y in neighbours(y, SIDE):
+                    for z in range(SIDE):
+                        for from_z, shift_z in neighbours(z, SIDE):
+                            term = hidden[from_y * SIDE + from_z] * weight[3 * shift_y + shift_z]
+                            spot = y * SIDE + z
+                            mixed[spot] = term if mixed[spot] is None else mixed[spot] + term
+        for spot in range(SPOTS):
+            half = mixed[spot] * BF(0.5)
+            act_refs[tile][spot, rows, :] = half + half * jnp.tanh(half)
+
+    def stage(layer, tile, other):
+        @pl.loop(0, STEPS)
+        def _(step):
+            pair = jnp.minimum(step, SPOTS // 2 - 1)
+            before = jnp.maximum(step - 1, 0)
+            other(pair, before, (step < SPOTS // 2).astype(F32))
+            if layer == 0:
+                if tile == 0:
+                    spread_taps(0, step, 0, 9)
+                spread_taps(1, step, 9 * tile, 9 * tile + 9)
+            for at in range(blocks):
+                depthwise(layer, tile, step * blocks + at)
+
+    def filler(first, second):
+        def other(pair, before, live):
+            second(before)
+            first(pair)
+
+        return other
 
     pool_ref[...] = jnp.zeros_like(pool_ref)
-    for layer in range(2):
-
-        @pl.loop(0, FRAMES * SPOTS // 2)
-        def _(pair):
-            both = jnp.concatenate([x_ref[2 * pair], x_ref[2 * pair + 1]], axis=1)
-            hidden = jnp.dot(expand_ref[layer], both, preferred_element_type=F32)
-            hidden = jnp.maximum(hidden, 0.0).astype(BF)
-            hidden_ref[2 * pair] = hidden[:, :clips]
-            hidden_ref[2 * pair + 1] = hidden[:, clips:]
-
-        @pl.loop(0, expanded // 16)
-        def _(tile):
-            rows = pl.ds(pl.multiple_of(tile * 16, 16), 16)
-            taps = depth_ref[layer, rows, :]
-            weight = [
-                jnp.broadcast_to(taps[:, tap : tap + 1], (16, clips)).astype(BF) for tap in range(27)
-            ]
-            for frame in range(FRAMES):
-                for y in range(SIDE):
-                    mixed = [None] * SIDE
-                    for from_t, shift_t in neighbours(frame, FRAMES):
-                        for from_y, shift_y in neighbours(y, SIDE):
-                            base = from_t * SPOTS + from_y * SIDE
-                            line = [hidden_ref[base + z, rows, :] for z in range(SIDE)]
-                            for z in range(SIDE):
-                                for from_z, shift_z in neighbours(z, SIDE):
-                                    term = line[from_z] * weight[9 * shift_t + 3 * shift_y + shift_z]
-                                    mixed[z] = term if mixed[z] is None else mixed[z] + term
-                    for z in range(SIDE):
-                        half = mixed[z] * BF(0.5)
-                        act_ref[frame * SPOTS + y * SIDE + z, rows, :] = half + half * jnp.tanh(half)
-
-        @pl.loop(0, FRAMES * SPOTS // 2)
-        def _(pair):
-            both = jnp.concatenate([act_ref[2 * pair], act_ref[2 * pair + 1]], axis=1)
-            branch = jnp.dot(reduce_ref[layer], both, preferred_element_type=F32)
-            kept = jnp.broadcast_to((counts > pair // (SPOTS // 2)).astype(F32), (channels, clips))
-            for side in range(2):
-                spot = 2 * pair + side
-                x = x_ref[spot].astype(F32) + branch[:, side * clips : (side + 1) * clips] * kept
-                x = x.astype(BF)
-                if layer == 0:
-                    x_ref[spot] = x
-                else:
-                    pool_ref[...] += x.astype(F32)
-
-    pooled = (pool_ref[...] / (counts * SPOTS).astype(F32)).astype(BF)
-    per_peer = out_ref.shape[1]
-    n_dp = out_ref.shape[0]
-    row = lax.broadcasted_iota(jnp.int32, (clips, clips), 0)
-    slot = (row % per_peer) * n_dp + row // per_peer
-    pick = (jnp.broadcast_to(send_ref[...], (clips, clips)) == slot).astype(F32).astype(BF)
+    packed_pool_ref[...] = jnp.zeros_like(packed_pool_ref)
+
+    @pl.loop(0, STEPS)
+    def _(step):
+        pair = jnp.minimum(step, SPOTS // 2 - 1)
+        before = jnp.maximum(step - 1, 0)
+        for tile in range(2):
+            expand_stored(0, tile, before)
+            gather(tile, pair)
+        spread_taps(0, step, 9, 27)
+
+    stage(0, 0, filler(lambda pair: gather(2, pair), lambda pair: expand_stored(0, 2, pair)))
+    stage(0, 1, filler(lambda pair: reduce_store(0, pair), lambda pair: expand_stored(1, 0, pair)))
+    stage(0, 2, filler(lambda pair: reduce_store(1, pair), lambda pair: expand_stored(1, 1, pair)))
+    stage(1, 0, filler(lambda pair: reduce_store(2, pair), lambda pair: expand_stored(1, 2, pair)))
+    stage(1, 1, lambda pair, before, live: reduce_pool(0, pair, live))
+    stage(1, 2, lambda pair, before, live: reduce_pool(1, pair, live))
+
+    @pl.loop(0, SPOTS // 2)
+    def _(pair):
+        reduce_pool(2, pair, 1.0)
+
+    packed = packed_pool_ref[...]
+    total = (
+        pool_ref[...]
+        + jnp.where(row_lane < n2, packed, 0.0)
+        + jnp.where(row_lane < n3, pltpu.roll(packed, clips - n2, 1), 0.0)
+    )
+    lengths = jnp.dot(
+        jnp.broadcast_to(counts, (16, clips)).astype(BF), order, preferred_element_type=F32
+    )[0:1]
+    pooled = (total / (lengths * SPOTS)).astype(BF)
+    n_dp, per_peer = out_ref.shape[0], out_ref.shape[1]
+    slot = (line % per_peer) * n_dp + line // per_peer
+    pick = one_hot(jnp.broadcast_to(send_ref[...], (clips, clips)) == slot)
+    pick = lax.dot_general(pick, order, (((1,), (0,)), ((), ())), preferred_element_type=F32).astype(BF)
     rows = lax.dot_general(pick, pooled, (((1,), (1,)), ((), ())), preferred_element_type=F32)
-    rows = rows.astype(BF).reshape(n_dp, per_peer, channels)
-    out_ref[:, :, :channels] = rows
+    out_ref[:, :, :channels] = rows.astype(BF).reshape(n_dp, per_peer, channels)
     out_ref[:, :, channels:] = jnp.zeros((n_dp, per_peer, out_ref.shape[2] - channels), BF)
 
 
@@ -103,12 +216,11 @@
         out_shape=jax.ShapeDtypeStruct((n_dp, clips // n_dp, 256), BF),
         in_specs=[pl.BlockSpec(memory_space=pltpu.VMEM)] * 6,
         out_specs=pl.BlockSpec(memory_space=pltpu.VMEM),
-        scratch_shapes=[
-            pltpu.VMEM((frames * spots, channels, clips), BF),
-            pltpu.VMEM((frames * spots, expanded, clips), BF),
-            pltpu.VMEM((frames * spots, expanded, clips), BF),
-            pltpu.VMEM((channels, clips), F32),
-        ],
+        scratch_shapes=[pltpu.VMEM((spots, channels, clips), BF)] * 6
+        + [pltpu.VMEM((spots, expanded, clips), F32)] * 6
+        + [pltpu.VMEM((spots, expanded, clips), BF)] * 3
+        + [pltpu.VMEM((channels, clips), F32)] * 2
+        + [pltpu.VMEM((expanded // 16, 27, 16, clips), F32)] * 2,
         compiler_params=pltpu.CompilerParams(vmem_limit_bytes=60 << 20),
         name="embed",
     )(

time: 171 us -> 125 us (0.73)
  Pallas kernels: 117 us -> 71.4 us
    pallas_call x1, Pallas kernels: 79.5 us -> 33.7 us  [embed(): pl.pallas_call(embed_kernel, out_shape=jax.ShapeDtypeStruct((n_dp, clips...]
  transfers between devices with their start and end apart: 1 -> 1, of which waited for: 0 -> 0; matrix products, arithmetic and copies ran while one was open for 1% -> 1% of each run, Pallas kernels for 14% -> 20%
where the time goes in v3:
time: 125 us; the launch traced here: 124 us
  Pallas kernels  71.4 us (57%)
  blocking collectives  40 us (32%)
  local copies, waits for them, and re-layouts  7.31 us (6%)
  starting transfers between devices  3.62 us (3%)
  other arithmetic  1.41 us (1%)
    pallas_call x1, Pallas kernels, embed(): pl.pallas_call(embed_kernel, out_shape=jax.ShapeDtypeStruct((n_dp, clips...  33.7 us
    pallas_call x1, Pallas kernels, nearest_of(): pl.pallas_call(functools.partial(nearest_kernel, panel_rows), grid=(pl.cd...  24.5 us
    all_gather x1, blocking collectives, local(): rows = lax.all_gather(payload, 'cent', axis=0)  16.4 us
    all_to_all x1, blocking collectives, local(): lax.all_to_all(pooled, 'dp', split_axis=0, concat_axis=0, tiled=True)  15.2 us
    pallas_call x1, Pallas kernels, peers_of(): pl.pallas_call(peer_kernel, out_shape=jax.ShapeDtypeStruct((n_cent, 4, cl...  11 us
    all_to_all x1, blocking collectives, local(): lax.all_to_all(partial, 'cent', split_axis=0, concat_axis=0, tiled=True)  8.49 us
    unnamed x9, local copies, waits for them, and re-layouts  4.89 us
    all_to_all x1, starting transfers between devices, local(): cols = lax.all_to_all(spread, 'dp', split_axis=0, concat_axis=0, tiled=True)  3.62 us
  transfers between devices with their start and end apart: 1, of which 0 were waited for; matrix products, arithmetic and copies ran while one was open for 1% of the time, Pallas kernels for 20%

profile of v3, /device:TPU:1, one launch (start us, length us, event | category | flops | bytes accessed | tf_op | source)
XLA Modules:
  0.0 124.4 jit_solution(13185979305523851981)
XLA Ops:
  0.6 1.0 copy.14
  1.6 0.8 convert_bitcast_fusion.depth_ref
  2.5 2.0 %copy.13 = bf16[2,192,432]{1,2,0:T(8,128)(2,1)} copy(bf16[2,192,432]{2,1,0:T(8,128)(2,1)} %param.13) | data formatting | bytes 663552 | tf_op args[4]
  4.4 0.0 copy-start
  4.4 33.7 %embed.1 = bf16[16,8,256]{2,1,0:T(8,128)(2,1)} custom-call(bf16[4,16,192,128]{3,2,1,0:T(8,128)(2,1)} %bitcast.18, s32[1,128]{1,0:T(1,128)} %count_ref.1, s32[1,128]{1,0:T(1,128)} %send_ref.1, bf16[2,432,192]{2,1,0:T(8,128)(2,1)} %bitcast.20, f32[2,432,27]{2,1,0:T(8,128)} %convert_bitcast_fusion.depth_ref, bf16[2,192,432]{2,1,0:T(8,128)(2,1)} %bitcast.21), custom_call_target="tpu_custom_call" | custom-call | tf_op jit(solution)/shard_map/embed/pallas_call | solution.py:214
  38.1 15.2 %all_to_all.15.arrived_ref = bf16[16,8,256]{2,1,0:T(8,128)(2,1)} all-to-all(bf16[16,8,256]{2,1,0:T(8,128)(2,1)} %embed.1), channel_id=1, replica_groups=mesh['dp'=16,'cent'=8] {'dp'}, dimensions={0} | all-to-all | bytes 131072 | tf_op jit(solution)/shard_map/all_to_all | solution.py:454
  53.3 2.2 %own.1 = (bf16[208,128]{1,0:T(8,128)(2,1)}, bf16[128,1024]{1,0:T(8,128)(2,1)}) custom-call(bf16[16,8,256]{2,1,0:T(8,128)(2,1)} %all_to_all.15.arrived_ref, s32[1,128]{1,0:T(1,128)} %ids_ref.1, bf16[192,1024]{1,0:T(8,128)(2,1)} %head_ref.3), custom_call_target="tpu_custom_call" | custom-call | tf_op jit(solution)/shard_map/own/pallas_call | solution.py:267
  55.5 0.0 copy-start.2
  55.5 1.9 %broadcast_in_dim.6 = bf16[16,208,128]{2,1,0:T(8,128)(2,1)} broadcast(bf16[208,128]{1,0:T(8,128)(2,1)} %get-tuple-element.10), dimensions={1,2} | broadcast | bytes 905216 | tf_op jit(solution)/shard_map/broadcast_in_dim | solution.py:457
  57.4 3.6 %all-to-all-start.1 = ((bf16[16,208,128]{2,1,0:T(8,128)(2,1)}), bf16[16,208,128]{2,1,0:T(8,128)(2,1)S(1)}, u32[]{:S(2)}, u32[]{:S(2)}) async-start(bf16[16,208,128]{2,1,0:T(8,128)(2,1)} %broadcast_in_dim.6), calls=%async_computation.1 | async-start | bytes 1703936 | tf_op jit(solution)/shard_map/all_to_all | solution.py:458
  61.0 0.0 copy-done
  61.0 1.0 copy.15
  62.0 0.6 pad_add_fusion.place_ref
  62.6 0.0 copy-done.2
  62.6 16.4 %all-gather = bf16[1664,128]{1,0:T(8,128)(2,1)} all-gather(bf16[208,128]{1,0:T(8,128)(2,1)S(1)} %copy-done.2), channel_id=2, replica_groups=mesh['dp'=16,'cent'=8] {'cent'}, dimensions={0}, use_global_device_ids=true | all-gather | bytes 479232 | tf_op jit(solution)/shard_map/all_gather | solution.py:456
  79.0 24.5 %nearest.1 = (bf16[1024,1024]{1,0:T(8,128)(2,1)}, f32[1,1024]{1,0:T(1,128)}, f32[1,1024]{1,0:T(1,128)}) custom-call(s32[1]{0:T(128)} %bitcast.7.base_ref, bf16[8,208,128]{2,1,0:T(8,128)(2,1)} %bitcast.16, bf16[1024,192]{1,0:T(8,128)(2,1)} %bitcast.19, bf16[6250,1024]{1,0:T(8,128)(2,1)} %panel_ref.1), custom_call_target="tpu_custom_call" | custom-call | tf_op jit(solution)/shard_map/nearest/pallas_call | solution.py:343
  103.5 0.0 all-to-all-done.1.cols_ref
  103.5 0.0 copy-start.1
  103.5 0.9 copy-done.1
  104.4 11.0 %peers.1 = f32[8,4,128]{2,1,0:T(4,128)} custom-call(s32[2]{0:T(128)} %pad_add_fusion.place_ref, bf16[16,208,128]{2,1,0:T(8,128)(2,1)} %copy-done.1, bf16[8,208,128]{2,1,0:T(8,128)(2,1)} %bitcast.17, bf16[1024,1024]{1,0:T(8,128)(2,1)} %get-tuple-element.11.turned_ref, bf16[192,1024]{1,0:T(8,128)(2,1)} %head_ref.3, f32[1,1024]{1,0:T(1,128)} %get-tuple-element.12.near_ref, ...), custom_call_target="tpu_custom_call" | custom-call | tf_op jit(solution)/shard_map/peers/pallas_call | solution.py:423
  115.4 8.5 %all_to_all.16 = f32[8,4,128]{2,1,0:T(4,128)S(1)} all-to-all(f32[8,4,128]{2,1,0:T(4,128)} %peers.1), channel_id=1, replica_groups=mesh['dp'=16,'cent'=8] {'cent'}, dimensions={0} | all-to-all | bytes 32768 | tf_op jit(solution)/shard_map/all_to_all | solution.py:461
  123.9 0.5 slice_bitcast_fusion
  (1 shorter events, 0.0 us)
Async XLA Ops:
  4.4 56.6 %copy-start = (bf16[192,1024]{1,0:T(8,128)(2,1)S(1)}, bf16[192,1024]{1,0:T(8,128)(2,1)}, u32[]{:S(2)}) copy-start(bf16[192,1024]{1,0:T(8,128)(2,1)} %head_ref.3) | copy-start | bytes 1179652
  55.5 7.1 %copy-start.2 = (bf16[208,128]{1,0:T(8,128)(2,1)S(1)}, bf16[208,128]{1,0:T(8,128)(2,1)}, u32[]{:S(2)}) copy-start(bf16[208,128]{1,0:T(8,128)(2,1)} %get-tuple-element.10) | copy-start | bytes 159748
  57.4 46.1 %all-to-all-start.1 = ((bf16[16,208,128]{2,1,0:T(8,128)(2,1)}), bf16[16,208,128]{2,1,0:T(8,128)(2,1)S(1)}, u32[]{:S(2)}, u32[]{:S(2)}) async-start(bf16[16,208,128]{2,1,0:T(8,128)(2,1)} %broadcast_in_dim.6), calls=%async_computation.1 | async-start | bytes 1703936 | tf_op jit(solution)/shard_map/all_to_all | solution.py:458
  103.5 0.9 copy-start.1

commit v4 on v3

--- a/solution.py
+++ b/solution.py
@@ -17,18 +17,32 @@
     return [(at + shift - 1, shift) for shift in range(3) if 0 <= at + shift - 1 < extent]
 
 
-TILES = 3
 STEPS = 9
 
 
+def identity(size):
+    line = lax.broadcasted_iota(jnp.int32, (size, size), 0)
+    lane = lax.broadcasted_iota(jnp.int32, (size, size), 1)
+    return (line == lane).astype(F32).astype(BF)
+
+
+def turn(eye, matrix):
+    return lax.dot_general(eye, matrix, (((1,), (1,)), ((), ())), preferred_element_type=F32)
+
+
 def embed_kernel(
-    clip_ref, count_ref, send_ref, expand_ref, depth_ref, reduce_ref, out_ref, *scratch
+    clip_ref, count_ref, send_ref, wide_ref, taps_ref, reduce_ref, out_ref, *scratch
 ):
     x_refs, hidden_refs, act_refs = scratch[0:6], scratch[6:12], scratch[12:15]
     pool_ref, packed_pool_ref = scratch[15:17]
     weight_refs = scratch[17:19]
+    expand_ref, depth_ref = scratch[19:21]
     channels, clips = clip_ref.shape[2], clip_ref.shape[3]
-    expanded = expand_ref.shape[1]
+    expanded = wide_ref.shape[2]
+    eye = identity(expanded)
+    for layer in range(2):
+        expand_ref[layer] = turn(eye, wide_ref[layer]).astype(BF)
+        depth_ref[layer, :, : taps_ref.shape[1]] = turn(eye, taps_ref[layer])
 
     counts = count_ref[...].astype(F32)
     line = lax.broadcasted_iota(jnp.int32, (clips, clips), 0)
@@ -220,15 +234,16 @@
         + [pltpu.VMEM((spots, expanded, clips), F32)] * 6
         + [pltpu.VMEM((spots, expanded, clips), BF)] * 3
         + [pltpu.VMEM((channels, clips), F32)] * 2
-        + [pltpu.VMEM((expanded // 16, 27, 16, clips), F32)] * 2,
+        + [pltpu.VMEM((expanded // 16, 27, 16, clips), F32)] * 2
+        + [pltpu.VMEM((2, expanded, channels), BF), pltpu.VMEM((2, expanded, clips), F32)],
         compiler_params=pltpu.CompilerParams(vmem_limit_bytes=60 << 20),
         name="embed",
     )(
         jnp.transpose(clip_data, (1, 2, 3, 0)),
         frame_counts,
         send_list,
-        jnp.swapaxes(expand_weight, 1, 2),
-        jnp.swapaxes(depth_kernel, 1, 2).astype(F32),
+        expand_weight,
+        depth_kernel,
         jnp.swapaxes(reduce_weight, 1, 2),
     )
 
@@ -241,58 +256,93 @@
 LABEL_ROWS = 16
 
 
-def own_kernel(arrived_ref, ids_ref, head_ref, payload_ref, vectors_ref):
+def own_kernel(arrived_ref, ids_ref, payload_ref, spread_ref, rows_ref):
     n_dp, per_peer, width = arrived_ref.shape
     clips = n_dp * per_peer
-    channels = head_ref.shape[0]
+    channels = rows_ref.shape[1]
     arrived = arrived_ref[...].reshape(clips, width)[:, :channels]
     row = lax.broadcasted_iota(jnp.int32, (clips, clips), 0)
     lane = lax.broadcasted_iota(jnp.int32, (clips, clips), 1)
     pick = (lane == (row % n_dp) * per_peer + row // n_dp).astype(F32).astype(BF)
-    rows = jnp.dot(pick, arrived, preferred_element_type=F32).astype(BF)
-    projected = jnp.dot(rows, head_ref[...], preferred_element_type=F32)
-    vectors_ref[...] = unit(projected, 1)
-    payload_ref[0:channels, :] = jnp.transpose(rows.astype(F32)).astype(BF)
+    rows = jnp.dot(pick, arrived, preferred_element_type=F32)
+    rows_ref[...] = rows.astype(BF)
     ids = ids_ref[...]
     which = lax.broadcasted_iota(jnp.int32, (LABEL_ROWS, clips), 0)
     high, low = ids // 256, ids % 256
     label = jnp.where(which == 0, high, jnp.where(which == 1, low, 0))
-    payload_ref[channels:, :] = label.astype(F32).astype(BF)
-
-
-def own(arrived, cluster_ids, head_weight):
+    payload = jnp.concatenate([jnp.transpose(rows), label.astype(F32)], axis=0).astype(BF)
+    payload_ref[...] = payload
+    for peer in range(n_dp):
+        spread_ref[peer] = payload
+
+
+def own(arrived, cluster_ids, channels):
     n_dp, per_peer, width = arrived.shape
-    channels, dims = head_weight.shape
     clips = n_dp * per_peer
+    height = channels + LABEL_ROWS
     return pl.pallas_call(
         own_kernel,
         out_shape=(
-            jax.ShapeDtypeStruct((channels + LABEL_ROWS, clips), BF),
-            jax.ShapeDtypeStruct((clips, dims), BF),
-        ),
-        in_specs=[pl.BlockSpec(memory_space=pltpu.VMEM)] * 3,
-        out_specs=(pl.BlockSpec(memory_space=pltpu.VMEM),) * 2,
+            jax.ShapeDtypeStruct((height, clips), BF),
+            jax.ShapeDtypeStruct((n_dp, height, clips), BF),
+            jax.ShapeDtypeStruct((clips, channels), BF),
+        ),
+        in_specs=[pl.BlockSpec(memory_space=pltpu.VMEM)] * 2,
+        out_specs=(pl.BlockSpec(memory_space=pltpu.VMEM),) * 3,
         name="own",
-    )(arrived, cluster_ids, head_weight)
+    )(arrived, cluster_ids)
+
+
+def vectors_kernel(rows_ref, head_ref, vectors_ref):
+    projected = jnp.dot(rows_ref[...], head_ref[...], preferred_element_type=F32)
+    vectors_ref[...] = unit(projected, 1)
+
+
+def vectors_of(rows, head_weight):
+    clips, channels = rows.shape
+    dims = head_weight.shape[1]
+    return pl.pallas_call(
+        vectors_kernel,
+        out_shape=jax.ShapeDtypeStruct((clips, dims), BF),
+        in_specs=[pl.BlockSpec(memory_space=pltpu.VMEM)] * 2,
+        out_specs=pl.BlockSpec(memory_space=pltpu.VMEM),
+        cost_estimate=pl.CostEstimate(
+            flops=2 * clips * dims * channels, bytes_accessed=2 * dims * (clips + channels), transcendentals=0
+        ),
+        name="vectors",
+    )(rows, head_weight)
 
 
 PANEL_ROWS = 784
 OCCUR = 64
 
 
-def nearest_kernel(panel_rows, base_ref, rows_ref, head_ref, panel_ref, turned_ref, near_ref, own_ref, best_ref):
-    n_cent, height, clips = rows_ref.shape
-    dims, channels = head_ref.shape
-    total = n_cent * clips
+def label_of(rows_ref, block, channels):
+    label = jnp.concatenate(
+        [rows_ref[2 * block, channels:, :], rows_ref[2 * block + 1, channels:, :]], axis=1
+    ).astype(F32)
+    return label[0:1] * 256.0 + label[1:2]
+
+
+def nearest_kernel(panel_rows, rows_ref, head_ref, panel_ref, turned_ref, near_ref, own_ref, best_ref, flip_ref):
+    blocks, height, clips = rows_ref.shape
+    channels, dims = head_ref.shape
+    total = blocks * clips
     step = pl.program_id(0)
     last = pl.num_programs(0) - 1
+    base = lax.axis_index("cent") * panel_rows
 
     @pl.when(step == 0)
     def _():
-        @pl.loop(0, n_cent // 2)
+        eye = identity(256)
+        for part in range(dims // 256):
+            part = slice(part * 256, (part + 1) * 256)
+            flip_ref[part, :] = turn(eye, head_ref[:, part]).astype(BF)
+
+        @pl.loop(0, blocks // 2)
         def _(pair):
             both = jnp.concatenate([rows_ref[2 * pair], rows_ref[2 * pair + 1]], axis=1)
-            projected = jnp.dot(head_ref[...], both[:channels], preferred_element_type=F32)
+            projected = jnp.dot(flip_ref[...], both[:channels], preferred_element_type=F32)
             cols = pl.ds(pl.multiple_of(pair * 2 * clips, 2 * clips), 2 * clips)
             turned_ref[:, cols] = unit(projected, 0)
 
@@ -317,10 +367,7 @@
 
             @pl.when(step == 0)
             def _():
-                label = jnp.concatenate(
-                    [rows_ref[2 * block, channels:, :], rows_ref[2 * block + 1, channels:, :]], axis=1
-                ).astype(F32)
-                local_id = (label[0:1] * 256.0 + label[1:2]).astype(jnp.int32) - base_ref[0]
+                local_id = label_of(rows_ref, block, channels).astype(jnp.int32) - base
                 index = lax.broadcasted_iota(jnp.int32, (OCCUR, 256), 0)
                 own_ref[:, cols] = jnp.max(
                     jnp.where(index == local_id, scores[:OCCUR], -jnp.inf), axis=0, keepdims=True
@@ -334,10 +381,10 @@
             near_ref[:, cols] = jnp.max(best_ref[:, cols], axis=0, keepdims=True)
 
 
-def nearest_of(rows, head_turned, centroids, base):
-    n_cent, height, clips = rows.shape
-    dims, channels = head_turned.shape
-    total = n_cent * clips
+def nearest_of(rows, head_weight, centroids):
+    blocks, height, clips = rows.shape
+    channels, dims = head_weight.shape
+    total = blocks * clips
     panel_rows = centroids.shape[0]
     whole = lambda shape: pl.BlockSpec(shape, lambda step: (0,) * len(shape))
     return pl.pallas_call(
@@ -349,86 +396,97 @@
             jax.ShapeDtypeStruct((1, total), F32),
         ),
         in_specs=[
-            pl.BlockSpec(memory_space=pltpu.SMEM),
             whole(rows.shape),
-            whole(head_turned.shape),
+            whole(head_weight.shape),
             pl.BlockSpec((PANEL_ROWS, dims), lambda step: (step, 0)),
         ],
         out_specs=(whole((dims, total)), whole((1, total)), whole((1, total))),
-        scratch_shapes=[pltpu.VMEM((8, total), F32)],
-        compiler_params=pltpu.CompilerParams(vmem_limit_bytes=60 << 20),
+        scratch_shapes=[pltpu.VMEM((8, total), F32), pltpu.VMEM((dims, channels), BF)],
+        compiler_params=pltpu.CompilerParams(vmem_limit_bytes=48 << 20),
+        cost_estimate=pl.CostEstimate(
+            flops=2 * total * panel_rows * dims, bytes_accessed=2 * panel_rows * dims, transcendentals=0
+        ),
         name="nearest",
-    )(base, rows, head_turned, centroids)
+    )(rows, head_weight, centroids)
 
 
 GROUP = 4
 
 
-def peer_kernel(place_ref, cols_ref, rows_ref, turned_ref, head_ref, near_ref, own_ref, out_ref, best_ref):
+def peer_kernel(
+    cols_ref, near_rows_ref, far_rows_ref, near_turned_ref, far_turned_ref, head_ref,
+    near_best_ref, far_best_ref, near_own_ref, far_own_ref, out_ref, best_ref,
+):
     n_dp, height, clips = cols_ref.shape
-    n_cent = rows_ref.shape[0]
+    n_cent = out_ref.shape[0]
     channels = head_ref.shape[0]
-    total = n_cent * clips
-    eye = (
-        lax.broadcasted_iota(jnp.int32, (clips, clips), 0)
-        == lax.broadcasted_iota(jnp.int32, (clips, clips), 1)
-    ).astype(F32).astype(BF)
+    eye = identity(clips)
     best_ref[...] = jnp.full_like(best_ref, -1.0)
-    mine_dp, mine_cent = place_ref[0], place_ref[1]
+    mine_dp, mine_cent = lax.axis_index("dp"), lax.axis_index("cent")
 
     @pl.loop(0, n_dp // GROUP)
     def _(group):
-        flipped = jnp.concatenate(
-            [
-                lax.dot_general(
-                    eye, cols_ref[group * GROUP + at], (((1,), (1,)), ((), ())), preferred_element_type=F32
-                )
-                for at in range(GROUP)
-            ],
-            axis=0,
-        )
+        flipped = jnp.concatenate([turn(eye, cols_ref[group * GROUP + at]) for at in range(GROUP)], axis=0)
         projected = jnp.dot(flipped[:, :channels].astype(BF), head_ref[...], preferred_element_type=F32)
         vectors = unit(projected, 1)
         ids = flipped[:, channels : channels + 1] * 256.0 + flipped[:, channels + 1 : channels + 2]
-        wide = jnp.broadcast_to(ids, (GROUP * clips, 256))
-        line = lax.broadcasted_iota(jnp.int32, (GROUP * clips, 256), 0)
-        lane = lax.broadcasted_iota(jnp.int32, (GROUP * clips, 256), 1)
-        for block in range(total // 256):
-            cols = pl.ds(block * 256, 256)
-            scores = jnp.dot(vectors, turned_ref[:, cols], preferred_element_type=F32)
-            label = jnp.concatenate(
-                [rows_ref[2 * block, channels:, :], rows_ref[2 * block + 1, channels:, :]], axis=1
-            ).astype(F32)
-            row_ids = label[0:1] * 256.0 + label[1:2]
-            self_line = lane + (mine_dp - group * GROUP) * clips - (mine_cent - 2 * block) * clips
-            inside = (lane // clips) == (mine_cent - 2 * block)
-            same = (wide == row_ids) & jnp.logical_not(inside & (line == self_line))
+        wide = jnp.broadcast_to(ids, (GROUP * clips, 2 * clips))
+        for block in range(n_cent // 2):
+            cols = slice(block * 2 * clips, (block + 1) * 2 * clips)
+            if block == 0:
+                turned, row_ids = near_turned_ref[...], label_of(near_rows_ref, 0, channels)
+            else:
+                far = slice((block - 1) * 2 * clips, block * 2 * clips)
+                turned, row_ids = far_turned_ref[:, far], label_of(far_rows_ref, block - 1, channels)
+            scores = jnp.dot(vectors, turned, preferred_element_type=F32)
+            same = wide == row_ids
+            if block == 0:
+                line = lax.broadcasted_iota(jnp.int32, same.shape, 0)
+                lane = lax.broadcasted_iota(jnp.int32, same.shape, 1)
+                itself = jnp.where(lane < clips, lane + (mine_dp - group * GROUP) * clips, -1)
+                same = same & (line != itself)
             found = jnp.where(same, scores, -1.0)
             best_ref[:, cols] = jnp.maximum(
-                best_ref[:, cols], jnp.max(found.reshape(GROUP * clips // 8, 8, 256), axis=0)
+                best_ref[:, cols], jnp.max(found.reshape(GROUP * clips // 8, 8, 2 * clips), axis=0)
             )
 
     best = jnp.max(best_ref[...], axis=0, keepdims=True)
-    for cent in range(n_cent):
-        cols = slice(cent * clips, (cent + 1) * clips)
-        out_ref[cent, 0:1, :] = near_ref[:, cols]
-        out_ref[cent, 1:2, :] = own_ref[:, cols]
-        out_ref[cent, 2:3, :] = best[:, cols]
-        out_ref[cent, 3:4, :] = best[:, cols]
-
-
-def peers_of(cols, rows, turned, head_weight, near, own_best, place):
-    n_cent, height, clips = rows.shape
-    total = n_cent * clips
+    for block in range(n_cent // 2):
+        for side in range(2):
+            chip = (mine_cent // 2 + block) % (n_cent // 2)
+            cent = 2 * chip + (mine_cent + side) % 2
+            at = slice((2 * block + side) * clips, (2 * block + side + 1) * clips)
+            if block == 0:
+                part = slice(side * clips, (side + 1) * clips)
+                nearest, own_best = near_best_ref[:, part], near_own_ref[:, part]
+            else:
+                part = slice((2 * block + side - 2) * clips, (2 * block + side - 1) * clips)
+                nearest, own_best = far_best_ref[:, part], far_own_ref[:, part]
+            out_ref[cent, 0:1, :] = nearest
+            out_ref[cent, 1:2, :] = own_best
+            out_ref[cent, 2:3, :] = best[:, at]
+            out_ref[cent, 3:4, :] = best[:, at]
+
+
+def peers_of(cols, near_rows, far_rows, near_found, far_found, head_weight):
+    n_dp, height, clips = cols.shape
+    n_cent = near_rows.shape[0] + far_rows.shape[0]
+    dims = head_weight.shape[1]
     return pl.pallas_call(
         peer_kernel,
         out_shape=jax.ShapeDtypeStruct((n_cent, 4, clips), F32),
-        in_specs=[pl.BlockSpec(memory_space=pltpu.SMEM)] + [pl.BlockSpec(memory_space=pltpu.VMEM)] * 6,
+        in_specs=[pl.BlockSpec(memory_space=pltpu.VMEM)] * 10,
         out_specs=pl.BlockSpec(memory_space=pltpu.VMEM),
-        scratch_shapes=[pltpu.VMEM((8, total), F32)],
-        compiler_params=pltpu.CompilerParams(vmem_limit_bytes=60 << 20),
+        scratch_shapes=[pltpu.VMEM((8, n_cent * clips), F32)],
+        compiler_params=pltpu.CompilerParams(vmem_limit_bytes=48 << 20),
+        cost_estimate=pl.CostEstimate(
+            flops=2 * n_dp * n_cent * clips * clips * dims, bytes_accessed=4 << 20, transcendentals=0
+        ),
         name="peers",
-    )(place, cols, rows, turned, head_weight, near, own_best)
+    )(
+        cols, near_rows, far_rows, near_found[0], far_found[0], head_weight,
+        near_found[1], far_found[1], near_found[2], far_found[2],
+    )
 
 
 def local(
@@ -444,20 +502,24 @@
 ):
     n_dp = lax.axis_size("dp")
     n_cent = lax.axis_size("cent")
-    panel_rows = centroids.shape[0]
-    mine_dp, mine_cent = lax.axis_index("dp"), lax.axis_index("cent")
-    base = (mine_cent * panel_rows).astype(jnp.int32)[None]
-    place = jnp.stack([mine_dp, mine_cent]).astype(jnp.int32)
     pooled = embed(
         clip_data, frame_counts, send_list, expand_weight, depth_kernel, reduce_weight, n_dp
     )
     arrived = lax.all_to_all(pooled, "dp", split_axis=0, concat_axis=0, tiled=True)
-    payload, vectors = own(arrived, cluster_ids, head_weight)
-    rows = lax.all_gather(payload, "cent", axis=0)
-    spread = jnp.broadcast_to(payload, (n_dp,) + payload.shape)
+    payload, spread, rows = own(arrived, cluster_ids, head_weight.shape[0])
+    partner = lax.ppermute(payload, "cent", [(at, at ^ 1) for at in range(n_cent)])
+    near_rows = jnp.stack([payload, partner])
+    far_rows = jnp.concatenate(
+        [
+            lax.ppermute(near_rows, "cent", [((at + 2 * chip) % n_cent, at) for at in range(n_cent)])
+            for chip in range(1, n_cent // 2)
+        ]
+    )
     cols = lax.all_to_all(spread, "dp", split_axis=0, concat_axis=0, tiled=True)
-    turned, near, own_best = nearest_of(rows, jnp.swapaxes(head_weight, 0, 1), centroids, base)
-    partial = peers_of(cols, rows, turned, head_weight, near, own_best, place)
+    vectors = vectors_of(rows, head_weight)
+    near_found = nearest_of(near_rows, head_weight, centroids)
+    far_found = nearest_of(far_rows, head_weight, centroids)
+    partial = peers_of(cols, near_rows, far_rows, near_found, far_found, head_weight)
     parts = lax.all_to_all(partial, "cent", split_axis=0, concat_axis=0, tiled=True)
     final = jnp.max(parts, axis=0)
     return (vectors, final[0], final[1], final[2])

time: 125 us -> 113 us (0.904)
  blocking collectives: 40 us -> 15.2 us
  starting transfers between devices: 3.62 us -> 14.7 us
  local copies, waits for them, and re-layouts: 7.31 us -> 4.65 us
  waiting for transfers between devices: 0.01 us -> 2.63 us
  Pallas kernels: 71.4 us -> 73.3 us
    all_gather x1 -> x0, blocking collectives: 16.4 us -> none  [local(): rows = lax.all_gather(payload, 'cent', axis=0)]
    all_to_all x1 -> x0, blocking collectives: 8.49 us -> none  [local(): lax.all_to_all(partial, 'cent', split_axis=0, concat_axis=0, tiled=True)]
    ppermute x0 -> x4, starting transfers between devices: none -> 6.99 us  [the longest x3 4.88 us: local(): lax.ppermute(near_rows, 'cent', [((at + 2 * chip) % n_cent, at) for at in...]
    all_to_all x0 -> x1, starting transfers between devices: none -> 4.05 us  [local(): lax.all_to_all(partial, 'cent', split_axis=0, concat_axis=0, tiled=True)]
    pallas_call x1, Pallas kernels: 11 us -> 7.91 us  [peers_of(): pl.pallas_call(peer_kernel, out_shape=jax.ShapeDtypeStruct((n_cent, 4, cl...]
    pallas_call x1 -> x2, Pallas kernels: 24.5 us -> 27.5 us  [nearest_of(): pl.pallas_call(functools.partial(nearest_kernel, panel_rows), grid=(pl.cd...]
    all_to_all x0 -> x1, waiting for transfers between devices: none -> 2.62 us  [local(): lax.all_to_all(partial, 'cent', split_axis=0, concat_axis=0, tiled=True)]
    broadcast_in_dim x1 -> x0, local copies, waits for them, and re-layouts: 1.9 us -> none  [local(): spread = jnp.broadcast_to(payload, (n_dp,) + payload.shape)]
  transfers between devices with their start and end apart: 1 -> 6, of which waited for: 0 -> 1; matrix products, arithmetic and copies ran while one was open for 1% -> 1% of each run, Pallas kernels for 20% -> 26%
where the time goes in v4:
time: 113 us; the launch traced here: 112 us
  Pallas kernels  73.3 us (65%)
  blocking collectives  15.2 us (13%)
  starting transfers between devices  14.7 us (13%)
  local copies, waits for them, and re-layouts  4.65 us (4%)
  waiting for transfers between devices  2.63 us (2%)
    pallas_call x1, Pallas kernels, embed(): pl.pallas_call(embed_kernel, out_shape=jax.ShapeDtypeStruct((n_dp, clips...  33.8 us
    pallas_call x2, Pallas kernels, nearest_of(): pl.pallas_call(functools.partial(nearest_kernel, panel_rows), grid=(pl.cd...  27.5 us
    all_to_all x1, blocking collectives, local(): lax.all_to_all(pooled, 'dp', split_axis=0, concat_axis=0, tiled=True)  15.2 us
    pallas_call x1, Pallas kernels, peers_of(): pl.pallas_call(peer_kernel, out_shape=jax.ShapeDtypeStruct((n_cent, 4, cl...  7.91 us
    ppermute x3, starting transfers between devices, local(): lax.ppermute(near_rows, 'cent', [((at + 2 * chip) % n_cent, at) for at in...  4.88 us
    unnamed x9, local copies, waits for them, and re-layouts  4.1 us
    all_to_all x1, starting transfers between devices, local(): lax.all_to_all(partial, 'cent', split_axis=0, concat_axis=0, tiled=True)  4.05 us
    all_to_all x1, starting transfers between devices, local(): cols = lax.all_to_all(spread, 'dp', split_axis=0, concat_axis=0, tiled=True)  3.62 us
  transfers between devices with their start and end apart: 6, of which 1 were waited for; matrix products, arithmetic and copies ran while one was open for 1% of the time, Pallas kernels for 26%

profile of v4, /device:TPU:1, one launch (start us, length us, event | category | flops | bytes accessed | tf_op | source)
XLA Modules:
  0.0 112.0 jit_solution(2544026452306211295)
XLA Ops:
  0.6 0.0 copy-start
  0.6 1.5 %copy.13.taps_ref = bf16[2,27,432]{2,1,0:T(8,128)(2,1)} copy(bf16[2,27,432]{2,0,1:T(2,128)(2,1)} %param.14) | data formatting | bytes 93312 | tf_op args[5]
  2.1 33.8 %embed.1 = bf16[16,8,256]{2,1,0:T(8,128)(2,1)} custom-call(bf16[4,16,192,128]{3,2,1,0:T(8,128)(2,1)} %bitcast.10, s32[1,128]{1,0:T(1,128)} %count_ref.1, s32[1,128]{1,0:T(1,128)} %send_ref.1, bf16[2,192,432]{2,1,0:T(8,128)(2,1)} %wide_ref.1, bf16[2,27,432]{2,1,0:T(8,128)(2,1)} %copy.13.taps_ref, bf16[2,192,432]{2,1,0:T(8,128)(2,1)} %bitcast.11), custom_call_target="tpu_custom_call" | custom-call | tf_op jit(solution)/shard_map/embed/pallas_call | solution.py:228
  36.0 15.2 %all_to_all.15.arrived_ref = bf16[16,8,256]{2,1,0:T(8,128)(2,1)} all-to-all(bf16[16,8,256]{2,1,0:T(8,128)(2,1)} %embed.1), channel_id=1, replica_groups=mesh['dp'=16,'cent'=8] {'dp'}, dimensions={0} | all-to-all | bytes 131072 | tf_op jit(solution)/shard_map/all_to_all | solution.py:508
  51.2 2.0 %own.1 = (bf16[208,128]{1,0:T(8,128)(2,1)}, bf16[16,208,128]{2,1,0:T(8,128)(2,1)}, bf16[128,192]{1,0:T(8,128)(2,1)}) custom-call(bf16[16,8,256]{2,1,0:T(8,128)(2,1)} %all_to_all.15.arrived_ref, s32[1,128]{1,0:T(1,128)} %ids_ref.1), custom_call_target="tpu_custom_call" | custom-call | tf_op jit(solution)/shard_map/own/pallas_call | solution.py:283
  53.2 2.1 %collective-permute-start = (bf16[208,128]{1,0:T(8,128)(2,1)}, bf16[208,128]{1,0:T(8,128)(2,1)S(1)}, u32[]{:S(2)}, u32[]{:S(2)}) collective-permute-start(bf16[208,128]{1,0:T(8,128)(2,1)} %get-tuple-element.15), channel_id=1, source_target_pairs={{0,1},{1,0},{2,3},{3,2},{4,5},{5,4},{6,7},{7,6},{8,9},{9,8},{10,11... | collective-permute-start | bytes 159752 | tf_op jit(solution)/shard_map/ppermute | solution.py:510
  55.3 3.6 %all-to-all-start.1 = ((bf16[16,208,128]{2,1,0:T(8,128)(2,1)}), bf16[16,208,128]{2,1,0:T(8,128)(2,1)S(1)}, u32[]{:S(2)}, u32[]{:S(2)}) async-start(bf16[16,208,128]{2,1,0:T(8,128)(2,1)} %get-tuple-element.14), calls=%async_computation.1 | async-start | bytes 1703936 | tf_op jit(solution)/shard_map/all_to_all | solution.py:518
  59.0 0.0 collective-permute-done
  59.0 0.8 pad_maximum_fusion.rows_ref.near_rows_ref
  59.8 1.3 %collective-permute-start.3 = (bf16[2,208,128]{2,1,0:T(8,128)(2,1)S(1)}, bf16[2,208,128]{2,1,0:T(8,128)(2,1)S(1)}, u32[]{:S(2)}, u32[]{:S(2)}) collective-permute-start(bf16[2,208,128]{2,1,0:T(8,128)(2,1)S(1)} %pad_maximum_fusion.rows_ref.near_rows_ref), channel_id=1, source_target_pairs={{6,0},{7,1},{0,2},{1,3},{2,4},{3,5},{4,6},{5,7},{14,8},{15,9},{8,1... | collective-permute-start | bytes 319496 | tf_op jit(solution)/shard_map/ppermute | solution.py:514
  61.1 2.4 %collective-permute-start.2 = (bf16[2,208,128]{2,1,0:T(8,128)(2,1)S(1)}, bf16[2,208,128]{2,1,0:T(8,128)(2,1)S(1)}, u32[]{:S(2)}, u32[]{:S(2)}) collective-permute-start(bf16[2,208,128]{2,1,0:T(8,128)(2,1)S(1)} %pad_maximum_fusion.rows_ref.near_rows_ref), channel_id=1, source_target_pairs={{4,0},{5,1},{6,2},{7,3},{0,4},{1,5},{2,6},{3,7},{12,8},{13,9},{14,... | collective-permute-start | bytes 319496 | tf_op jit(solution)/shard_map/ppermute | solution.py:514
  63.5 1.2 %collective-permute-start.1 = (bf16[2,208,128]{2,1,0:T(8,128)(2,1)S(1)}, bf16[2,208,128]{2,1,0:T(8,128)(2,1)S(1)}, u32[]{:S(2)}, u32[]{:S(2)}) collective-permute-start(bf16[2,208,128]{2,1,0:T(8,128)(2,1)S(1)} %pad_maximum_fusion.rows_ref.near_rows_ref), channel_id=1, source_target_pairs={{2,0},{3,1},{4,2},{5,3},{6,4},{7,5},{0,6},{1,7},{10,8},{11,9},{12,... | collective-permute-start | bytes 319496 | tf_op jit(solution)/shard_map/ppermute | solution.py:514
  64.7 0.0 copy-done
  64.7 9.8 %nearest.2 = (bf16[1024,256]{1,0:T(8,128)(2,1)S(1)}, f32[1,256]{1,0:T(1,128)S(1)}, f32[1,256]{1,0:T(1,128)S(1)}) custom-call(bf16[2,208,128]{2,1,0:T(8,128)(2,1)S(1)} %pad_maximum_fusion.rows_ref.near_rows_ref, bf16[192,1024]{1,0:T(8,128)(2,1)S(1)} %copy-done, bf16[6250,1024]{1,0:T(8,128)(2,1)} %panel_ref.3), custom_call_target="tpu_custom_call" | custom-call | flops 3276800000 | bytes 12800000 | tf_op jit(solution)/shard_map/nearest/pallas_call | solution.py:390
  74.5 0.0 collective-permute-done.1
  74.5 0.0 collective-permute-done.2
  74.6 0.0 collective-permute-done.3
  74.6 17.7 %nearest.3 = (bf16[1024,768]{1,0:T(8,128)(2,1)S(1)}, f32[1,768]{1,0:T(1,128)S(1)}, f32[1,768]{1,0:T(1,128)S(1)}) custom-call(bf16[6,208,128]{2,1,0:T(8,128)(2,1)S(1)} %constant_dynamic-update-slice_fusion.rows_ref.far_rows_ref, bf16[192,1024]{1,0:T(8,128)(2,1)S(1)} %copy-done, bf16[6250,1024]{1,0:T(8,128)(2,1)} %panel_ref.3), custom_call_target="tpu_custom_call" | custom-call | flops 9830400000 | bytes 12800000 | tf_op jit(solution)/shard_map/nearest/pallas_call | solution.py:390
  92.3 0.0 copy-start.1
  92.3 1.2 %copy-done.1 = bf16[1024,768]{1,0:T(8,128)(2,1)} copy-done((bf16[1024,768]{1,0:T(8,128)(2,1)}, bf16[1024,768]{1,0:T(8,128)(2,1)S(1)}, u32[]{:S(2)}) %copy-start.1) | copy-done | bytes 1572888
  93.4 0.0 all-to-all-done.1.cols_ref
  93.4 0.0 copy-start.2
  93.4 1.4 %copy-done.2 = bf16[1024,768]{1,0:T(8,128)(2,1)S(1)} copy-done((bf16[1024,768]{1,0:T(8,128)(2,1)S(1)}, bf16[1024,768]{1,0:T(8,128)(2,1)}, u32[]{:S(2)}) %copy-start.2) | copy-done | bytes 1572888
  94.8 7.9 %peers.1 = f32[8,4,128]{2,1,0:T(4,128)} custom-call(bf16[16,208,128]{2,1,0:T(8,128)(2,1)S(1)} %all-to-all-done.1.cols_ref, bf16[2,208,128]{2,1,0:T(8,128)(2,1)S(1)} %pad_maximum_fusion.rows_ref.near_rows_ref, bf16[6,208,128]{2,1,0:T(8,128)(2,1)S(1)} %constant_dynamic-update-slice_fusion.rows_ref.far_rows_ref, ...), custom_call_target="tpu_custom_call" | custom-call | flops 4294967296 | bytes 4194304 | tf_op jit(solution)/shard_map/peers/pallas_call | solution.py:475
  102.8 4.0 %all-to-all-start.2 = ((f32[8,4,128]{2,1,0:T(4,128)}), f32[8,4,128]{2,1,0:T(4,128)S(1)}, u32[]{:S(2)}, u32[]{:S(2)}) async-start(f32[8,4,128]{2,1,0:T(4,128)} %peers.1), calls=%async_computation.2 | async-start | bytes 32768 | tf_op jit(solution)/shard_map/all_to_all | solution.py:523
  106.8 2.1 %vectors.1 = bf16[128,1024]{1,0:T(8,128)(2,1)} custom-call(bf16[128,192]{1,0:T(8,128)(2,1)} %get-tuple-element.13.rows_ref, bf16[192,1024]{1,0:T(8,128)(2,1)} %head_ref.7), custom_call_target="tpu_custom_call" | custom-call | flops 50331648 | bytes 655360 | tf_op jit(solution)/shard_map/vectors/pallas_call | solution.py:304
  108.9 2.6 %all-to-all-done.2 = f32[8,4,128]{2,1,0:T(4,128)S(1)} async-done(((f32[8,4,128]{2,1,0:T(4,128)}), f32[8,4,128]{2,1,0:T(4,128)S(1)}, u32[]{:S(2)}, u32[]{:S(2)}) %all-to-all-start.2) | async-done | bytes 16416 | tf_op jit(solution)/shard_map/all_to_all | solution.py:523
  111.5 0.5 slice_bitcast_fusion
  (4 shorter events, 0.1 us)
Async XLA Ops:
  0.6 64.1 %copy-start = (bf16[192,1024]{1,0:T(8,128)(2,1)S(1)}, bf16[192,1024]{1,0:T(8,128)(2,1)}, u32[]{:S(2)}) copy-start(bf16[192,1024]{1,0:T(8,128)(2,1)} %head_ref.7) | copy-start | bytes 1179652
  53.2 5.7 %collective-permute-start = (bf16[208,128]{1,0:T(8,128)(2,1)}, bf16[208,128]{1,0:T(8,128)(2,1)S(1)}, u32[]{:S(2)}, u32[]{:S(2)}) collective-permute-start(bf16[208,128]{1,0:T(8,128)(2,1)} %get-tuple-element.15), channel_id=1, source_target_pairs={{0,1},{1,0},{2,3},{3,2},{4,5},{5,4},{6,7},{7,6},{8,9},{9,8},{10,11... | collective-permute-start | bytes 159752 | tf_op jit(solution)/shard_map/ppermute | solution.py:510
  55.3 38.1 %all-to-all-start.1 = ((bf16[16,208,128]{2,1,0:T(8,128)(2,1)}), bf16[16,208,128]{2,1,0:T(8,128)(2,1)S(1)}, u32[]{:S(2)}, u32[]{:S(2)}) async-start(bf16[16,208,128]{2,1,0:T(8,128)(2,1)} %get-tuple-element.14), calls=%async_computation.1 | async-start | bytes 1703936 | tf_op jit(solution)/shard_map/all_to_all | solution.py:518
  59.8 14.8 %collective-permute-start.3 = (bf16[2,208,128]{2,1,0:T(8,128)(2,1)S(1)}, bf16[2,208,128]{2,1,0:T(8,128)(2,1)S(1)}, u32[]{:S(2)}, u32[]{:S(2)}) collective-permute-start(bf16[2,208,128]{2,1,0:T(8,128)(2,1)S(1)} %pad_maximum_fusion.rows_ref.near_rows_ref), channel_id=1, source_target_pairs={{6,0},{7,1},{0,2},{1,3},{2,4},{3,5},{4,6},{5,7},{14,8},{15,9},{8,1... | collective-permute-start | bytes 319496 | tf_op jit(solution)/shard_map/ppermute | solution.py:514
  61.1 13.4 %collective-permute-start.2 = (bf16[2,208,128]{2,1,0:T(8,128)(2,1)S(1)}, bf16[2,208,128]{2,1,0:T(8,128)(2,1)S(1)}, u32[]{:S(2)}, u32[]{:S(2)}) collective-permute-start(bf16[2,208,128]{2,1,0:T(8,128)(2,1)S(1)} %pad_maximum_fusion.rows_ref.near_rows_ref), channel_id=1, source_target_pairs={{4,0},{5,1},{6,2},{7,3},{0,4},{1,5},{2,6},{3,7},{12,8},{13,9},{14,... | collective-permute-start | bytes 319496 | tf_op jit(solution)/shard_map/ppermute | solution.py:514
  63.5 11.0 %collective-permute-start.1 = (bf16[2,208,128]{2,1,0:T(8,128)(2,1)S(1)}, bf16[2,208,128]{2,1,0:T(8,128)(2,1)S(1)}, u32[]{:S(2)}, u32[]{:S(2)}) collective-permute-start(bf16[2,208,128]{2,1,0:T(8,128)(2,1)S(1)} %pad_maximum_fusion.rows_ref.near_rows_ref), channel_id=1, source_target_pairs={{2,0},{3,1},{4,2},{5,3},{6,4},{7,5},{0,6},{1,7},{10,8},{11,9},{12,... | collective-permute-start | bytes 319496 | tf_op jit(solution)/shard_map/ppermute | solution.py:514
  92.3 1.2 %copy-start.1 = (bf16[1024,768]{1,0:T(8,128)(2,1)}, bf16[1024,768]{1,0:T(8,128)(2,1)S(1)}, u32[]{:S(2)}) copy-start(bf16[1024,768]{1,0:T(8,128)(2,1)S(1)} %get-tuple-element.17.far_turned_ref) | copy-start | bytes 4718596
  93.4 1.4 %copy-start.2 = (bf16[1024,768]{1,0:T(8,128)(2,1)S(1)}, bf16[1024,768]{1,0:T(8,128)(2,1)}, u32[]{:S(2)}) copy-start(bf16[1024,768]{1,0:T(8,128)(2,1)} %copy-done.1) | copy-start | bytes 4718596
  102.8 8.7 %all-to-all-start.2 = ((f32[8,4,128]{2,1,0:T(4,128)}), f32[8,4,128]{2,1,0:T(4,128)S(1)}, u32[]{:S(2)}, u32[]{:S(2)}) async-start(f32[8,4,128]{2,1,0:T(4,128)} %peers.1), calls=%async_computation.2 | async-start | bytes 32768 | tf_op jit(solution)/shard_map/all_to_all | solution.py:523

commit v5 on v4

--- a/solution.py
+++ b/solution.py
@@ -31,13 +31,20 @@
 
 
 def embed_kernel(
-    clip_ref, count_ref, send_ref, wide_ref, taps_ref, reduce_ref, out_ref, *scratch
+    stored_ref, count_ref, send_ref, wide_ref, taps_ref, reduce_ref, out_ref, *scratch
 ):
     x_refs, hidden_refs, act_refs = scratch[0:6], scratch[6:12], scratch[12:15]
     pool_ref, packed_pool_ref = scratch[15:17]
     weight_refs = scratch[17:19]
     expand_ref, depth_ref = scratch[19:21]
+    clip_ref, arrival = scratch[21:23]
     channels, clips = clip_ref.shape[2], clip_ref.shape[3]
+    copies = [
+        pltpu.make_async_copy(stored_ref.at[frame], clip_ref.at[frame], arrival.at[frame])
+        for frame in range(clip_ref.shape[0])
+    ]
+    for copy in copies:
+        copy.start()
     expanded = wide_ref.shape[2]
     eye = identity(expanded)
     for layer in range(2):
@@ -182,6 +189,8 @@
 
     pool_ref[...] = jnp.zeros_like(pool_ref)
     packed_pool_ref[...] = jnp.zeros_like(packed_pool_ref)
+    copies[0].wait()
+    copies[1].wait()
 
     @pl.loop(0, STEPS)
     def _(step):
@@ -192,6 +201,8 @@
             gather(tile, pair)
         spread_taps(0, step, 9, 27)
 
+    copies[2].wait()
+    copies[3].wait()
     stage(0, 0, filler(lambda pair: gather(2, pair), lambda pair: expand_stored(0, 2, pair)))
     stage(0, 1, filler(lambda pair: reduce_store(0, pair), lambda pair: expand_stored(1, 0, pair)))
     stage(0, 2, filler(lambda pair: reduce_store(1, pair), lambda pair: expand_stored(1, 1, pair)))
@@ -228,15 +239,16 @@
     return pl.pallas_call(
         embed_kernel,
         out_shape=jax.ShapeDtypeStruct((n_dp, clips // n_dp, 256), BF),
-        in_specs=[pl.BlockSpec(memory_space=pltpu.VMEM)] * 6,
+        in_specs=[pl.BlockSpec(memory_space=pltpu.HBM)] + [pl.BlockSpec(memory_space=pltpu.VMEM)] * 5,
         out_specs=pl.BlockSpec(memory_space=pltpu.VMEM),
         scratch_shapes=[pltpu.VMEM((spots, channels, clips), BF)] * 6
         + [pltpu.VMEM((spots, expanded, clips), F32)] * 6
         + [pltpu.VMEM((spots, expanded, clips), BF)] * 3
         + [pltpu.VMEM((channels, clips), F32)] * 2
         + [pltpu.VMEM((expanded // 16, 27, 16, clips), F32)] * 2
-        + [pltpu.VMEM((2, expanded, channels), BF), pltpu.VMEM((2, expanded, clips), F32)],
-        compiler_params=pltpu.CompilerParams(vmem_limit_bytes=60 << 20),
+        + [pltpu.VMEM((2, expanded, channels), BF), pltpu.VMEM((2, expanded, clips), F32)]
+        + [pltpu.VMEM((frames, spots, channels, clips), BF), pltpu.SemaphoreType.DMA((frames,))],
+        compiler_params=pltpu.CompilerParams(vmem_limit_bytes=52 << 20),
         name="embed",
     )(
         jnp.transpose(clip_data, (1, 2, 3, 0)),
@@ -324,99 +336,120 @@
     return label[0:1] * 256.0 + label[1:2]
 
 
-def nearest_kernel(panel_rows, rows_ref, head_ref, panel_ref, turned_ref, near_ref, own_ref, best_ref, flip_ref):
+def fetch(stored_ref, panel_ref, arrival):
+    even = panel_ref.shape[0]
+    copies = []
+    for part in range(arrival.shape[0]):
+        at = slice(part * PANEL_ROWS, min(even, (part + 1) * PANEL_ROWS))
+        copy = pltpu.make_async_copy(stored_ref.at[at], panel_ref.at[at], arrival.at[part])
+        copy.start()
+        copies.append((at, copy))
+    return copies
+
+
+def score_rows(
+    rows_ref, head_ref, tail_ref, panel_rows, panel_ref, copies, turned_ref, near_ref, own_ref, best_ref, flip_ref
+):
     blocks, height, clips = rows_ref.shape
     channels, dims = head_ref.shape
-    total = blocks * clips
-    step = pl.program_id(0)
-    last = pl.num_programs(0) - 1
     base = lax.axis_index("cent") * panel_rows
-
-    @pl.when(step == 0)
-    def _():
-        eye = identity(256)
-        for part in range(dims // 256):
-            part = slice(part * 256, (part + 1) * 256)
-            flip_ref[part, :] = turn(eye, head_ref[:, part]).astype(BF)
+    eye = identity(256)
+    for part in range(dims // 256):
+        part = slice(part * 256, (part + 1) * 256)
+        flip_ref[part, :] = turn(eye, head_ref[:, part]).astype(BF)
+
+    @pl.loop(0, blocks // 2)
+    def _(pair):
+        both = jnp.concatenate([rows_ref[2 * pair], rows_ref[2 * pair + 1]], axis=1)
+        projected = jnp.dot(flip_ref[...], both[:channels], preferred_element_type=F32)
+        turned_ref[pair] = unit(projected, 0)
+        scores = jnp.dot(tail_ref[...], turned_ref[pair], preferred_element_type=F32)
+        index = lax.broadcasted_iota(jnp.int32, scores.shape, 0)
+        best_ref[pair] = jnp.where(index < panel_rows - panel_ref.shape[0], scores, -jnp.inf)
+
+    copies[0][1].wait()
+
+    @pl.loop(0, blocks // 2)
+    def _(pair):
+        scores = jnp.dot(panel_ref[:OCCUR, :], turned_ref[pair], preferred_element_type=F32)
+        local_id = label_of(rows_ref, pair, channels).astype(jnp.int32) - base
+        index = lax.broadcasted_iota(jnp.int32, (OCCUR, 2 * clips), 0)
+        own_ref[pair] = jnp.max(jnp.where(index == local_id, scores, -jnp.inf), axis=0, keepdims=True)
+
+    for part, (at, copy) in enumerate(copies):
+        if part > 0:
+            copy.wait()
 
         @pl.loop(0, blocks // 2)
         def _(pair):
-            both = jnp.concatenate([rows_ref[2 * pair], rows_ref[2 * pair + 1]], axis=1)
-            projected = jnp.dot(flip_ref[...], both[:channels], preferred_element_type=F32)
-            cols = pl.ds(pl.multiple_of(pair * 2 * clips, 2 * clips), 2 * clips)
-            turned_ref[:, cols] = unit(projected, 0)
-
-        best_ref[...] = jnp.full_like(best_ref, -jnp.inf)
-
-    def score(cols):
-        return jnp.dot(panel_ref[...], turned_ref[:, cols], preferred_element_type=F32)
-
-    def keep(scores, cols):
-        rows = scores.shape[0]
-        best_ref[:, cols] = jnp.maximum(
-            best_ref[:, cols], jnp.max(scores.reshape(rows // 8, 8, scores.shape[1]), axis=0)
-        )
-
-    for block in range(total // 256):
-        cols = pl.ds(block * 256, 256)
-
-        @pl.when(step < last)
-        def _():
-            scores = score(cols)
-            keep(scores, cols)
-
-            @pl.when(step == 0)
-            def _():
-                local_id = label_of(rows_ref, block, channels).astype(jnp.int32) - base
-                index = lax.broadcasted_iota(jnp.int32, (OCCUR, 256), 0)
-                own_ref[:, cols] = jnp.max(
-                    jnp.where(index == local_id, scores[:OCCUR], -jnp.inf), axis=0, keepdims=True
-                )
-
-        @pl.when(step == last)
-        def _():
-            scores = score(cols)
-            index = lax.broadcasted_iota(jnp.int32, scores.shape, 0) + last * panel_ref.shape[0]
-            keep(jnp.where(index < panel_rows, scores, -jnp.inf), cols)
-            near_ref[:, cols] = jnp.max(best_ref[:, cols], axis=0, keepdims=True)
-
-
-def nearest_of(rows, head_weight, centroids):
+            scores = jnp.dot(panel_ref[at, :], turned_ref[pair], preferred_element_type=F32)
+            best_ref[pair] = jnp.maximum(
+                best_ref[pair], jnp.max(scores.reshape((at.stop - at.start) // 8, 8, 2 * clips), axis=0)
+            )
+
+    for pair in range(blocks // 2):
+        near_ref[pair] = jnp.max(best_ref[pair], axis=0, keepdims=True)
+
+
+def near_kernel(
+    rows_ref, head_ref, tail_ref, stored_ref, turned_ref, near_ref, own_ref, best_ref, flip_ref, panel_ref, arrival
+):
+    copies = fetch(stored_ref, panel_ref, arrival)
+    score_rows(
+        rows_ref, head_ref, tail_ref, stored_ref.shape[0], panel_ref, copies,
+        turned_ref, near_ref, own_ref, best_ref, flip_ref,
+    )
+
+
+def panel_specs(panel_rows, dims):
+    even = panel_rows // 8 * 8
+    return (
+        [pl.BlockSpec((8, dims), lambda step: (even // 8, 0)), pl.BlockSpec(memory_space=pltpu.HBM)],
+        [pltpu.VMEM((even, dims), BF), pltpu.SemaphoreType.DMA((pl.cdiv(even, PANEL_ROWS),))],
+    )
+
+
+def scores_shape(pairs, dims, width):
+    return [
+        jax.ShapeDtypeStruct((pairs, dims, width), BF),
+        jax.ShapeDtypeStruct((pairs, 1, width), F32),
+        jax.ShapeDtypeStruct((pairs, 1, width), F32),
+    ]
+
+
+def near_of(rows, head_weight, centroids):
     blocks, height, clips = rows.shape
     channels, dims = head_weight.shape
-    total = blocks * clips
+    pairs = blocks // 2
     panel_rows = centroids.shape[0]
-    whole = lambda shape: pl.BlockSpec(shape, lambda step: (0,) * len(shape))
+    specs, scratch = panel_specs(panel_rows, dims)
     return pl.pallas_call(
-        functools.partial(nearest_kernel, panel_rows),
-        grid=(pl.cdiv(panel_rows, PANEL_ROWS),),
-        out_shape=(
-            jax.ShapeDtypeStruct((dims, total), BF),
-            jax.ShapeDtypeStruct((1, total), F32),
-            jax.ShapeDtypeStruct((1, total), F32),
+        near_kernel,
+        grid=(1,),
+        out_shape=scores_shape(pairs, dims, 2 * clips),
+        in_specs=[pl.BlockSpec(memory_space=pltpu.VMEM)] * 2 + specs,
+        out_specs=[pl.BlockSpec(memory_space=pltpu.VMEM)] * 3,
+        scratch_shapes=[pltpu.VMEM((pairs, 8, 2 * clips), F32), pltpu.VMEM((dims, channels), BF)] + scratch,
+        compiler_params=pltpu.CompilerParams(vmem_limit_bytes=52 << 20),
+        cost_estimate=pl.CostEstimate(
+            flops=2 * blocks * clips * panel_rows * dims, bytes_accessed=2 * panel_rows * dims, transcendentals=0
         ),
-        in_specs=[
-            whole(rows.shape),
-            whole(head_weight.shape),
-            pl.BlockSpec((PANEL_ROWS, dims), lambda step: (step, 0)),
-        ],
-        out_specs=(whole((dims, total)), whole((1, total)), whole((1, total))),
-        scratch_shapes=[pltpu.VMEM((8, total), F32), pltpu.VMEM((dims, channels), BF)],
-        compiler_params=pltpu.CompilerParams(vmem_limit_bytes=48 << 20),
-        cost_estimate=pl.CostEstimate(
-            flops=2 * total * panel_rows * dims, bytes_accessed=2 * panel_rows * dims, transcendentals=0
-        ),
-        name="nearest",
-    )(rows, head_weight, centroids)
+        name="near",
+    )(rows, head_weight, centroids, centroids)
 
 
 GROUP = 4
 
 
-def peer_kernel(
-    cols_ref, near_rows_ref, far_rows_ref, near_turned_ref, far_turned_ref, head_ref,
-    near_best_ref, far_best_ref, near_own_ref, far_own_ref, out_ref, best_ref,
+def far_kernel(
+    near_rows_ref, near_turned_ref, near_best_ref, near_own_ref, far_rows_ref, cols_ref, head_ref, tail_ref, stored_ref,
+    out_ref, far_turned_ref, far_best_ref, far_own_ref, running_ref, flip_ref, panel_ref, arrival, best_ref,
 ):
+    copies = fetch(stored_ref, panel_ref, arrival)
+    score_rows(
+        far_rows_ref, head_ref, tail_ref, stored_ref.shape[0], panel_ref, copies,
+        far_turned_ref, far_best_ref, far_own_ref, running_ref, flip_ref,
+    )
     n_dp, height, clips = cols_ref.shape
     n_cent = out_ref.shape[0]
     channels = head_ref.shape[0]
@@ -434,10 +467,9 @@
         for block in range(n_cent // 2):
             cols = slice(block * 2 * clips, (block + 1) * 2 * clips)
             if block == 0:
-                turned, row_ids = near_turned_ref[...], label_of(near_rows_ref, 0, channels)
+                turned, row_ids = near_turned_ref[0], label_of(near_rows_ref, 0, channels)
             else:
-                far = slice((block - 1) * 2 * clips, block * 2 * clips)
-                turned, row_ids = far_turned_ref[:, far], label_of(far_rows_ref, block - 1, channels)
+                turned, row_ids = far_turned_ref[block - 1], label_of(far_rows_ref, block - 1, channels)
             scores = jnp.dot(vectors, turned, preferred_element_type=F32)
             same = wide == row_ids
             if block == 0:
@@ -456,37 +488,43 @@
             chip = (mine_cent // 2 + block) % (n_cent // 2)
             cent = 2 * chip + (mine_cent + side) % 2
             at = slice((2 * block + side) * clips, (2 * block + side + 1) * clips)
+            part = slice(side * clips, (side + 1) * clips)
             if block == 0:
-                part = slice(side * clips, (side + 1) * clips)
-                nearest, own_best = near_best_ref[:, part], near_own_ref[:, part]
+                nearest, own_best = near_best_ref[0, :, part], near_own_ref[0, :, part]
             else:
-                part = slice((2 * block + side - 2) * clips, (2 * block + side - 1) * clips)
-                nearest, own_best = far_best_ref[:, part], far_own_ref[:, part]
+                nearest, own_best = far_best_ref[block - 1, :, part], far_own_ref[block - 1, :, part]
             out_ref[cent, 0:1, :] = nearest
             out_ref[cent, 1:2, :] = own_best
             out_ref[cent, 2:3, :] = best[:, at]
             out_ref[cent, 3:4, :] = best[:, at]
 
 
-def peers_of(cols, near_rows, far_rows, near_found, far_found, head_weight):
+def far_of(near_rows, near_found, far_rows, cols, head_weight, centroids):
     n_dp, height, clips = cols.shape
     n_cent = near_rows.shape[0] + far_rows.shape[0]
-    dims = head_weight.shape[1]
+    channels, dims = head_weight.shape
+    pairs = far_rows.shape[0] // 2
+    panel_rows = centroids.shape[0]
+    specs, scratch = panel_specs(panel_rows, dims)
+    found = [pltpu.VMEM(part.shape, part.dtype) for part in scores_shape(pairs, dims, 2 * clips)]
     return pl.pallas_call(
-        peer_kernel,
+        far_kernel,
+        grid=(1,),
         out_shape=jax.ShapeDtypeStruct((n_cent, 4, clips), F32),
-        in_specs=[pl.BlockSpec(memory_space=pltpu.VMEM)] * 10,
+        in_specs=[pl.BlockSpec(memory_space=pltpu.VMEM)] * 7 + specs,
         out_specs=pl.BlockSpec(memory_space=pltpu.VMEM),
-        scratch_shapes=[pltpu.VMEM((8, n_cent * clips), F32)],
-        compiler_params=pltpu.CompilerParams(vmem_limit_bytes=48 << 20),
+        scratch_shapes=found
+        + [pltpu.VMEM((pairs, 8, 2 * clips), F32), pltpu.VMEM((dims, channels), BF)]
+        + scratch
+        + [pltpu.VMEM((8, n_cent * clips), F32)],
+        compiler_params=pltpu.CompilerParams(vmem_limit_bytes=44 << 20),
         cost_estimate=pl.CostEstimate(
-            flops=2 * n_dp * n_cent * clips * clips * dims, bytes_accessed=4 << 20, transcendentals=0
+            flops=2 * clips * dims * (2 * pairs * panel_rows + n_dp * n_cent * clips),
+            bytes_accessed=2 * panel_rows * dims,
+            transcendentals=0,
         ),
-        name="peers",
-    )(
-        cols, near_rows, far_rows, near_found[0], far_found[0], head_weight,
-        near_found[1], far_found[1], near_found[2], far_found[2],
-    )
+        name="far",
+    )(near_rows, *near_found, far_rows, cols, head_weight, centroids, centroids)
 
 
 def local(
@@ -517,9 +555,8 @@
     )
     cols = lax.all_to_all(spread, "dp", split_axis=0, concat_axis=0, tiled=True)
     vectors = vectors_of(rows, head_weight)
-    near_found = nearest_of(near_rows, head_weight, centroids)
-    far_found = nearest_of(far_rows, head_weight, centroids)
-    partial = peers_of(cols, near_rows, far_rows, near_found, far_found, head_weight)
+    near_found = near_of(near_rows, head_weight, centroids)
+    partial = far_of(near_rows, near_found, far_rows, cols, head_weight, centroids)
     parts = lax.all_to_all(partial, "cent", split_axis=0, concat_axis=0, tiled=True)
     final = jnp.max(parts, axis=0)
     return (vectors, final[0], final[1], final[2])

time: 113 us -> 114 us (level)
  Pallas kernels: 73.3 us -> 71.8 us
    pallas_call x1, Pallas kernels: 33.8 us -> 31.6 us  [embed(): pl.pallas_call(embed_kernel, out_shape=jax.ShapeDtypeStruct((n_dp, clips...]
    unnamed x9 -> x13, local copies, waits for them, and re-layouts: 4.1 us -> 5.12 us
    pallas_call x3 -> x2, Pallas kernels: 35.4 us -> 36.1 us  [the longest x1 26 us: far_of(): pl.pallas_call(far_kernel, grid=(1,), out_shape=jax.ShapeDtypeStruct((n_c...]
  transfers between devices with their start and end apart: 6 -> 6, of which waited for: 1 -> 2; matrix products, arithmetic and copies ran while one was open for 1% -> 1% of each run, Pallas kernels for 26% -> 11%
where the time goes in v5:
time: 114 us; the launch traced here: 113 us
  Pallas kernels  71.8 us (63%)
  starting transfers between devices  15.1 us (13%)
  blocking collectives  15 us (13%)
  local copies, waits for them, and re-layouts  5.64 us (5%)
  waiting for transfers between devices  3.73 us (3%)
    pallas_call x1, Pallas kernels, embed(): pl.pallas_call(embed_kernel, out_shape=jax.ShapeDtypeStruct((n_dp, clips...  31.6 us
    pallas_call x1, Pallas kernels, far_of(): pl.pallas_call(far_kernel, grid=(1,), out_shape=jax.ShapeDtypeStruct((n_c...  26 us
    all_to_all x1, blocking collectives, local(): lax.all_to_all(pooled, 'dp', split_axis=0, concat_axis=0, tiled=True)  15 us
    pallas_call x1, Pallas kernels, near_of(): pl.pallas_call(near_kernel, grid=(1,), out_shape=scores_shape(pairs, dims...  10.1 us
    unnamed x13, local copies, waits for them, and re-layouts  5.12 us
    ppermute x3, starting transfers between devices, local(): lax.ppermute(near_rows, 'cent', [((at + 2 * chip) % n_cent, at) for at in...  4.89 us
    all_to_all x1, starting transfers between devices, local(): lax.all_to_all(partial, 'cent', split_axis=0, concat_axis=0, tiled=True)  4.43 us
    all_to_all x1, starting transfers between devices, local(): cols = lax.all_to_all(spread, 'dp', split_axis=0, concat_axis=0, tiled=True)  3.62 us
  transfers between devices with their start and end apart: 6, of which 2 were waited for; matrix products, arithmetic and copies ran while one was open for 1% of the time, Pallas kernels for 11%

profile of v5, /device:TPU:1, one launch (start us, length us, event | category | flops | bytes accessed | tf_op | source)
XLA Modules:
  0.0 112.9 jit_solution(17105194083879245222)
XLA Ops:
  0.6 0.8 copy.13.taps_ref
  1.5 0.0 copy-start.2
  1.5 1.0 copy-done.2
  2.5 0.0 copy-start.3
  2.5 1.0 copy-done.3
  3.5 0.7 copy-done.4
  4.1 0.0 copy-start.5
  4.1 0.7 copy-done.5
  4.8 31.6 %embed.1 = bf16[16,8,256]{2,1,0:T(8,128)(2,1)S(1)} custom-call(bf16[4,16,192,128]{3,2,1,0:T(8,128)(2,1)} %bitcast.11, s32[1,128]{1,0:T(1,128)S(1)} %copy-done.4, s32[1,128]{1,0:T(1,128)S(1)} %copy-done.5, bf16[2,192,432]{2,1,0:T(8,128)(2,1)S(1)} %copy-done.2, bf16[2,27,432]{2,1,0:T(8,128)(2,1)S(1)} %copy.13.taps_ref, bf16[2,192,432]{2,1,0:T(8,128)(2,1)S(1)} %bitcast.10), custom_call_target="tpu_custom_call" | custom-call | tf_op jit(solution)/shard_map/embed/pallas_call | solution.py:239
  36.4 15.0 %all_to_all.15.arrived_ref = bf16[16,8,256]{2,1,0:T(8,128)(2,1)} all-to-all(bf16[16,8,256]{2,1,0:T(8,128)(2,1)S(1)} %embed.1), channel_id=1, replica_groups=mesh['dp'=16,'cent'=8] {'dp'}, dimensions={0} | all-to-all | bytes 131072 | tf_op jit(solution)/shard_map/all_to_all | solution.py:546
  51.4 2.0 %own.1 = (bf16[208,128]{1,0:T(8,128)(2,1)}, bf16[16,208,128]{2,1,0:T(8,128)(2,1)}, bf16[128,192]{1,0:T(8,128)(2,1)}) custom-call(bf16[16,8,256]{2,1,0:T(8,128)(2,1)} %all_to_all.15.arrived_ref, s32[1,128]{1,0:T(1,128)} %ids_ref.1), custom_call_target="tpu_custom_call" | custom-call | tf_op jit(solution)/shard_map/own/pallas_call | solution.py:295
  53.4 3.6 %all-to-all-start.1 = ((bf16[16,208,128]{2,1,0:T(8,128)(2,1)}), bf16[16,208,128]{2,1,0:T(8,128)(2,1)S(1)}, u32[]{:S(2)}, u32[]{:S(2)}) async-start(bf16[16,208,128]{2,1,0:T(8,128)(2,1)} %get-tuple-element.15), calls=%async_computation.1 | async-start | bytes 1703936 | tf_op jit(solution)/shard_map/all_to_all | solution.py:556
  57.0 2.2 %collective-permute-start = (bf16[208,128]{1,0:T(8,128)(2,1)}, bf16[208,128]{1,0:T(8,128)(2,1)S(1)}, u32[]{:S(2)}, u32[]{:S(2)}) collective-permute-start(bf16[208,128]{1,0:T(8,128)(2,1)} %get-tuple-element.11), channel_id=1, source_target_pairs={{0,1},{1,0},{2,3},{3,2},{4,5},{5,4},{6,7},{7,6},{8,9},{9,8},{10,11... | collective-permute-start | bytes 159752 | tf_op jit(solution)/shard_map/ppermute | solution.py:548
  59.2 1.1 collective-permute-done
  60.3 0.8 pad_maximum_fusion.1.rows_ref.near_rows_ref
  61.1 1.3 %collective-permute-start.3 = (bf16[2,208,128]{2,1,0:T(8,128)(2,1)S(1)}, bf16[2,208,128]{2,1,0:T(8,128)(2,1)S(1)}, u32[]{:S(2)}, u32[]{:S(2)}) collective-permute-start(bf16[2,208,128]{2,1,0:T(8,128)(2,1)S(1)} %pad_maximum_fusion.1.rows_ref.near_rows_ref), channel_id=1, source_target_pairs={{6,0},{7,1},{0,2},{1,3},{2,4},{3,5},{4,6},{5,7},{14,8},{15,9},{8,1... | collective-permute-start | bytes 319496 | tf_op jit(solution)/shard_map/ppermute | solution.py:552
  62.4 2.5 %collective-permute-start.2 = (bf16[2,208,128]{2,1,0:T(8,128)(2,1)S(1)}, bf16[2,208,128]{2,1,0:T(8,128)(2,1)S(1)}, u32[]{:S(2)}, u32[]{:S(2)}) collective-permute-start(bf16[2,208,128]{2,1,0:T(8,128)(2,1)S(1)} %pad_maximum_fusion.1.rows_ref.near_rows_ref), channel_id=1, source_target_pairs={{4,0},{5,1},{6,2},{7,3},{0,4},{1,5},{2,6},{3,7},{12,8},{13,9},{14,... | collective-permute-start | bytes 319496 | tf_op jit(solution)/shard_map/ppermute | solution.py:552
  64.9 1.2 %collective-permute-start.1 = (bf16[2,208,128]{2,1,0:T(8,128)(2,1)S(1)}, bf16[2,208,128]{2,1,0:T(8,128)(2,1)S(1)}, u32[]{:S(2)}, u32[]{:S(2)}) collective-permute-start(bf16[2,208,128]{2,1,0:T(8,128)(2,1)S(1)} %pad_maximum_fusion.1.rows_ref.near_rows_ref), channel_id=1, source_target_pairs={{2,0},{3,1},{4,2},{5,3},{6,4},{7,5},{0,6},{1,7},{10,8},{11,9},{12,... | collective-permute-start | bytes 319496 | tf_op jit(solution)/shard_map/ppermute | solution.py:552
  66.0 0.0 copy-start
  66.0 1.0 copy-done
  67.0 0.0 copy-start.1
  67.0 10.1 %near.1 = (bf16[1,1024,256]{2,1,0:T(8,128)(2,1)S(1)}, f32[1,1,256]{2,1,0:T(1,128)S(1)}, f32[1,1,256]{2,1,0:T(1,128)S(1)}) custom-call(bf16[2,208,128]{2,1,0:T(8,128)(2,1)S(1)} %pad_maximum_fusion.1.rows_ref.near_rows_ref, bf16[192,1024]{1,0:T(8,128)(2,1)S(1)} %copy-done, bf16[6250,1024]{1,0:T(8,128)(2,1)} %stored_ref.3, bf16[6250,1024]{1,0:T(8,128)(2,1)} %stored_ref.3), custom_call_target="tpu_custom_call" | custom-call | flops 3276800000 | bytes 12800000 | tf_op jit(solution)/shard_map/near/pallas_call | solution.py:426
  77.2 0.0 collective-permute-done.3
  77.2 0.0 collective-permute-done.2
  77.2 0.0 collective-permute-done.1
  77.2 0.0 all-to-all-done.1.cols_ref
  77.3 0.0 copy-done.1
  77.3 26.0 %far.1 = f32[8,4,128]{2,1,0:T(4,128)} custom-call(bf16[2,208,128]{2,1,0:T(8,128)(2,1)S(1)} %pad_maximum_fusion.1.rows_ref.near_rows_ref, bf16[1,1024,256]{2,1,0:T(8,128)(2,1)S(1)} %get-tuple-element.12.near_turned_ref, f32[1,1,256]{2,1,0:T(1,128)S(1)} %get-tuple-element.13.near_best_ref, f32[1,1,256]{2,1,0:T(1,128)S(1)} %get-tuple-element.14.near_own_ref, ...), custom_call_target="tpu_custom_call" | custom-call | flops 14125367296 | bytes 12800000 | tf_op jit(solution)/shard_map/far/pallas_call | solution.py:510
  103.3 4.4 %all-to-all-start.2 = ((f32[8,4,128]{2,1,0:T(4,128)}), f32[8,4,128]{2,1,0:T(4,128)S(1)}, u32[]{:S(2)}, u32[]{:S(2)}) async-start(f32[8,4,128]{2,1,0:T(4,128)} %far.1), calls=%async_computation.2 | async-start | bytes 32768 | tf_op jit(solution)/shard_map/all_to_all | solution.py:560
  107.7 2.1 %vectors.1 = bf16[128,1024]{1,0:T(8,128)(2,1)} custom-call(bf16[128,192]{1,0:T(8,128)(2,1)} %get-tuple-element.10.rows_ref, bf16[192,1024]{1,0:T(8,128)(2,1)} %head_ref.5), custom_call_target="tpu_custom_call" | custom-call | flops 50331648 | bytes 655360 | tf_op jit(solution)/shard_map/vectors/pallas_call | solution.py:316
  109.8 2.6 %all-to-all-done.2 = f32[8,4,128]{2,1,0:T(4,128)S(1)} async-done(((f32[8,4,128]{2,1,0:T(4,128)}), f32[8,4,128]{2,1,0:T(4,128)S(1)}, u32[]{:S(2)}, u32[]{:S(2)}) %all-to-all-start.2) | async-done | bytes 16416 | tf_op jit(solution)/shard_map/all_to_all | solution.py:560
  112.4 0.5 slice_bitcast_fusion
  (3 shorter events, 0.1 us)
Async XLA Ops:
  1.5 1.0 copy-start.2
  2.5 1.0 copy-start.3
  3.5 0.7 copy-start.4
  4.1 0.7 copy-start.5
  53.4 23.8 %all-to-all-start.1 = ((bf16[16,208,128]{2,1,0:T(8,128)(2,1)}), bf16[16,208,128]{2,1,0:T(8,128)(2,1)S(1)}, u32[]{:S(2)}, u32[]{:S(2)}) async-start(bf16[16,208,128]{2,1,0:T(8,128)(2,1)} %get-tuple-element.15), calls=%async_computation.1 | async-start | bytes 1703936 | tf_op jit(solution)/shard_map/all_to_all | solution.py:556
  57.0 3.3 %collective-permute-start = (bf16[208,128]{1,0:T(8,128)(2,1)}, bf16[208,128]{1,0:T(8,128)(2,1)S(1)}, u32[]{:S(2)}, u32[]{:S(2)}) collective-permute-start(bf16[208,128]{1,0:T(8,128)(2,1)} %get-tuple-element.11), channel_id=1, source_target_pairs={{0,1},{1,0},{2,3},{3,2},{4,5},{5,4},{6,7},{7,6},{8,9},{9,8},{10,11... | collective-permute-start | bytes 159752 | tf_op jit(solution)/shard_map/ppermute | solution.py:548
  61.1 16.0 %collective-permute-start.3 = (bf16[2,208,128]{2,1,0:T(8,128)(2,1)S(1)}, bf16[2,208,128]{2,1,0:T(8,128)(2,1)S(1)}, u32[]{:S(2)}, u32[]{:S(2)}) collective-permute-start(bf16[2,208,128]{2,1,0:T(8,128)(2,1)S(1)} %pad_maximum_fusion.1.rows_ref.near_rows_ref), channel_id=1, source_target_pairs={{6,0},{7,1},{0,2},{1,3},{2,4},{3,5},{4,6},{5,7},{14,8},{15,9},{8,1... | collective-permute-start | bytes 319496 | tf_op jit(solution)/shard_map/ppermute | solution.py:552
  62.4 14.8 %collective-permute-start.2 = (bf16[2,208,128]{2,1,0:T(8,128)(2,1)S(1)}, bf16[2,208,128]{2,1,0:T(8,128)(2,1)S(1)}, u32[]{:S(2)}, u32[]{:S(2)}) collective-permute-start(bf16[2,208,128]{2,1,0:T(8,128)(2,1)S(1)} %pad_maximum_fusion.1.rows_ref.near_rows_ref), channel_id=1, source_target_pairs={{4,0},{5,1},{6,2},{7,3},{0,4},{1,5},{2,6},{3,7},{12,8},{13,9},{14,... | collective-permute-start | bytes 319496 | tf_op jit(solution)/shard_map/ppermute | solution.py:552
  64.9 12.3 %collective-permute-start.1 = (bf16[2,208,128]{2,1,0:T(8,128)(2,1)S(1)}, bf16[2,208,128]{2,1,0:T(8,128)(2,1)S(1)}, u32[]{:S(2)}, u32[]{:S(2)}) collective-permute-start(bf16[2,208,128]{2,1,0:T(8,128)(2,1)S(1)} %pad_maximum_fusion.1.rows_ref.near_rows_ref), channel_id=1, source_target_pairs={{2,0},{3,1},{4,2},{5,3},{6,4},{7,5},{0,6},{1,7},{10,8},{11,9},{12,... | collective-permute-start | bytes 319496 | tf_op jit(solution)/shard_map/ppermute | solution.py:552
  66.0 1.0 copy-start
  67.0 10.2 %copy-start.1 = (bf16[192,1024]{1,0:T(8,128)(2,1)S(1)}, bf16[192,1024]{1,0:T(8,128)(2,1)}, u32[]{:S(2)}) copy-start(bf16[192,1024]{1,0:T(8,128)(2,1)} %head_ref.5) | copy-start | bytes 1179652
  103.3 9.1 %all-to-all-start.2 = ((f32[8,4,128]{2,1,0:T(4,128)}), f32[8,4,128]{2,1,0:T(4,128)S(1)}, u32[]{:S(2)}, u32[]{:S(2)}) async-start(f32[8,4,128]{2,1,0:T(4,128)} %far.1), calls=%async_computation.2 | async-start | bytes 32768 | tf_op jit(solution)/shard_map/all_to_all | solution.py:560

commit v6 on v5

--- a/solution.py
+++ b/solution.py
@@ -31,20 +31,36 @@
 
 
 def embed_kernel(
-    stored_ref, count_ref, send_ref, wide_ref, taps_ref, reduce_ref, out_ref, *scratch
+    stored_ref, counts_hbm, send_hbm, wide_hbm, taps_ref, reduce_hbm, head_hbm, panel_hbm,
+    out_ref, panel_ref, head_ref, flip_ref, *scratch,
 ):
-    x_refs, hidden_refs, act_refs = scratch[0:6], scratch[6:12], scratch[12:15]
-    pool_ref, packed_pool_ref = scratch[15:17]
-    weight_refs = scratch[17:19]
-    expand_ref, depth_ref = scratch[19:21]
-    clip_ref, arrival = scratch[21:23]
+    x_refs, act_refs = scratch[0:6], scratch[10:13]
+    hidden_refs = scratch[6:10] + scratch[6:8]
+    pool_ref, packed_pool_ref = scratch[13:15]
+    weight_refs = scratch[15:17]
+    expand_ref, depth_ref, clip_ref, arrival = scratch[17:21]
+    count_ref, send_ref, wide_ref, reduce_ref, ready = scratch[21:26]
     channels, clips = clip_ref.shape[2], clip_ref.shape[3]
+    early = [
+        pltpu.make_async_copy(source, target, ready.at[at])
+        for at, (source, target) in enumerate(
+            [(counts_hbm, count_ref), (send_hbm, send_ref), (wide_hbm, wide_ref), (reduce_hbm, reduce_ref)]
+        )
+    ]
+    late = [
+        pltpu.make_async_copy(source, target, ready.at[4 + at])
+        for at, (source, target) in enumerate([(head_hbm, head_ref), (panel_hbm, panel_ref)])
+    ]
+    for copy in early:
+        copy.start()
     copies = [
         pltpu.make_async_copy(stored_ref.at[frame], clip_ref.at[frame], arrival.at[frame])
         for frame in range(clip_ref.shape[0])
     ]
     for copy in copies:
         copy.start()
+    for copy in early:
+        copy.wait()
     expanded = wide_ref.shape[2]
     eye = identity(expanded)
     for layer in range(2):
@@ -203,6 +219,8 @@
 
     copies[2].wait()
     copies[3].wait()
+    for copy in late:
+        copy.start()
     stage(0, 0, filler(lambda pair: gather(2, pair), lambda pair: expand_stored(0, 2, pair)))
     stage(0, 1, filler(lambda pair: reduce_store(0, pair), lambda pair: expand_stored(1, 0, pair)))
     stage(0, 2, filler(lambda pair: reduce_store(1, pair), lambda pair: expand_stored(1, 1, pair)))
@@ -214,6 +232,11 @@
     def _(pair):
         reduce_pool(2, pair, 1.0)
 
+    late[0].wait()
+    small = identity(256)
+    for part in range(flip_ref.shape[0] // 256):
+        part = slice(part * 256, (part + 1) * 256)
+        flip_ref[part, :] = turn(small, head_ref[:, part]).astype(BF)
     packed = packed_pool_ref[...]
     total = (
         pool_ref[...]
@@ -231,24 +254,41 @@
     rows = lax.dot_general(pick, pooled, (((1,), (1,)), ((), ())), preferred_element_type=F32)
     out_ref[:, :, :channels] = rows.astype(BF).reshape(n_dp, per_peer, channels)
     out_ref[:, :, channels:] = jnp.zeros((n_dp, per_peer, out_ref.shape[2] - channels), BF)
-
-
-def embed(clip_data, frame_counts, send_list, expand_weight, depth_kernel, reduce_weight, n_dp):
+    late[1].wait()
+
+
+def embed(
+    clip_data, frame_counts, send_list, expand_weight, depth_kernel, reduce_weight, head_weight, centroids, n_dp
+):
     clips, frames, spots, channels = clip_data.shape
     expanded = expand_weight.shape[2]
+    dims = head_weight.shape[1]
+    stored = pl.BlockSpec(memory_space=pltpu.HBM)
+    local_ref = pl.BlockSpec(memory_space=pltpu.VMEM)
     return pl.pallas_call(
         embed_kernel,
-        out_shape=jax.ShapeDtypeStruct((n_dp, clips // n_dp, 256), BF),
-        in_specs=[pl.BlockSpec(memory_space=pltpu.HBM)] + [pl.BlockSpec(memory_space=pltpu.VMEM)] * 5,
-        out_specs=pl.BlockSpec(memory_space=pltpu.VMEM),
+        out_shape=(
+            jax.ShapeDtypeStruct((n_dp, clips // n_dp, 256), BF),
+            pltpu.VMEM(centroids.shape, BF),
+            pltpu.VMEM(head_weight.shape, BF),
+            pltpu.VMEM((dims, channels), BF),
+        ),
+        in_specs=[stored] * 4 + [local_ref] + [stored] * 3,
+        out_specs=(local_ref,) * 4,
         scratch_shapes=[pltpu.VMEM((spots, channels, clips), BF)] * 6
-        + [pltpu.VMEM((spots, expanded, clips), F32)] * 6
+        + [pltpu.VMEM((spots, expanded, clips), F32)] * 4
         + [pltpu.VMEM((spots, expanded, clips), BF)] * 3
         + [pltpu.VMEM((channels, clips), F32)] * 2
         + [pltpu.VMEM((expanded // 16, 27, 16, clips), F32)] * 2
         + [pltpu.VMEM((2, expanded, channels), BF), pltpu.VMEM((2, expanded, clips), F32)]
-        + [pltpu.VMEM((frames, spots, channels, clips), BF), pltpu.SemaphoreType.DMA((frames,))],
-        compiler_params=pltpu.CompilerParams(vmem_limit_bytes=52 << 20),
+        + [pltpu.VMEM((frames, spots, channels, clips), BF), pltpu.SemaphoreType.DMA((frames,))]
+        + [pltpu.VMEM((1, clips), jnp.int32)] * 2
+        + [
+            pltpu.VMEM((2, channels, expanded), BF),
+            pltpu.VMEM((2, channels, expanded), BF),
+            pltpu.SemaphoreType.DMA((6,)),
+        ],
+        compiler_params=pltpu.CompilerParams(vmem_limit_bytes=48 << 20),
         name="embed",
     )(
         jnp.transpose(clip_data, (1, 2, 3, 0)),
@@ -257,6 +297,8 @@
         expand_weight,
         depth_kernel,
         jnp.swapaxes(reduce_weight, 1, 2),
+        head_weight,
+        centroids,
     )
 
 
@@ -268,7 +310,7 @@
 LABEL_ROWS = 16
 
 
-def own_kernel(arrived_ref, ids_ref, payload_ref, spread_ref, rows_ref):
+def own_kernel(arrived_ref, ids_ref, payload_ref, rows_ref):
     n_dp, per_peer, width = arrived_ref.shape
     clips = n_dp * per_peer
     channels = rows_ref.shape[1]
@@ -284,8 +326,6 @@
     label = jnp.where(which == 0, high, jnp.where(which == 1, low, 0))
     payload = jnp.concatenate([jnp.transpose(rows), label.astype(F32)], axis=0).astype(BF)
     payload_ref[...] = payload
-    for peer in range(n_dp):
-        spread_ref[peer] = payload
 
 
 def own(arrived, cluster_ids, channels):
@@ -296,11 +336,11 @@
         own_kernel,
         out_shape=(
             jax.ShapeDtypeStruct((height, clips), BF),
-            jax.ShapeDtypeStruct((n_dp, height, clips), BF),
             jax.ShapeDtypeStruct((clips, channels), BF),
         ),
         in_specs=[pl.BlockSpec(memory_space=pltpu.VMEM)] * 2,
-        out_specs=(pl.BlockSpec(memory_space=pltpu.VMEM),) * 3,
+        out_specs=(pl.BlockSpec(memory_space=pltpu.VMEM),) * 2,
+        compiler_params=pltpu.CompilerParams(vmem_limit_bytes=8 << 20),
         name="own",
     )(arrived, cluster_ids)
 
@@ -318,6 +358,7 @@
         out_shape=jax.ShapeDtypeStruct((clips, dims), BF),
         in_specs=[pl.BlockSpec(memory_space=pltpu.VMEM)] * 2,
         out_specs=pl.BlockSpec(memory_space=pltpu.VMEM),
+        compiler_params=pltpu.CompilerParams(vmem_limit_bytes=8 << 20),
         cost_estimate=pl.CostEstimate(
             flops=2 * clips * dims * channels, bytes_accessed=2 * dims * (clips + channels), transcendentals=0
         ),
@@ -336,126 +377,138 @@
     return label[0:1] * 256.0 + label[1:2]
 
 
-def fetch(stored_ref, panel_ref, arrival):
-    even = panel_ref.shape[0]
-    copies = []
-    for part in range(arrival.shape[0]):
-        at = slice(part * PANEL_ROWS, min(even, (part + 1) * PANEL_ROWS))
-        copy = pltpu.make_async_copy(stored_ref.at[at], panel_ref.at[at], arrival.at[part])
-        copy.start()
-        copies.append((at, copy))
-    return copies
-
-
-def score_rows(
-    rows_ref, head_ref, tail_ref, panel_rows, panel_ref, copies, turned_ref, near_ref, own_ref, best_ref, flip_ref
-):
+def score_rows(rows_ref, flip_ref, panel_ref, turned_ref, near_ref, own_ref, best_ref, send_turned, arrive):
     blocks, height, clips = rows_ref.shape
-    channels, dims = head_ref.shape
+    channels = flip_ref.shape[1]
+    panel_rows = panel_ref.shape[0]
     base = lax.axis_index("cent") * panel_rows
-    eye = identity(256)
-    for part in range(dims // 256):
-        part = slice(part * 256, (part + 1) * 256)
-        flip_ref[part, :] = turn(eye, head_ref[:, part]).astype(BF)
 
     @pl.loop(0, blocks // 2)
     def _(pair):
         both = jnp.concatenate([rows_ref[2 * pair], rows_ref[2 * pair + 1]], axis=1)
         projected = jnp.dot(flip_ref[...], both[:channels], preferred_element_type=F32)
         turned_ref[pair] = unit(projected, 0)
-        scores = jnp.dot(tail_ref[...], turned_ref[pair], preferred_element_type=F32)
-        index = lax.broadcasted_iota(jnp.int32, scores.shape, 0)
-        best_ref[pair] = jnp.where(index < panel_rows - panel_ref.shape[0], scores, -jnp.inf)
-
-    copies[0][1].wait()
+        best_ref[pair] = jnp.full((8, 2 * clips), -jnp.inf, F32)
+
+    send_turned()
+    full = panel_rows // PANEL_ROWS
+    left = panel_rows - full * PANEL_ROWS
+    whole = left // 8 * 8
+    for step in range(full):
+        arrive(step)
+        rows = slice(step * PANEL_ROWS, (step + 1) * PANEL_ROWS)
+
+        @pl.loop(0, blocks // 2)
+        def _(pair):
+            scores = jnp.dot(panel_ref[rows, :], turned_ref[pair], preferred_element_type=F32)
+            best_ref[pair] = jnp.maximum(
+                best_ref[pair], jnp.max(scores.reshape(PANEL_ROWS // 8, 8, 2 * clips), axis=0)
+            )
+            if step == 0:
+                local_id = label_of(rows_ref, pair, channels).astype(jnp.int32) - base
+                index = lax.broadcasted_iota(jnp.int32, (OCCUR, 2 * clips), 0)
+                own_ref[pair] = jnp.max(
+                    jnp.where(index == local_id, scores[:OCCUR], -jnp.inf), axis=0, keepdims=True
+                )
+
+    arrive(full)
 
     @pl.loop(0, blocks // 2)
     def _(pair):
-        scores = jnp.dot(panel_ref[:OCCUR, :], turned_ref[pair], preferred_element_type=F32)
-        local_id = label_of(rows_ref, pair, channels).astype(jnp.int32) - base
-        index = lax.broadcasted_iota(jnp.int32, (OCCUR, 2 * clips), 0)
-        own_ref[pair] = jnp.max(jnp.where(index == local_id, scores, -jnp.inf), axis=0, keepdims=True)
-
-    for part, (at, copy) in enumerate(copies):
-        if part > 0:
-            copy.wait()
-
-        @pl.loop(0, blocks // 2)
-        def _(pair):
-            scores = jnp.dot(panel_ref[at, :], turned_ref[pair], preferred_element_type=F32)
-            best_ref[pair] = jnp.maximum(
-                best_ref[pair], jnp.max(scores.reshape((at.stop - at.start) // 8, 8, 2 * clips), axis=0)
-            )
-
-    for pair in range(blocks // 2):
-        near_ref[pair] = jnp.max(best_ref[pair], axis=0, keepdims=True)
+        scores = jnp.dot(
+            panel_ref[full * PANEL_ROWS : panel_rows, :], turned_ref[pair], preferred_element_type=F32
+        )
+        best = jnp.maximum(
+            best_ref[pair], jnp.max(scores[:whole].reshape(whole // 8, 8, 2 * clips), axis=0)
+        )
+        near_ref[pair] = jnp.maximum(
+            jnp.max(best, axis=0, keepdims=True), jnp.max(scores[whole:], axis=0, keepdims=True)
+        )
 
 
 def near_kernel(
-    rows_ref, head_ref, tail_ref, stored_ref, turned_ref, near_ref, own_ref, best_ref, flip_ref, panel_ref, arrival
+    rows_ref, flip_ref, panel_ref, turned_hbm, near_ref, own_ref, spread_ref, turned_ref, best_ref, done
 ):
-    copies = fetch(stored_ref, panel_ref, arrival)
+    for peer in range(spread_ref.shape[0]):
+        spread_ref[peer] = rows_ref[0]
+    copy = pltpu.make_async_copy(turned_ref, turned_hbm, done)
     score_rows(
-        rows_ref, head_ref, tail_ref, stored_ref.shape[0], panel_ref, copies,
-        turned_ref, near_ref, own_ref, best_ref, flip_ref,
-    )
-
-
-def panel_specs(panel_rows, dims):
-    even = panel_rows // 8 * 8
-    return (
-        [pl.BlockSpec((8, dims), lambda step: (even // 8, 0)), pl.BlockSpec(memory_space=pltpu.HBM)],
-        [pltpu.VMEM((even, dims), BF), pltpu.SemaphoreType.DMA((pl.cdiv(even, PANEL_ROWS),))],
-    )
-
-
-def scores_shape(pairs, dims, width):
-    return [
-        jax.ShapeDtypeStruct((pairs, dims, width), BF),
+        rows_ref, flip_ref, panel_ref, turned_ref, near_ref, own_ref, best_ref, copy.start, lambda step: None
+    )
+    copy.wait()
+
+
+def far_kernel(
+    rows_ref, flip_ref, stored_ref, turned_hbm, near_ref, own_ref, turned_ref, best_ref, done, panel_ref, arrival
+):
+    panel_copy = pltpu.make_async_copy(stored_ref, panel_ref, arrival)
+    panel_copy.start()
+    copy = pltpu.make_async_copy(turned_ref, turned_hbm, done)
+
+    def arrive(step):
+        if step == 0:
+            panel_copy.wait()
+
+    score_rows(rows_ref, flip_ref, panel_ref, turned_ref, near_ref, own_ref, best_ref, copy.start, arrive)
+    copy.wait()
+
+
+def scored(kernel, name, rows, flip, panel, limit, spread=None):
+    blocks, height, clips = rows.shape
+    dims, channels = flip.shape
+    pairs, width = blocks // 2, 2 * clips
+    panel_rows = panel.shape[0]
+    here = pl.BlockSpec(memory_space=pltpu.VMEM)
+    stored = pl.BlockSpec(memory_space=pltpu.HBM)
+    shapes = [
+        pltpu.HBM((pairs, dims, width), BF),
         jax.ShapeDtypeStruct((pairs, 1, width), F32),
         jax.ShapeDtypeStruct((pairs, 1, width), F32),
     ]
-
-
-def near_of(rows, head_weight, centroids):
-    blocks, height, clips = rows.shape
-    channels, dims = head_weight.shape
-    pairs = blocks // 2
-    panel_rows = centroids.shape[0]
-    specs, scratch = panel_specs(panel_rows, dims)
+    scratch = [
+        pltpu.VMEM((pairs, dims, width), BF),
+        pltpu.VMEM((pairs, 8, width), F32),
+        pltpu.SemaphoreType.DMA(()),
+    ]
+    if spread is None:
+        scratch += [pltpu.VMEM(panel.shape, BF), pltpu.SemaphoreType.DMA(())]
+    else:
+        shapes.append(jax.ShapeDtypeStruct((spread, height, clips), BF))
     return pl.pallas_call(
-        near_kernel,
-        grid=(1,),
-        out_shape=scores_shape(pairs, dims, 2 * clips),
-        in_specs=[pl.BlockSpec(memory_space=pltpu.VMEM)] * 2 + specs,
-        out_specs=[pl.BlockSpec(memory_space=pltpu.VMEM)] * 3,
-        scratch_shapes=[pltpu.VMEM((pairs, 8, 2 * clips), F32), pltpu.VMEM((dims, channels), BF)] + scratch,
-        compiler_params=pltpu.CompilerParams(vmem_limit_bytes=52 << 20),
+        kernel,
+        out_shape=shapes,
+        in_specs=[here, here, stored if spread is None else here],
+        out_specs=[stored] + [here] * (len(shapes) - 1),
+        scratch_shapes=scratch,
+        compiler_params=pltpu.CompilerParams(vmem_limit_bytes=limit << 20),
         cost_estimate=pl.CostEstimate(
             flops=2 * blocks * clips * panel_rows * dims, bytes_accessed=2 * panel_rows * dims, transcendentals=0
         ),
-        name="near",
-    )(rows, head_weight, centroids, centroids)
+        name=name,
+    )(rows, flip, panel)
 
 
 GROUP = 4
 
 
-def far_kernel(
-    near_rows_ref, near_turned_ref, near_best_ref, near_own_ref, far_rows_ref, cols_ref, head_ref, tail_ref, stored_ref,
-    out_ref, far_turned_ref, far_best_ref, far_own_ref, running_ref, flip_ref, panel_ref, arrival, best_ref,
+def peer_kernel(
+    near_rows_ref, near_turned_hbm, near_best_ref, near_own_ref, far_rows_ref, far_turned_hbm, far_best_ref, far_own_ref,
+    cols_ref, head_ref, out_ref, near_turned_ref, far_turned_ref, best_ref, arrival,
 ):
-    copies = fetch(stored_ref, panel_ref, arrival)
-    score_rows(
-        far_rows_ref, head_ref, tail_ref, stored_ref.shape[0], panel_ref, copies,
-        far_turned_ref, far_best_ref, far_own_ref, running_ref, flip_ref,
-    )
+    copies = [
+        pltpu.make_async_copy(near_turned_hbm, near_turned_ref, arrival.at[0]),
+        pltpu.make_async_copy(far_turned_hbm, far_turned_ref, arrival.at[1]),
+    ]
+    for copy in copies:
+        copy.start()
     n_dp, height, clips = cols_ref.shape
     n_cent = out_ref.shape[0]
     channels = head_ref.shape[0]
     eye = identity(clips)
     best_ref[...] = jnp.full_like(best_ref, -1.0)
     mine_dp, mine_cent = lax.axis_index("dp"), lax.axis_index("cent")
+    for copy in copies:
+        copy.wait()
 
     @pl.loop(0, n_dp // GROUP)
     def _(group):
@@ -499,32 +552,32 @@
             out_ref[cent, 3:4, :] = best[:, at]
 
 
-def far_of(near_rows, near_found, far_rows, cols, head_weight, centroids):
+def peers_of(near_rows, near_found, far_rows, far_found, cols, head_weight):
     n_dp, height, clips = cols.shape
     n_cent = near_rows.shape[0] + far_rows.shape[0]
-    channels, dims = head_weight.shape
-    pairs = far_rows.shape[0] // 2
-    panel_rows = centroids.shape[0]
-    specs, scratch = panel_specs(panel_rows, dims)
-    found = [pltpu.VMEM(part.shape, part.dtype) for part in scores_shape(pairs, dims, 2 * clips)]
+    dims = head_weight.shape[1]
+    here = pl.BlockSpec(memory_space=pltpu.VMEM)
+    stored = pl.BlockSpec(memory_space=pltpu.HBM)
+    near_found, far_found = [
+        [pltpu.with_memory_space_constraint(found[0], pltpu.HBM), *found[1:]] for found in (near_found, far_found)
+    ]
     return pl.pallas_call(
-        far_kernel,
-        grid=(1,),
+        peer_kernel,
         out_shape=jax.ShapeDtypeStruct((n_cent, 4, clips), F32),
-        in_specs=[pl.BlockSpec(memory_space=pltpu.VMEM)] * 7 + specs,
-        out_specs=pl.BlockSpec(memory_space=pltpu.VMEM),
-        scratch_shapes=found
-        + [pltpu.VMEM((pairs, 8, 2 * clips), F32), pltpu.VMEM((dims, channels), BF)]
-        + scratch
-        + [pltpu.VMEM((8, n_cent * clips), F32)],
-        compiler_params=pltpu.CompilerParams(vmem_limit_bytes=44 << 20),
+        in_specs=[here, stored, here, here] * 2 + [here] * 2,
+        out_specs=here,
+        scratch_shapes=[
+            pltpu.VMEM(near_found[0].shape, BF),
+            pltpu.VMEM(far_found[0].shape, BF),
+            pltpu.VMEM((8, n_cent * clips), F32),
+            pltpu.SemaphoreType.DMA((2,)),
+        ],
+        compiler_params=pltpu.CompilerParams(vmem_limit_bytes=16 << 20),
         cost_estimate=pl.CostEstimate(
-            flops=2 * clips * dims * (2 * pairs * panel_rows + n_dp * n_cent * clips),
-            bytes_accessed=2 * panel_rows * dims,
-            transcendentals=0,
+            flops=2 * n_dp * n_cent * clips * clips * dims, bytes_accessed=4 << 20, transcendentals=0
         ),
-        name="far",
-    )(near_rows, *near_found, far_rows, cols, head_weight, centroids, centroids)
+        name="peers",
+    )(near_rows, *near_found, far_rows, *far_found, cols, head_weight)
 
 
 def local(
@@ -540,11 +593,11 @@
 ):
     n_dp = lax.axis_size("dp")
     n_cent = lax.axis_size("cent")
-    pooled = embed(
-        clip_data, frame_counts, send_list, expand_weight, depth_kernel, reduce_weight, n_dp
+    pooled, panel, head, flip = embed(
+        clip_data, frame_counts, send_list, expand_weight, depth_kernel, reduce_weight, head_weight, centroids, n_dp
     )
     arrived = lax.all_to_all(pooled, "dp", split_axis=0, concat_axis=0, tiled=True)
-    payload, spread, rows = own(arrived, cluster_ids, head_weight.shape[0])
+    payload, rows = own(arrived, cluster_ids, head_weight.shape[0])
     partner = lax.ppermute(payload, "cent", [(at, at ^ 1) for at in range(n_cent)])
     near_rows = jnp.stack([payload, partner])
     far_rows = jnp.concatenate(
@@ -553,10 +606,13 @@
             for chip in range(1, n_cent // 2)
         ]
     )
+    *near_found, spread = scored(near_kernel, "near", near_rows, flip, panel, 16, n_dp)
     cols = lax.all_to_all(spread, "dp", split_axis=0, concat_axis=0, tiled=True)
-    vectors = vectors_of(rows, head_weight)
-    near_found = near_of(near_rows, head_weight, centroids)
-    partial = far_of(near_rows, near_found, far_rows, cols, head_weight, centroids)
+    vectors = vectors_of(rows, head)
+    far_found = scored(
+        far_kernel, "far", far_rows, flip, pltpu.with_memory_space_constraint(centroids, pltpu.HBM), 32
+    )
+    partial = peers_of(near_rows, near_found, far_rows, far_found, cols, head)
     parts = lax.all_to_all(partial, "cent", split_axis=0, concat_axis=0, tiled=True)
     final = jnp.max(parts, axis=0)
     return (vectors, final[0], final[1], final[2])

time: 114 us -> 108 us (0.947)
  local copies, waits for them, and re-layouts: 5.64 us -> 2.03 us
  Pallas kernels: 71.8 us -> 70.2 us
    unnamed x13 -> x5, local copies, waits for them, and re-layouts: 5.12 us -> 1.49 us
    pallas_call x1, Pallas kernels: 2.01 us -> 0.23 us  [own(): pl.pallas_call(own_kernel, out_shape=(jax.ShapeDtypeStruct((height, clips...]
    pallas_call x3 -> x4, Pallas kernels: 67.7 us -> 69 us  [the longest x1 34.6 us: embed(): pl.pallas_call(embed_kernel, out_shape=(jax.ShapeDtypeStruct((n_dp, clips...]
  transfers between devices with their start and end apart: 6 -> 6, of which waited for: 2 -> 2; matrix products, arithmetic and copies ran while one was open for 1% -> 0% of each run, Pallas kernels for 11% -> 24%
where the time goes in v6:
time: 108 us
  Pallas kernels  70.2 us (65%)
  starting transfers between devices  15.3 us (14%)
  blocking collectives  15.1 us (14%)
  waiting for transfers between devices  4.55 us (4%)
  local copies, waits for them, and re-layouts  2.03 us (2%)
    pallas_call x1, Pallas kernels, embed(): pl.pallas_call(embed_kernel, out_shape=(jax.ShapeDtypeStruct((n_dp, clips...  34.6 us
    pallas_call x2, Pallas kernels, scored(): pl.pallas_call(kernel, out_shape=shapes, in_specs=[here, here, stored if...  25 us
    all_to_all x1, blocking collectives, local(): lax.all_to_all(pooled, 'dp', split_axis=0, concat_axis=0, tiled=True)  15.1 us
    pallas_call x1, Pallas kernels, peers_of(): pl.pallas_call(peer_kernel, out_shape=jax.ShapeDtypeStruct((n_cent, 4, cl...  9.39 us
    ppermute x3, starting transfers between devices, local(): lax.ppermute(near_rows, 'cent', [((at + 2 * chip) % n_cent, at) for at in...  4.91 us
    all_to_all x1, starting transfers between devices, local(): lax.all_to_all(partial, 'cent', split_axis=0, concat_axis=0, tiled=True)  4.43 us
    all_to_all x1, starting transfers between devices, local(): cols = lax.all_to_all(spread, 'dp', split_axis=0, concat_axis=0, tiled=True)  3.82 us
    all_to_all x1, waiting for transfers between devices, local(): lax.all_to_all(partial, 'cent', split_axis=0, concat_axis=0, tiled=True)  3.65 us
  transfers between devices with their start and end apart: 6, of which 2 were waited for; matrix products, arithmetic and copies ran while one was open for 0% of the time, Pallas kernels for 24%

profile of v6, /device:TPU:1, one launch (start us, length us, event | category | flops | bytes accessed | tf_op | source)
XLA Modules:
  0.0 108.0 jit_solution(3202253615463295633)
XLA Ops:
  0.6 0.0 copy-start
  0.6 1.5 %copy.13.taps_ref = bf16[2,27,432]{2,1,0:T(8,128)(2,1)} copy(bf16[2,27,432]{2,0,1:T(2,128)(2,1)} %param.14) | data formatting | bytes 93312 | tf_op args[5]
  2.1 34.6 %embed.1 = (bf16[16,8,256]{2,1,0:T(8,128)(2,1)}, bf16[6250,1024]{1,0:T(8,128)(2,1)S(1)}, bf16[192,1024]{1,0:T(8,128)(2,1)S(1)}, bf16[1024,192]{1,0:T(8,128)(2,1)S(1)}) custom-call(bf16[4,16,192,128]{3,2,1,0:T(8,128)(2,1)} %bitcast.11, s32[1,128]{1,0:T(1,128)} %counts_hbm.1, s32[1,128]{1,0:T(1,128)} %send_hbm.1, bf16[2,192,432]{2,1,0:T(8,128)(2,1)} %wide_hbm.1, ...), custom_call_target="tpu_custom_call" | custom-call | tf_op jit(solution)/shard_map/embed/pallas_call | solution.py:268
  36.7 15.1 %all_to_all.15.arrived_ref = bf16[16,8,256]{2,1,0:T(8,128)(2,1)S(1)} all-to-all(bf16[16,8,256]{2,1,0:T(8,128)(2,1)} %get-tuple-element.17), channel_id=1, replica_groups=mesh['dp'=16,'cent'=8] {'dp'}, dimensions={0} | all-to-all | bytes 131072 | tf_op jit(solution)/shard_map/all_to_all | solution.py:599
  51.8 0.0 copy-done
  51.8 0.2 own.1
  52.1 2.2 %collective-permute-start = (bf16[208,128]{1,0:T(8,128)(2,1)S(1)}, bf16[208,128]{1,0:T(8,128)(2,1)S(1)}, u32[]{:S(2)}, u32[]{:S(2)}) collective-permute-start(bf16[208,128]{1,0:T(8,128)(2,1)S(1)} %get-tuple-element.20), channel_id=1, source_target_pairs={{0,1},{1,0},{2,3},{3,2},{4,5},{5,4},{6,7},{7,6},{8,9},{9,8},{10,11... | collective-permute-start | bytes 159752 | tf_op jit(solution)/shard_map/ppermute | solution.py:601
  54.2 0.9 collective-permute-done
  55.1 1.3 %collective-permute-start.3 = (bf16[2,208,128]{2,1,0:T(8,128)(2,1)S(1)}, bf16[2,208,128]{2,1,0:T(8,128)(2,1)S(1)}, u32[]{:S(2)}, u32[]{:S(2)}) collective-permute-start(bf16[2,208,128]{2,1,0:T(8,128)(2,1)S(1)} %pad_maximum_fusion.rows_ref.near_rows_ref), channel_id=1, source_target_pairs={{6,0},{7,1},{0,2},{1,3},{2,4},{3,5},{4,6},{5,7},{14,8},{15,9},{8,1... | collective-permute-start | bytes 319496 | tf_op jit(solution)/shard_map/ppermute | solution.py:605
  56.5 2.4 %collective-permute-start.2 = (bf16[2,208,128]{2,1,0:T(8,128)(2,1)S(1)}, bf16[2,208,128]{2,1,0:T(8,128)(2,1)S(1)}, u32[]{:S(2)}, u32[]{:S(2)}) collective-permute-start(bf16[2,208,128]{2,1,0:T(8,128)(2,1)S(1)} %pad_maximum_fusion.rows_ref.near_rows_ref), channel_id=1, source_target_pairs={{4,0},{5,1},{6,2},{7,3},{0,4},{1,5},{2,6},{3,7},{12,8},{13,9},{14,... | collective-permute-start | bytes 319496 | tf_op jit(solution)/shard_map/ppermute | solution.py:605
  58.9 1.2 %collective-permute-start.1 = (bf16[2,208,128]{2,1,0:T(8,128)(2,1)S(1)}, bf16[2,208,128]{2,1,0:T(8,128)(2,1)S(1)}, u32[]{:S(2)}, u32[]{:S(2)}) collective-permute-start(bf16[2,208,128]{2,1,0:T(8,128)(2,1)S(1)} %pad_maximum_fusion.rows_ref.near_rows_ref), channel_id=1, source_target_pairs={{2,0},{3,1},{4,2},{5,3},{6,4},{7,5},{0,6},{1,7},{10,8},{11,9},{12,... | collective-permute-start | bytes 319496 | tf_op jit(solution)/shard_map/ppermute | solution.py:605
  60.1 5.6 %near.1 = (bf16[1,1024,256]{2,1,0:T(8,128)(2,1)}, f32[1,1,256]{2,1,0:T(1,128)S(1)}, f32[1,1,256]{2,1,0:T(1,128)S(1)}, bf16[16,208,128]{2,1,0:T(8,128)(2,1)}) custom-call(bf16[2,208,128]{2,1,0:T(8,128)(2,1)S(1)} %pad_maximum_fusion.rows_ref.near_rows_ref, bf16[1024,192]{1,0:T(8,128)(2,1)S(1)} %get-tuple-element.21.flip_ref, ...), custom_call_target="tpu_custom_call" | custom-call | flops 3276800000 | bytes 12800000 | tf_op jit(solution)/shard_map/near/pallas_call | solution.py:477
  65.7 3.8 %all-to-all-start.1 = ((bf16[16,208,128]{2,1,0:T(8,128)(2,1)}), bf16[16,208,128]{2,1,0:T(8,128)(2,1)S(1)}, u32[]{:S(2)}, u32[]{:S(2)}) async-start(bf16[16,208,128]{2,1,0:T(8,128)(2,1)} %get-tuple-element.29), calls=%async_computation.1 | async-start | bytes 1703936 | tf_op jit(solution)/shard_map/all_to_all | solution.py:610
  69.5 0.0 collective-permute-done.1
  69.5 0.0 collective-permute-done.2
  69.6 0.0 collective-permute-done.3
  69.6 19.4 %far.1 = (bf16[3,1024,256]{2,1,0:T(8,128)(2,1)}, f32[3,1,256]{2,1,0:T(1,128)S(1)}, f32[3,1,256]{2,1,0:T(1,128)S(1)}) custom-call(bf16[6,208,128]{2,1,0:T(8,128)(2,1)S(1)} %constant_dynamic-update-slice_fusion.rows_ref.far_rows_ref, bf16[1024,192]{1,0:T(8,128)(2,1)S(1)} %get-tuple-element.21.flip_ref, bf16[6250,1024]{1,0:T(8,128)(2,1)} %stored_ref.1), custom_call_target="tpu_custom_call" | custom-call | flops 9830400000 | bytes 12800000 | tf_op jit(solution)/shard_map/far/pallas_call | solution.py:477
  88.9 0.0 all-to-all-done.1.cols_ref
  89.0 9.4 %peers.1 = f32[8,4,128]{2,1,0:T(4,128)} custom-call(bf16[2,208,128]{2,1,0:T(8,128)(2,1)S(1)} %pad_maximum_fusion.rows_ref.near_rows_ref, bf16[1,1024,256]{2,1,0:T(8,128)(2,1)} %get-tuple-element.23.near_turned_hbm, f32[1,1,256]{2,1,0:T(1,128)S(1)} %get-tuple-element.24.near_best_ref, f32[1,1,256]{2,1,0:T(1,128)S(1)} %get-tuple-element.25.near_own_ref, ...), custom_call_target="tpu_custom_call" | custom-call | flops 4294967296 | bytes 4194304 | tf_op jit(solution)/shard_map/peers/pallas_call | solution.py:564
  98.4 4.4 %all-to-all-start.2 = ((f32[8,4,128]{2,1,0:T(4,128)}), f32[8,4,128]{2,1,0:T(4,128)S(1)}, u32[]{:S(2)}, u32[]{:S(2)}) async-start(f32[8,4,128]{2,1,0:T(4,128)} %peers.1), calls=%async_computation.2 | async-start | bytes 32768 | tf_op jit(solution)/shard_map/all_to_all | solution.py:616
  102.8 1.0 vectors.1
  103.8 3.7 %all-to-all-done.2 = f32[8,4,128]{2,1,0:T(4,128)S(1)} async-done(((f32[8,4,128]{2,1,0:T(4,128)}), f32[8,4,128]{2,1,0:T(4,128)S(1)}, u32[]{:S(2)}, u32[]{:S(2)}) %all-to-all-start.2) | async-done | bytes 16416 | tf_op jit(solution)/shard_map/all_to_all | solution.py:616
  107.5 0.5 slice_bitcast_fusion
  (5 shorter events, 0.1 us)
Async XLA Ops:
  0.6 51.2 %copy-start = (s32[1,128]{1,0:T(1,128)S(1)}, s32[1,128]{1,0:T(1,128)}, u32[]{:S(2)}) copy-start(s32[1,128]{1,0:T(1,128)} %ids_ref.1) | copy-start | bytes 1540
  52.1 3.1 %collective-permute-start = (bf16[208,128]{1,0:T(8,128)(2,1)S(1)}, bf16[208,128]{1,0:T(8,128)(2,1)S(1)}, u32[]{:S(2)}, u32[]{:S(2)}) collective-permute-start(bf16[208,128]{1,0:T(8,128)(2,1)S(1)} %get-tuple-element.20), channel_id=1, source_target_pairs={{0,1},{1,0},{2,3},{3,2},{4,5},{5,4},{6,7},{7,6},{8,9},{9,8},{10,11... | collective-permute-start | bytes 159752 | tf_op jit(solution)/shard_map/ppermute | solution.py:601
  55.1 14.4 %collective-permute-start.3 = (bf16[2,208,128]{2,1,0:T(8,128)(2,1)S(1)}, bf16[2,208,128]{2,1,0:T(8,128)(2,1)S(1)}, u32[]{:S(2)}, u32[]{:S(2)}) collective-permute-start(bf16[2,208,128]{2,1,0:T(8,128)(2,1)S(1)} %pad_maximum_fusion.rows_ref.near_rows_ref), channel_id=1, source_target_pairs={{6,0},{7,1},{0,2},{1,3},{2,4},{3,5},{4,6},{5,7},{14,8},{15,9},{8,1... | collective-permute-start | bytes 319496 | tf_op jit(solution)/shard_map/ppermute | solution.py:605
  56.5 13.1 %collective-permute-start.2 = (bf16[2,208,128]{2,1,0:T(8,128)(2,1)S(1)}, bf16[2,208,128]{2,1,0:T(8,128)(2,1)S(1)}, u32[]{:S(2)}, u32[]{:S(2)}) collective-permute-start(bf16[2,208,128]{2,1,0:T(8,128)(2,1)S(1)} %pad_maximum_fusion.rows_ref.near_rows_ref), channel_id=1, source_target_pairs={{4,0},{5,1},{6,2},{7,3},{0,4},{1,5},{2,6},{3,7},{12,8},{13,9},{14,... | collective-permute-start | bytes 319496 | tf_op jit(solution)/shard_map/ppermute | solution.py:605
  58.9 10.6 %collective-permute-start.1 = (bf16[2,208,128]{2,1,0:T(8,128)(2,1)S(1)}, bf16[2,208,128]{2,1,0:T(8,128)(2,1)S(1)}, u32[]{:S(2)}, u32[]{:S(2)}) collective-permute-start(bf16[2,208,128]{2,1,0:T(8,128)(2,1)S(1)} %pad_maximum_fusion.rows_ref.near_rows_ref), channel_id=1, source_target_pairs={{2,0},{3,1},{4,2},{5,3},{6,4},{7,5},{0,6},{1,7},{10,8},{11,9},{12,... | collective-permute-start | bytes 319496 | tf_op jit(solution)/shard_map/ppermute | solution.py:605
  65.7 23.3 %all-to-all-start.1 = ((bf16[16,208,128]{2,1,0:T(8,128)(2,1)}), bf16[16,208,128]{2,1,0:T(8,128)(2,1)S(1)}, u32[]{:S(2)}, u32[]{:S(2)}) async-start(bf16[16,208,128]{2,1,0:T(8,128)(2,1)} %get-tuple-element.29), calls=%async_computation.1 | async-start | bytes 1703936 | tf_op jit(solution)/shard_map/all_to_all | solution.py:610
  98.4 9.1 %all-to-all-start.2 = ((f32[8,4,128]{2,1,0:T(4,128)}), f32[8,4,128]{2,1,0:T(4,128)S(1)}, u32[]{:S(2)}, u32[]{:S(2)}) async-start(f32[8,4,128]{2,1,0:T(4,128)} %peers.1), calls=%async_computation.2 | async-start | bytes 32768 | tf_op jit(solution)/shard_map/all_to_all | solution.py:616

commit v7 on v6

--- a/solution.py
+++ b/solution.py
@@ -368,6 +368,7 @@
 
 PANEL_ROWS = 784
 OCCUR = 64
+LEFT = 2
 
 
 def label_of(rows_ref, block, channels):
@@ -377,32 +378,29 @@
     return label[0:1] * 256.0 + label[1:2]
 
 
-def score_rows(rows_ref, flip_ref, panel_ref, turned_ref, near_ref, own_ref, best_ref, send_turned, arrive):
+def score_rows(rows_ref, flip_ref, panel_ref, turned_ref, near_ref, own_ref, best_ref, send_turned, arrive, extra):
     blocks, height, clips = rows_ref.shape
     channels = flip_ref.shape[1]
-    panel_rows = panel_ref.shape[0]
-    base = lax.axis_index("cent") * panel_rows
+    panel_rows = panel_ref.shape[0] // 8 * 8
 
     @pl.loop(0, blocks // 2)
     def _(pair):
         both = jnp.concatenate([rows_ref[2 * pair], rows_ref[2 * pair + 1]], axis=1)
         projected = jnp.dot(flip_ref[...], both[:channels], preferred_element_type=F32)
         turned_ref[pair] = unit(projected, 0)
-        best_ref[pair] = jnp.full((8, 2 * clips), -jnp.inf, F32)
+        best_ref[pair] = jnp.dot(extra, turned_ref[pair], preferred_element_type=F32)
 
     send_turned()
-    full = panel_rows // PANEL_ROWS
-    left = panel_rows - full * PANEL_ROWS
-    whole = left // 8 * 8
-    for step in range(full):
+    base = lax.axis_index("cent") * (panel_rows + LEFT)
+    for step in range(pl.cdiv(panel_rows, PANEL_ROWS)):
         arrive(step)
-        rows = slice(step * PANEL_ROWS, (step + 1) * PANEL_ROWS)
+        rows = slice(step * PANEL_ROWS, min(panel_rows, (step + 1) * PANEL_ROWS))
 
         @pl.loop(0, blocks // 2)
         def _(pair):
             scores = jnp.dot(panel_ref[rows, :], turned_ref[pair], preferred_element_type=F32)
             best_ref[pair] = jnp.maximum(
-                best_ref[pair], jnp.max(scores.reshape(PANEL_ROWS // 8, 8, 2 * clips), axis=0)
+                best_ref[pair], jnp.max(scores.reshape((rows.stop - rows.start) // 8, 8, 2 * clips), axis=0)
             )
             if step == 0:
                 local_id = label_of(rows_ref, pair, channels).astype(jnp.int32) - base
@@ -411,49 +409,43 @@
                     jnp.where(index == local_id, scores[:OCCUR], -jnp.inf), axis=0, keepdims=True
                 )
 
-    arrive(full)
-
-    @pl.loop(0, blocks // 2)
-    def _(pair):
-        scores = jnp.dot(
-            panel_ref[full * PANEL_ROWS : panel_rows, :], turned_ref[pair], preferred_element_type=F32
-        )
-        best = jnp.maximum(
-            best_ref[pair], jnp.max(scores[:whole].reshape(whole // 8, 8, 2 * clips), axis=0)
-        )
-        near_ref[pair] = jnp.maximum(
-            jnp.max(best, axis=0, keepdims=True), jnp.max(scores[whole:], axis=0, keepdims=True)
-        )
+    for pair in range(blocks // 2):
+        near_ref[pair] = jnp.max(best_ref[pair], axis=0, keepdims=True)
 
 
 def near_kernel(
-    rows_ref, flip_ref, panel_ref, turned_hbm, near_ref, own_ref, spread_ref, turned_ref, best_ref, done
+    rows_ref, flip_ref, panel_ref, turned_hbm, near_ref, own_ref, spread_ref, extra_ref, turned_ref, best_ref, done
 ):
     for peer in range(spread_ref.shape[0]):
         spread_ref[peer] = rows_ref[0]
+    panel_rows = panel_ref.shape[0]
+    left = panel_ref[panel_rows - LEFT : panel_rows, :]
+    extra = jnp.concatenate([left] * (8 // LEFT), axis=0)
+    extra_ref[...] = extra
     copy = pltpu.make_async_copy(turned_ref, turned_hbm, done)
     score_rows(
-        rows_ref, flip_ref, panel_ref, turned_ref, near_ref, own_ref, best_ref, copy.start, lambda step: None
+        rows_ref, flip_ref, panel_ref, turned_ref, near_ref, own_ref, best_ref, copy.start, lambda step: None, extra
     )
     copy.wait()
 
 
 def far_kernel(
-    rows_ref, flip_ref, stored_ref, turned_hbm, near_ref, own_ref, turned_ref, best_ref, done, panel_ref, arrival
+    rows_ref, flip_ref, stored_ref, extra_ref, turned_hbm, near_ref, own_ref, turned_ref, best_ref, done, panel_ref, arrival
 ):
-    panel_copy = pltpu.make_async_copy(stored_ref, panel_ref, arrival)
-    panel_copy.start()
+    copies = []
+    for step in range(arrival.shape[0]):
+        rows = slice(step * PANEL_ROWS, min(panel_ref.shape[0], (step + 1) * PANEL_ROWS))
+        copies.append(pltpu.make_async_copy(stored_ref.at[rows], panel_ref.at[rows], arrival.at[step]))
+        copies[-1].start()
     copy = pltpu.make_async_copy(turned_ref, turned_hbm, done)
-
-    def arrive(step):
-        if step == 0:
-            panel_copy.wait()
-
-    score_rows(rows_ref, flip_ref, panel_ref, turned_ref, near_ref, own_ref, best_ref, copy.start, arrive)
+    score_rows(
+        rows_ref, flip_ref, panel_ref, turned_ref, near_ref, own_ref, best_ref,
+        copy.start, lambda step: copies[step].wait(), extra_ref[...],
+    )
     copy.wait()
 
 
-def scored(kernel, name, rows, flip, panel, limit, spread=None):
+def scored(kernel, name, rows, flip, panel, limit, spread=None, extra=None):
     blocks, height, clips = rows.shape
     dims, channels = flip.shape
     pairs, width = blocks // 2, 2 * clips
@@ -471,13 +463,18 @@
         pltpu.SemaphoreType.DMA(()),
     ]
     if spread is None:
-        scratch += [pltpu.VMEM(panel.shape, BF), pltpu.SemaphoreType.DMA(())]
+        even = panel_rows // 8 * 8
+        scratch += [
+            pltpu.VMEM((even, dims), BF), pltpu.SemaphoreType.DMA((pl.cdiv(even, PANEL_ROWS),))
+        ]
     else:
+        assert panel_rows % 8 == LEFT
         shapes.append(jax.ShapeDtypeStruct((spread, height, clips), BF))
+        shapes.append(jax.ShapeDtypeStruct((8, dims), BF))
     return pl.pallas_call(
         kernel,
         out_shape=shapes,
-        in_specs=[here, here, stored if spread is None else here],
+        in_specs=[here, here] + ([stored, here] if spread is None else [here]),
         out_specs=[stored] + [here] * (len(shapes) - 1),
         scratch_shapes=scratch,
         compiler_params=pltpu.CompilerParams(vmem_limit_bytes=limit << 20),
@@ -485,7 +482,7 @@
             flops=2 * blocks * clips * panel_rows * dims, bytes_accessed=2 * panel_rows * dims, transcendentals=0
         ),
         name=name,
-    )(rows, flip, panel)
+    )(rows, flip, panel, *([extra] if spread is None else []))
 
 
 GROUP = 4
@@ -507,8 +504,6 @@
     eye = identity(clips)
     best_ref[...] = jnp.full_like(best_ref, -1.0)
     mine_dp, mine_cent = lax.axis_index("dp"), lax.axis_index("cent")
-    for copy in copies:
-        copy.wait()
 
     @pl.loop(0, n_dp // GROUP)
     def _(group):
@@ -519,6 +514,8 @@
         wide = jnp.broadcast_to(ids, (GROUP * clips, 2 * clips))
         for block in range(n_cent // 2):
             cols = slice(block * 2 * clips, (block + 1) * 2 * clips)
+            if block < 2:
+                pl.when(group == 0)(copies[block].wait)
             if block == 0:
                 turned, row_ids = near_turned_ref[0], label_of(near_rows_ref, 0, channels)
             else:
@@ -606,11 +603,11 @@
             for chip in range(1, n_cent // 2)
         ]
     )
-    *near_found, spread = scored(near_kernel, "near", near_rows, flip, panel, 16, n_dp)
+    *near_found, spread, extra = scored(near_kernel, "near", near_rows, flip, panel, 16, n_dp)
     cols = lax.all_to_all(spread, "dp", split_axis=0, concat_axis=0, tiled=True)
     vectors = vectors_of(rows, head)
     far_found = scored(
-        far_kernel, "far", far_rows, flip, pltpu.with_memory_space_constraint(centroids, pltpu.HBM), 32
+        far_kernel, "far", far_rows, flip, pltpu.with_memory_space_constraint(centroids, pltpu.HBM), 32, extra=extra
     )
     partial = peers_of(near_rows, near_found, far_rows, far_found, cols, head)
     parts = lax.all_to_all(partial, "cent", split_axis=0, concat_axis=0, tiled=True)

time: 108 us -> 108 us (level)
    pallas_call x2, Pallas kernels: 25 us -> 22.2 us  [scored(): pl.pallas_call(kernel, out_shape=shapes, in_specs=[here, here] + ([stored...]
    pallas_call x1, Pallas kernels: 9.39 us -> 11.6 us  [peers_of(): pl.pallas_call(peer_kernel, out_shape=jax.ShapeDtypeStruct((n_cent, 4, cl...]
  transfers between devices with their start and end apart: 6 -> 6, of which waited for: 2 -> 2; matrix products, arithmetic and copies ran while one was open for 0% -> 0% of each run, Pallas kernels for 24% -> 22%
where the time goes in v7:
time: 108 us; the launch traced here: 107 us
  Pallas kernels  69.7 us (65%)
  starting transfers between devices  15.3 us (14%)
  blocking collectives  15.1 us (14%)
  waiting for transfers between devices  4.55 us (4%)
  local copies, waits for them, and re-layouts  2.03 us (2%)
    pallas_call x1, Pallas kernels, embed(): pl.pallas_call(embed_kernel, out_shape=(jax.ShapeDtypeStruct((n_dp, clips...  34.6 us
    pallas_call x2, Pallas kernels, scored(): pl.pallas_call(kernel, out_shape=shapes, in_specs=[here, here] + ([stored...  22.2 us
    all_to_all x1, blocking collectives, local(): lax.all_to_all(pooled, 'dp', split_axis=0, concat_axis=0, tiled=True)  15.1 us
    pallas_call x1, Pallas kernels, peers_of(): pl.pallas_call(peer_kernel, out_shape=jax.ShapeDtypeStruct((n_cent, 4, cl...  11.6 us
    ppermute x3, starting transfers between devices, local(): lax.ppermute(near_rows, 'cent', [((at + 2 * chip) % n_cent, at) for at in...  4.91 us
    all_to_all x1, starting transfers between devices, local(): lax.all_to_all(partial, 'cent', split_axis=0, concat_axis=0, tiled=True)  4.42 us
    all_to_all x1, starting transfers between devices, local(): cols = lax.all_to_all(spread, 'dp', split_axis=0, concat_axis=0, tiled=True)  3.82 us
    all_to_all x1, waiting for transfers between devices, local(): lax.all_to_all(partial, 'cent', split_axis=0, concat_axis=0, tiled=True)  3.65 us
  transfers between devices with their start and end apart: 6, of which 2 were waited for; matrix products, arithmetic and copies ran while one was open for 0% of the time, Pallas kernels for 22%

profile of v7, /device:TPU:1, one launch (start us, length us, event | category | flops | bytes accessed | tf_op | source)
XLA Modules:
  0.0 107.5 jit_solution(15957056786563029634)
XLA Ops:
  0.6 0.0 copy-start
  0.6 1.5 %copy.13.taps_ref = bf16[2,27,432]{2,1,0:T(8,128)(2,1)} copy(bf16[2,27,432]{2,0,1:T(2,128)(2,1)} %param.14) | data formatting | bytes 93312 | tf_op args[5]
  2.1 34.6 %embed.1 = (bf16[16,8,256]{2,1,0:T(8,128)(2,1)}, bf16[6250,1024]{1,0:T(8,128)(2,1)S(1)}, bf16[192,1024]{1,0:T(8,128)(2,1)S(1)}, bf16[1024,192]{1,0:T(8,128)(2,1)S(1)}) custom-call(bf16[4,16,192,128]{3,2,1,0:T(8,128)(2,1)} %bitcast.11, s32[1,128]{1,0:T(1,128)} %counts_hbm.1, s32[1,128]{1,0:T(1,128)} %send_hbm.1, bf16[2,192,432]{2,1,0:T(8,128)(2,1)} %wide_hbm.1, ...), custom_call_target="tpu_custom_call" | custom-call | tf_op jit(solution)/shard_map/embed/pallas_call | solution.py:268
  36.7 15.1 %all_to_all.15.arrived_ref = bf16[16,8,256]{2,1,0:T(8,128)(2,1)S(1)} all-to-all(bf16[16,8,256]{2,1,0:T(8,128)(2,1)} %get-tuple-element.18), channel_id=1, replica_groups=mesh['dp'=16,'cent'=8] {'dp'}, dimensions={0} | all-to-all | bytes 131072 | tf_op jit(solution)/shard_map/all_to_all | solution.py:596
  51.8 0.0 copy-done
  51.8 0.2 own.1
  52.1 2.2 %collective-permute-start = (bf16[208,128]{1,0:T(8,128)(2,1)S(1)}, bf16[208,128]{1,0:T(8,128)(2,1)S(1)}, u32[]{:S(2)}, u32[]{:S(2)}) collective-permute-start(bf16[208,128]{1,0:T(8,128)(2,1)S(1)} %get-tuple-element.21), channel_id=1, source_target_pairs={{0,1},{1,0},{2,3},{3,2},{4,5},{5,4},{6,7},{7,6},{8,9},{9,8},{10,11... | collective-permute-start | bytes 159752 | tf_op jit(solution)/shard_map/ppermute | solution.py:598
  54.2 0.9 collective-permute-done
  55.1 1.3 %collective-permute-start.3 = (bf16[2,208,128]{2,1,0:T(8,128)(2,1)S(1)}, bf16[2,208,128]{2,1,0:T(8,128)(2,1)S(1)}, u32[]{:S(2)}, u32[]{:S(2)}) collective-permute-start(bf16[2,208,128]{2,1,0:T(8,128)(2,1)S(1)} %pad_maximum_fusion.rows_ref.near_rows_ref), channel_id=1, source_target_pairs={{6,0},{7,1},{0,2},{1,3},{2,4},{3,5},{4,6},{5,7},{14,8},{15,9},{8,1... | collective-permute-start | bytes 319496 | tf_op jit(solution)/shard_map/ppermute | solution.py:602
  56.5 2.4 %collective-permute-start.2 = (bf16[2,208,128]{2,1,0:T(8,128)(2,1)S(1)}, bf16[2,208,128]{2,1,0:T(8,128)(2,1)S(1)}, u32[]{:S(2)}, u32[]{:S(2)}) collective-permute-start(bf16[2,208,128]{2,1,0:T(8,128)(2,1)S(1)} %pad_maximum_fusion.rows_ref.near_rows_ref), channel_id=1, source_target_pairs={{4,0},{5,1},{6,2},{7,3},{0,4},{1,5},{2,6},{3,7},{12,8},{13,9},{14,... | collective-permute-start | bytes 319496 | tf_op jit(solution)/shard_map/ppermute | solution.py:602
  58.9 1.2 %collective-permute-start.1 = (bf16[2,208,128]{2,1,0:T(8,128)(2,1)S(1)}, bf16[2,208,128]{2,1,0:T(8,128)(2,1)S(1)}, u32[]{:S(2)}, u32[]{:S(2)}) collective-permute-start(bf16[2,208,128]{2,1,0:T(8,128)(2,1)S(1)} %pad_maximum_fusion.rows_ref.near_rows_ref), channel_id=1, source_target_pairs={{2,0},{3,1},{4,2},{5,3},{6,4},{7,5},{0,6},{1,7},{10,8},{11,9},{12,... | collective-permute-start | bytes 319496 | tf_op jit(solution)/shard_map/ppermute | solution.py:602
  60.1 5.7 %near.1 = (bf16[1,1024,256]{2,1,0:T(8,128)(2,1)}, f32[1,1,256]{2,1,0:T(1,128)S(1)}, f32[1,1,256]{2,1,0:T(1,128)S(1)}, bf16[16,208,128]{2,1,0:T(8,128)(2,1)}, bf16[8,1024]{1,0:T(8,128)(2,1)S(1)}) custom-call(bf16[2,208,128]{2,1,0:T(8,128)(2,1)S(1)} %pad_maximum_fusion.rows_ref.near_rows_ref, bf16[1024,192]{1,0:T(8,128)(2,1)S(1)} %get-tuple-element.22.flip_ref, ...), custom_call_target="tpu_custom_call" | custom-call | flops 3276800000 | bytes 12800000 | tf_op jit(solution)/shard_map/near/pallas_call | solution.py:474
  65.8 3.8 %all-to-all-start.1 = ((bf16[16,208,128]{2,1,0:T(8,128)(2,1)}), bf16[16,208,128]{2,1,0:T(8,128)(2,1)S(1)}, u32[]{:S(2)}, u32[]{:S(2)}) async-start(bf16[16,208,128]{2,1,0:T(8,128)(2,1)} %get-tuple-element.31), calls=%async_computation.1 | async-start | bytes 1703936 | tf_op jit(solution)/shard_map/all_to_all | solution.py:607
  69.6 0.0 collective-permute-done.1
  69.6 0.0 collective-permute-done.2
  69.7 0.0 collective-permute-done.3
  69.7 16.5 %far.1 = (bf16[3,1024,256]{2,1,0:T(8,128)(2,1)}, f32[3,1,256]{2,1,0:T(1,128)S(1)}, f32[3,1,256]{2,1,0:T(1,128)S(1)}) custom-call(bf16[6,208,128]{2,1,0:T(8,128)(2,1)S(1)} %constant_dynamic-update-slice_fusion.rows_ref.far_rows_ref, bf16[1024,192]{1,0:T(8,128)(2,1)S(1)} %get-tuple-element.22.flip_ref, bf16[6250,1024]{1,0:T(8,128)(2,1)} %stored_ref.1, ...), custom_call_target="tpu_custom_call" | custom-call | flops 9830400000 | bytes 12800000 | tf_op jit(solution)/shard_map/far/pallas_call | solution.py:474
  86.2 0.0 all-to-all-done.1.cols_ref
  86.2 11.6 %peers.1 = f32[8,4,128]{2,1,0:T(4,128)} custom-call(bf16[2,208,128]{2,1,0:T(8,128)(2,1)S(1)} %pad_maximum_fusion.rows_ref.near_rows_ref, bf16[1,1024,256]{2,1,0:T(8,128)(2,1)} %get-tuple-element.24.near_turned_hbm, f32[1,1,256]{2,1,0:T(1,128)S(1)} %get-tuple-element.25.near_best_ref, f32[1,1,256]{2,1,0:T(1,128)S(1)} %get-tuple-element.26.near_own_ref, ...), custom_call_target="tpu_custom_call" | custom-call | flops 4294967296 | bytes 4194304 | tf_op jit(solution)/shard_map/peers/pallas_call | solution.py:561
  97.8 4.4 %all-to-all-start.2 = ((f32[8,4,128]{2,1,0:T(4,128)}), f32[8,4,128]{2,1,0:T(4,128)S(1)}, u32[]{:S(2)}, u32[]{:S(2)}) async-start(f32[8,4,128]{2,1,0:T(4,128)} %peers.1), calls=%async_computation.2 | async-start | bytes 32768 | tf_op jit(solution)/shard_map/all_to_all | solution.py:613
  102.2 1.0 vectors.1
  103.3 3.7 %all-to-all-done.2 = f32[8,4,128]{2,1,0:T(4,128)S(1)} async-done(((f32[8,4,128]{2,1,0:T(4,128)}), f32[8,4,128]{2,1,0:T(4,128)S(1)}, u32[]{:S(2)}, u32[]{:S(2)}) %all-to-all-start.2) | async-done | bytes 16416 | tf_op jit(solution)/shard_map/all_to_all | solution.py:613
  106.9 0.5 slice_bitcast_fusion
  (5 shorter events, 0.1 us)
Async XLA Ops:
  0.6 51.2 %copy-start = (s32[1,128]{1,0:T(1,128)S(1)}, s32[1,128]{1,0:T(1,128)}, u32[]{:S(2)}) copy-start(s32[1,128]{1,0:T(1,128)} %ids_ref.1) | copy-start | bytes 1540
  52.1 3.1 %collective-permute-start = (bf16[208,128]{1,0:T(8,128)(2,1)S(1)}, bf16[208,128]{1,0:T(8,128)(2,1)S(1)}, u32[]{:S(2)}, u32[]{:S(2)}) collective-permute-start(bf16[208,128]{1,0:T(8,128)(2,1)S(1)} %get-tuple-element.21), channel_id=1, source_target_pairs={{0,1},{1,0},{2,3},{3,2},{4,5},{5,4},{6,7},{7,6},{8,9},{9,8},{10,11... | collective-permute-start | bytes 159752 | tf_op jit(solution)/shard_map/ppermute | solution.py:598
  55.1 14.5 %collective-permute-start.3 = (bf16[2,208,128]{2,1,0:T(8,128)(2,1)S(1)}, bf16[2,208,128]{2,1,0:T(8,128)(2,1)S(1)}, u32[]{:S(2)}, u32[]{:S(2)}) collective-permute-start(bf16[2,208,128]{2,1,0:T(8,128)(2,1)S(1)} %pad_maximum_fusion.rows_ref.near_rows_ref), channel_id=1, source_target_pairs={{6,0},{7,1},{0,2},{1,3},{2,4},{3,5},{4,6},{5,7},{14,8},{15,9},{8,1... | collective-permute-start | bytes 319496 | tf_op jit(solution)/shard_map/ppermute | solution.py:602
  56.5 13.2 %collective-permute-start.2 = (bf16[2,208,128]{2,1,0:T(8,128)(2,1)S(1)}, bf16[2,208,128]{2,1,0:T(8,128)(2,1)S(1)}, u32[]{:S(2)}, u32[]{:S(2)}) collective-permute-start(bf16[2,208,128]{2,1,0:T(8,128)(2,1)S(1)} %pad_maximum_fusion.rows_ref.near_rows_ref), channel_id=1, source_target_pairs={{4,0},{5,1},{6,2},{7,3},{0,4},{1,5},{2,6},{3,7},{12,8},{13,9},{14,... | collective-permute-start | bytes 319496 | tf_op jit(solution)/shard_map/ppermute | solution.py:602
  58.9 10.7 %collective-permute-start.1 = (bf16[2,208,128]{2,1,0:T(8,128)(2,1)S(1)}, bf16[2,208,128]{2,1,0:T(8,128)(2,1)S(1)}, u32[]{:S(2)}, u32[]{:S(2)}) collective-permute-start(bf16[2,208,128]{2,1,0:T(8,128)(2,1)S(1)} %pad_maximum_fusion.rows_ref.near_rows_ref), channel_id=1, source_target_pairs={{2,0},{3,1},{4,2},{5,3},{6,4},{7,5},{0,6},{1,7},{10,8},{11,9},{12,... | collective-permute-start | bytes 319496 | tf_op jit(solution)/shard_map/ppermute | solution.py:602
  65.8 20.4 %all-to-all-start.1 = ((bf16[16,208,128]{2,1,0:T(8,128)(2,1)}), bf16[16,208,128]{2,1,0:T(8,128)(2,1)S(1)}, u32[]{:S(2)}, u32[]{:S(2)}) async-start(bf16[16,208,128]{2,1,0:T(8,128)(2,1)} %get-tuple-element.31), calls=%async_computation.1 | async-start | bytes 1703936 | tf_op jit(solution)/shard_map/all_to_all | solution.py:607
  97.8 9.1 %all-to-all-start.2 = ((f32[8,4,128]{2,1,0:T(4,128)}), f32[8,4,128]{2,1,0:T(4,128)S(1)}, u32[]{:S(2)}, u32[]{:S(2)}) async-start(f32[8,4,128]{2,1,0:T(4,128)} %peers.1), calls=%async_computation.2 | async-start | bytes 32768 | tf_op jit(solution)/shard_map/all_to_all | solution.py:613

commit v8 on v7

--- a/solution.py
+++ b/solution.py
@@ -59,13 +59,13 @@
     ]
     for copy in copies:
         copy.start()
-    for copy in early:
-        copy.wait()
     expanded = wide_ref.shape[2]
     eye = identity(expanded)
+    early[0].wait()
+    early[2].wait()
     for layer in range(2):
         expand_ref[layer] = turn(eye, wide_ref[layer]).astype(BF)
-        depth_ref[layer, :, : taps_ref.shape[1]] = turn(eye, taps_ref[layer])
+        depth_ref[layer, :, : taps_ref.shape[0]] = turn(eye, taps_ref[:, layer, :])
 
     counts = count_ref[...].astype(F32)
     line = lax.broadcasted_iota(jnp.int32, (clips, clips), 0)
@@ -219,6 +219,8 @@
 
     copies[2].wait()
     copies[3].wait()
+    early[1].wait()
+    early[3].wait()
     for copy in late:
         copy.start()
     stage(0, 0, filler(lambda pair: gather(2, pair), lambda pair: expand_stored(0, 2, pair)))
@@ -295,7 +297,7 @@
         frame_counts,
         send_list,
         expand_weight,
-        depth_kernel,
+        jnp.transpose(depth_kernel, (1, 0, 2)),
         jnp.swapaxes(reduce_weight, 1, 2),
         head_weight,
         centroids,
@@ -378,7 +380,9 @@
     return label[0:1] * 256.0 + label[1:2]
 
 
-def score_rows(rows_ref, flip_ref, panel_ref, turned_ref, near_ref, own_ref, best_ref, send_turned, arrive, extra):
+def score_rows(
+    rows_ref, flip_ref, panel_ref, turned_ref, near_ref, own_ref, best_ref, line_ref, send_turned, arrive, extra
+):
     blocks, height, clips = rows_ref.shape
     channels = flip_ref.shape[1]
     panel_rows = panel_ref.shape[0] // 8 * 8
@@ -386,8 +390,15 @@
     @pl.loop(0, blocks // 2)
     def _(pair):
         both = jnp.concatenate([rows_ref[2 * pair], rows_ref[2 * pair + 1]], axis=1)
-        projected = jnp.dot(flip_ref[...], both[:channels], preferred_element_type=F32)
-        turned_ref[pair] = unit(projected, 0)
+        parts = [slice(at, at + 256) for at in range(0, flip_ref.shape[0], 256)]
+        square = jnp.zeros((8, 2 * clips), F32)
+        for part in parts:
+            projected = jnp.dot(flip_ref[part, :], both[:channels], preferred_element_type=F32)
+            line_ref[part, :] = projected
+            square += jnp.sum((projected * projected).reshape(32, 8, 2 * clips), axis=0)
+        scale = lax.rsqrt(jnp.sum(square, axis=0, keepdims=True) + 1e-06)
+        for part in parts:
+            turned_ref[pair, part, :] = (line_ref[part, :] * scale).astype(BF)
         best_ref[pair] = jnp.dot(extra, turned_ref[pair], preferred_element_type=F32)
 
     send_turned()
@@ -414,7 +425,7 @@
 
 
 def near_kernel(
-    rows_ref, flip_ref, panel_ref, turned_hbm, near_ref, own_ref, spread_ref, extra_ref, turned_ref, best_ref, done
+    rows_ref, flip_ref, panel_ref, turned_hbm, near_ref, own_ref, spread_ref, extra_ref, turned_ref, best_ref, line_ref, done
 ):
     for peer in range(spread_ref.shape[0]):
         spread_ref[peer] = rows_ref[0]
@@ -424,13 +435,15 @@
     extra_ref[...] = extra
     copy = pltpu.make_async_copy(turned_ref, turned_hbm, done)
     score_rows(
-        rows_ref, flip_ref, panel_ref, turned_ref, near_ref, own_ref, best_ref, copy.start, lambda step: None, extra
+        rows_ref, flip_ref, panel_ref, turned_ref, near_ref, own_ref, best_ref, line_ref,
+        copy.start, lambda step: None, extra
     )
     copy.wait()
 
 
 def far_kernel(
-    rows_ref, flip_ref, stored_ref, extra_ref, turned_hbm, near_ref, own_ref, turned_ref, best_ref, done, panel_ref, arrival
+    rows_ref, flip_ref, stored_ref, extra_ref, turned_hbm, near_ref, own_ref, turned_ref, best_ref, line_ref, done,
+    panel_ref, arrival,
 ):
     copies = []
     for step in range(arrival.shape[0]):
@@ -439,7 +452,7 @@
         copies[-1].start()
     copy = pltpu.make_async_copy(turned_ref, turned_hbm, done)
     score_rows(
-        rows_ref, flip_ref, panel_ref, turned_ref, near_ref, own_ref, best_ref,
+        rows_ref, flip_ref, panel_ref, turned_ref, near_ref, own_ref, best_ref, line_ref,
         copy.start, lambda step: copies[step].wait(), extra_ref[...],
     )
     copy.wait()
@@ -460,6 +473,7 @@
     scratch = [
         pltpu.VMEM((pairs, dims, width), BF),
         pltpu.VMEM((pairs, 8, width), F32),
+        pltpu.VMEM((dims, width), F32),
         pltpu.SemaphoreType.DMA(()),
     ]
     if spread is None:
@@ -505,8 +519,7 @@
     best_ref[...] = jnp.full_like(best_ref, -1.0)
     mine_dp, mine_cent = lax.axis_index("dp"), lax.axis_index("cent")
 
-    @pl.loop(0, n_dp // GROUP)
-    def _(group):
+    def visit(group, first):
         flipped = jnp.concatenate([turn(eye, cols_ref[group * GROUP + at]) for at in range(GROUP)], axis=0)
         projected = jnp.dot(flipped[:, :channels].astype(BF), head_ref[...], preferred_element_type=F32)
         vectors = unit(projected, 1)
@@ -514,8 +527,8 @@
         wide = jnp.broadcast_to(ids, (GROUP * clips, 2 * clips))
         for block in range(n_cent // 2):
             cols = slice(block * 2 * clips, (block + 1) * 2 * clips)
-            if block < 2:
-                pl.when(group == 0)(copies[block].wait)
+            if first and block < 2:
+                copies[block].wait()
             if block == 0:
                 turned, row_ids = near_turned_ref[0], label_of(near_rows_ref, 0, channels)
             else:
@@ -531,6 +544,12 @@
             best_ref[:, cols] = jnp.maximum(
                 best_ref[:, cols], jnp.max(found.reshape(GROUP * clips // 8, 8, 2 * clips), axis=0)
             )
+
+    visit(0, True)
+
+    @pl.loop(1, n_dp // GROUP)
+    def _(group):
+        visit(group, False)
 
     best = jnp.max(best_ref[...], axis=0, keepdims=True)
     for block in range(n_cent // 2):

time: 108 us -> 104 us (0.963)
  Pallas kernels: 69.7 us -> 66.8 us
  local copies, waits for them, and re-layouts: 2.03 us -> 0.57 us
    pallas_call x1, Pallas kernels: 11.6 us -> 9.34 us  [peers_of(): pl.pallas_call(peer_kernel, out_shape=jax.ShapeDtypeStruct((n_cent, 4, cl...]
    unnamed x5 -> x4, local copies, waits for them, and re-layouts: 1.49 us -> 0.03 us
where the time goes in v8:
time: 104 us; the launch traced here: 103 us
  Pallas kernels  66.8 us (64%)
  starting transfers between devices  15.3 us (15%)
  blocking collectives  15.1 us (15%)
  waiting for transfers between devices  4.55 us (4%)
    pallas_call x1, Pallas kernels, embed(): pl.pallas_call(embed_kernel, out_shape=(jax.ShapeDtypeStruct((n_dp, clips...  34.4 us
    pallas_call x2, Pallas kernels, scored(): pl.pallas_call(kernel, out_shape=shapes, in_specs=[here, here] + ([stored...  21.9 us
    all_to_all x1, blocking collectives, local(): lax.all_to_all(pooled, 'dp', split_axis=0, concat_axis=0, tiled=True)  15.1 us
    pallas_call x1, Pallas kernels, peers_of(): pl.pallas_call(peer_kernel, out_shape=jax.ShapeDtypeStruct((n_cent, 4, cl...  9.34 us
    ppermute x3, starting transfers between devices, local(): lax.ppermute(near_rows, 'cent', [((at + 2 * chip) % n_cent, at) for at in...  4.87 us
    all_to_all x1, starting transfers between devices, local(): lax.all_to_all(partial, 'cent', split_axis=0, concat_axis=0, tiled=True)  4.42 us
    all_to_all x1, starting transfers between devices, local(): cols = lax.all_to_all(spread, 'dp', split_axis=0, concat_axis=0, tiled=True)  3.82 us
    all_to_all x1, waiting for transfers between devices, local(): lax.all_to_all(partial, 'cent', split_axis=0, concat_axis=0, tiled=True)  3.65 us
  transfers between devices with their start and end apart: 6, of which 2 were waited for; matrix products, arithmetic and copies ran while one was open for 0% of the time, Pallas kernels for 22%

profile of v8, /device:TPU:1, one launch (start us, length us, event | category | flops | bytes accessed | tf_op | source)
XLA Modules:
  0.0 103.1 jit_solution(8208482994710340681)
XLA Ops:
  0.6 0.0 copy-start
  0.6 34.4 %embed.1 = (bf16[16,8,256]{2,1,0:T(8,128)(2,1)}, bf16[6250,1024]{1,0:T(8,128)(2,1)S(1)}, bf16[192,1024]{1,0:T(8,128)(2,1)S(1)}, bf16[1024,192]{1,0:T(8,128)(2,1)S(1)}) custom-call(bf16[4,16,192,128]{3,2,1,0:T(8,128)(2,1)} %bitcast.12, s32[1,128]{1,0:T(1,128)} %counts_hbm.1, s32[1,128]{1,0:T(1,128)} %send_hbm.1, bf16[2,192,432]{2,1,0:T(8,128)(2,1)} %wide_hbm.1, ...), custom_call_target="tpu_custom_call" | custom-call | tf_op jit(solution)/shard_map/embed/pallas_call | solution.py:270
  35.0 15.1 %all_to_all.15.arrived_ref = bf16[16,8,256]{2,1,0:T(8,128)(2,1)S(1)} all-to-all(bf16[16,8,256]{2,1,0:T(8,128)(2,1)} %get-tuple-element.18), channel_id=1, replica_groups=mesh['dp'=16,'cent'=8] {'dp'}, dimensions={0} | all-to-all | bytes 131072 | tf_op jit(solution)/shard_map/all_to_all | solution.py:615
  50.1 0.0 copy-done
  50.1 0.2 own.1
  50.4 2.2 %collective-permute-start = (bf16[208,128]{1,0:T(8,128)(2,1)S(1)}, bf16[208,128]{1,0:T(8,128)(2,1)S(1)}, u32[]{:S(2)}, u32[]{:S(2)}) collective-permute-start(bf16[208,128]{1,0:T(8,128)(2,1)S(1)} %get-tuple-element.21), channel_id=1, source_target_pairs={{0,1},{1,0},{2,3},{3,2},{4,5},{5,4},{6,7},{7,6},{8,9},{9,8},{10,11... | collective-permute-start | bytes 159752 | tf_op jit(solution)/shard_map/ppermute | solution.py:617
  52.6 0.9 collective-permute-done
  53.5 1.3 %collective-permute-start.3 = (bf16[2,208,128]{2,1,0:T(8,128)(2,1)S(1)}, bf16[2,208,128]{2,1,0:T(8,128)(2,1)S(1)}, u32[]{:S(2)}, u32[]{:S(2)}) collective-permute-start(bf16[2,208,128]{2,1,0:T(8,128)(2,1)S(1)} %pad_maximum_fusion.rows_ref.near_rows_ref), channel_id=1, source_target_pairs={{6,0},{7,1},{0,2},{1,3},{2,4},{3,5},{4,6},{5,7},{14,8},{15,9},{8,1... | collective-permute-start | bytes 319496 | tf_op jit(solution)/shard_map/ppermute | solution.py:621
  54.7 2.5 %collective-permute-start.2 = (bf16[2,208,128]{2,1,0:T(8,128)(2,1)S(1)}, bf16[2,208,128]{2,1,0:T(8,128)(2,1)S(1)}, u32[]{:S(2)}, u32[]{:S(2)}) collective-permute-start(bf16[2,208,128]{2,1,0:T(8,128)(2,1)S(1)} %pad_maximum_fusion.rows_ref.near_rows_ref), channel_id=1, source_target_pairs={{4,0},{5,1},{6,2},{7,3},{0,4},{1,5},{2,6},{3,7},{12,8},{13,9},{14,... | collective-permute-start | bytes 319496 | tf_op jit(solution)/shard_map/ppermute | solution.py:621
  57.2 1.1 %collective-permute-start.1 = (bf16[2,208,128]{2,1,0:T(8,128)(2,1)S(1)}, bf16[2,208,128]{2,1,0:T(8,128)(2,1)S(1)}, u32[]{:S(2)}, u32[]{:S(2)}) collective-permute-start(bf16[2,208,128]{2,1,0:T(8,128)(2,1)S(1)} %pad_maximum_fusion.rows_ref.near_rows_ref), channel_id=1, source_target_pairs={{2,0},{3,1},{4,2},{5,3},{6,4},{7,5},{0,6},{1,7},{10,8},{11,9},{12,... | collective-permute-start | bytes 319496 | tf_op jit(solution)/shard_map/ppermute | solution.py:621
  58.3 5.6 %near.1 = (bf16[1,1024,256]{2,1,0:T(8,128)(2,1)}, f32[1,1,256]{2,1,0:T(1,128)S(1)}, f32[1,1,256]{2,1,0:T(1,128)S(1)}, bf16[16,208,128]{2,1,0:T(8,128)(2,1)}, bf16[8,1024]{1,0:T(8,128)(2,1)S(1)}) custom-call(bf16[2,208,128]{2,1,0:T(8,128)(2,1)S(1)} %pad_maximum_fusion.rows_ref.near_rows_ref, bf16[1024,192]{1,0:T(8,128)(2,1)S(1)} %get-tuple-element.22.flip_ref, ...), custom_call_target="tpu_custom_call" | custom-call | flops 3276800000 | bytes 12800000 | tf_op jit(solution)/shard_map/near/pallas_call | solution.py:488
  64.0 3.8 %all-to-all-start.1 = ((bf16[16,208,128]{2,1,0:T(8,128)(2,1)}), bf16[16,208,128]{2,1,0:T(8,128)(2,1)S(1)}, u32[]{:S(2)}, u32[]{:S(2)}) async-start(bf16[16,208,128]{2,1,0:T(8,128)(2,1)} %get-tuple-element.31), calls=%async_computation.1 | async-start | bytes 1703936 | tf_op jit(solution)/shard_map/all_to_all | solution.py:626
  67.8 0.0 collective-permute-done.1
  67.8 0.0 collective-permute-done.2
  67.9 0.0 collective-permute-done.3
  67.9 16.2 %far.1 = (bf16[3,1024,256]{2,1,0:T(8,128)(2,1)}, f32[3,1,256]{2,1,0:T(1,128)S(1)}, f32[3,1,256]{2,1,0:T(1,128)S(1)}) custom-call(bf16[6,208,128]{2,1,0:T(8,128)(2,1)S(1)} %constant_dynamic-update-slice_fusion.rows_ref.far_rows_ref, bf16[1024,192]{1,0:T(8,128)(2,1)S(1)} %get-tuple-element.22.flip_ref, bf16[6250,1024]{1,0:T(8,128)(2,1)} %stored_ref.1, ...), custom_call_target="tpu_custom_call" | custom-call | flops 9830400000 | bytes 12800000 | tf_op jit(solution)/shard_map/far/pallas_call | solution.py:488
  84.1 0.0 all-to-all-done.1.cols_ref
  84.1 9.3 %peers.1 = f32[8,4,128]{2,1,0:T(4,128)} custom-call(bf16[2,208,128]{2,1,0:T(8,128)(2,1)S(1)} %pad_maximum_fusion.rows_ref.near_rows_ref, bf16[1,1024,256]{2,1,0:T(8,128)(2,1)} %get-tuple-element.24.near_turned_hbm, f32[1,1,256]{2,1,0:T(1,128)S(1)} %get-tuple-element.25.near_best_ref, f32[1,1,256]{2,1,0:T(1,128)S(1)} %get-tuple-element.26.near_own_ref, ...), custom_call_target="tpu_custom_call" | custom-call | flops 4294967296 | bytes 4194304 | tf_op jit(solution)/shard_map/peers/pallas_call | solution.py:580
  93.5 4.4 %all-to-all-start.2 = ((f32[8,4,128]{2,1,0:T(4,128)}), f32[8,4,128]{2,1,0:T(4,128)S(1)}, u32[]{:S(2)}, u32[]{:S(2)}) async-start(f32[8,4,128]{2,1,0:T(4,128)} %peers.1), calls=%async_computation.2 | async-start | bytes 32768 | tf_op jit(solution)/shard_map/all_to_all | solution.py:632
  97.9 1.0 vectors.1
  98.9 3.7 %all-to-all-done.2 = f32[8,4,128]{2,1,0:T(4,128)S(1)} async-done(((f32[8,4,128]{2,1,0:T(4,128)}), f32[8,4,128]{2,1,0:T(4,128)S(1)}, u32[]{:S(2)}, u32[]{:S(2)}) %all-to-all-start.2) | async-done | bytes 16416 | tf_op jit(solution)/shard_map/all_to_all | solution.py:632
  102.6 0.5 slice_bitcast_fusion
  (5 shorter events, 0.1 us)
Async XLA Ops:
  0.6 49.5 %copy-start = (s32[1,128]{1,0:T(1,128)S(1)}, s32[1,128]{1,0:T(1,128)}, u32[]{:S(2)}) copy-start(s32[1,128]{1,0:T(1,128)} %ids_ref.1) | copy-start | bytes 1540
  50.4 3.1 %collective-permute-start = (bf16[208,128]{1,0:T(8,128)(2,1)S(1)}, bf16[208,128]{1,0:T(8,128)(2,1)S(1)}, u32[]{:S(2)}, u32[]{:S(2)}) collective-permute-start(bf16[208,128]{1,0:T(8,128)(2,1)S(1)} %get-tuple-element.21), channel_id=1, source_target_pairs={{0,1},{1,0},{2,3},{3,2},{4,5},{5,4},{6,7},{7,6},{8,9},{9,8},{10,11... | collective-permute-start | bytes 159752 | tf_op jit(solution)/shard_map/ppermute | solution.py:617
  53.5 14.4 %collective-permute-start.3 = (bf16[2,208,128]{2,1,0:T(8,128)(2,1)S(1)}, bf16[2,208,128]{2,1,0:T(8,128)(2,1)S(1)}, u32[]{:S(2)}, u32[]{:S(2)}) collective-permute-start(bf16[2,208,128]{2,1,0:T(8,128)(2,1)S(1)} %pad_maximum_fusion.rows_ref.near_rows_ref), channel_id=1, source_target_pairs={{6,0},{7,1},{0,2},{1,3},{2,4},{3,5},{4,6},{5,7},{14,8},{15,9},{8,1... | collective-permute-start | bytes 319496 | tf_op jit(solution)/shard_map/ppermute | solution.py:621
  54.7 13.1 %collective-permute-start.2 = (bf16[2,208,128]{2,1,0:T(8,128)(2,1)S(1)}, bf16[2,208,128]{2,1,0:T(8,128)(2,1)S(1)}, u32[]{:S(2)}, u32[]{:S(2)}) collective-permute-start(bf16[2,208,128]{2,1,0:T(8,128)(2,1)S(1)} %pad_maximum_fusion.rows_ref.near_rows_ref), channel_id=1, source_target_pairs={{4,0},{5,1},{6,2},{7,3},{0,4},{1,5},{2,6},{3,7},{12,8},{13,9},{14,... | collective-permute-start | bytes 319496 | tf_op jit(solution)/shard_map/ppermute | solution.py:621
  57.2 10.6 %collective-permute-start.1 = (bf16[2,208,128]{2,1,0:T(8,128)(2,1)S(1)}, bf16[2,208,128]{2,1,0:T(8,128)(2,1)S(1)}, u32[]{:S(2)}, u32[]{:S(2)}) collective-permute-start(bf16[2,208,128]{2,1,0:T(8,128)(2,1)S(1)} %pad_maximum_fusion.rows_ref.near_rows_ref), channel_id=1, source_target_pairs={{2,0},{3,1},{4,2},{5,3},{6,4},{7,5},{0,6},{1,7},{10,8},{11,9},{12,... | collective-permute-start | bytes 319496 | tf_op jit(solution)/shard_map/ppermute | solution.py:621
  64.0 20.2 %all-to-all-start.1 = ((bf16[16,208,128]{2,1,0:T(8,128)(2,1)}), bf16[16,208,128]{2,1,0:T(8,128)(2,1)S(1)}, u32[]{:S(2)}, u32[]{:S(2)}) async-start(bf16[16,208,128]{2,1,0:T(8,128)(2,1)} %get-tuple-element.31), calls=%async_computation.1 | async-start | bytes 1703936 | tf_op jit(solution)/shard_map/all_to_all | solution.py:626
  93.5 9.1 %all-to-all-start.2 = ((f32[8,4,128]{2,1,0:T(4,128)}), f32[8,4,128]{2,1,0:T(4,128)S(1)}, u32[]{:S(2)}, u32[]{:S(2)}) async-start(f32[8,4,128]{2,1,0:T(4,128)} %peers.1), calls=%async_computation.2 | async-start | bytes 32768 | tf_op jit(solution)/shard_map/all_to_all | solution.py:632

commit v9 on v8

--- a/solution.py
+++ b/solution.py
@@ -80,9 +80,15 @@
     blocks = expanded // 16 // STEPS
     one_hot = lambda mask: mask.astype(F32).astype(BF)
     order = one_hot(rank == lane)
+    none = jnp.zeros((clips, clips), BF)
     place = [
-        order,
-        one_hot((rank == lane) & (count_line > 1)),
+        jnp.concatenate(
+            [
+                jnp.concatenate([order, none], axis=1),
+                jnp.concatenate([none, one_hot((rank == lane) & (count_line > 1))], axis=1),
+            ],
+            axis=0,
+        ),
         jnp.concatenate(
             [
                 one_hot((rank == lane) & (count_line > 2)),
@@ -101,20 +107,19 @@
         hidden_refs[3 * layer + tile][2 * pair] = hidden[:, :clips]
         hidden_refs[3 * layer + tile][2 * pair + 1] = hidden[:, clips:]
 
-    def gather(tile, pair):
-        if tile < 2:
-            spots = jnp.concatenate([clip_ref[tile, 2 * pair], clip_ref[tile, 2 * pair + 1]], axis=0)
-        else:
-            spots = jnp.concatenate(
-                [
-                    jnp.concatenate([clip_ref[2, 2 * pair + side], clip_ref[3, 2 * pair + side]], axis=1)
-                    for side in range(2)
-                ],
-                axis=0,
-            )
-        x = jnp.dot(spots, place[tile], preferred_element_type=F32).astype(BF)
-        x_refs[tile][2 * pair] = x[:channels]
-        x_refs[tile][2 * pair + 1] = x[channels:]
+    def gather(first, pair):
+        spots = jnp.concatenate(
+            [
+                jnp.concatenate([clip_ref[first, 2 * pair + side], clip_ref[first + 1, 2 * pair + side]], axis=1)
+                for side in range(2)
+            ],
+            axis=0,
+        )
+        x = jnp.dot(spots, place[first // 2], preferred_element_type=F32).astype(BF)
+        for side in range(2):
+            rows = slice(side * channels, (side + 1) * channels)
+            for at in range(x.shape[1] // clips):
+                x_refs[first + at][2 * pair + side] = x[rows, at * clips : (at + 1) * clips]
 
     def expand_stored(layer, tile, pair):
         x_ref = x_refs[3 * layer + tile]
@@ -214,7 +219,7 @@
         before = jnp.maximum(step - 1, 0)
         for tile in range(2):
             expand_stored(0, tile, before)
-            gather(tile, pair)
+        gather(0, pair)
         spread_taps(0, step, 9, 27)
 
     copies[2].wait()
@@ -425,10 +430,15 @@
 
 
 def near_kernel(
-    rows_ref, flip_ref, panel_ref, turned_hbm, near_ref, own_ref, spread_ref, extra_ref, turned_ref, best_ref, line_ref, done
+    rows_ref, flip_ref, panel_ref, turned_hbm, near_ref, own_ref, spread_hbm, extra_ref, turned_ref, best_ref, line_ref, done,
+    spread_done,
 ):
-    for peer in range(spread_ref.shape[0]):
-        spread_ref[peer] = rows_ref[0]
+    sends = [
+        pltpu.make_async_copy(rows_ref.at[0], spread_hbm.at[peer], spread_done.at[peer])
+        for peer in range(spread_hbm.shape[0])
+    ]
+    for send in sends:
+        send.start()
     panel_rows = panel_ref.shape[0]
     left = panel_ref[panel_rows - LEFT : panel_rows, :]
     extra = jnp.concatenate([left] * (8 // LEFT), axis=0)
@@ -438,6 +448,8 @@
         rows_ref, flip_ref, panel_ref, turned_ref, near_ref, own_ref, best_ref, line_ref,
         copy.start, lambda step: None, extra
     )
+    for send in sends:
+        send.wait()
     copy.wait()
 
 
@@ -483,13 +495,14 @@
         ]
     else:
         assert panel_rows % 8 == LEFT
-        shapes.append(jax.ShapeDtypeStruct((spread, height, clips), BF))
+        scratch.append(pltpu.SemaphoreType.DMA((spread,)))
+        shapes.append(pltpu.HBM((spread, height, clips), BF))
         shapes.append(jax.ShapeDtypeStruct((8, dims), BF))
     return pl.pallas_call(
         kernel,
         out_shape=shapes,
         in_specs=[here, here] + ([stored, here] if spread is None else [here]),
-        out_specs=[stored] + [here] * (len(shapes) - 1),
+        out_specs=[stored, here, here] + ([] if spread is None else [stored, here]),
         scratch_shapes=scratch,
         compiler_params=pltpu.CompilerParams(vmem_limit_bytes=limit << 20),
         cost_estimate=pl.CostEstimate(
@@ -503,15 +516,11 @@
 
 
 def peer_kernel(
-    near_rows_ref, near_turned_hbm, near_best_ref, near_own_ref, far_rows_ref, far_turned_hbm, far_best_ref, far_own_ref,
-    cols_ref, head_ref, out_ref, near_turned_ref, far_turned_ref, best_ref, arrival,
+    near_rows_ref, near_turned_ref, near_best_ref, near_own_ref, far_rows_ref, far_turned_hbm, far_best_ref, far_own_ref,
+    cols_ref, head_ref, out_ref, far_turned_ref, best_ref, arrival,
 ):
-    copies = [
-        pltpu.make_async_copy(near_turned_hbm, near_turned_ref, arrival.at[0]),
-        pltpu.make_async_copy(far_turned_hbm, far_turned_ref, arrival.at[1]),
-    ]
-    for copy in copies:
-        copy.start()
+    far_copy = pltpu.make_async_copy(far_turned_hbm, far_turned_ref, arrival)
+    far_copy.start()
     n_dp, height, clips = cols_ref.shape
     n_cent = out_ref.shape[0]
     channels = head_ref.shape[0]
@@ -527,8 +536,8 @@
         wide = jnp.broadcast_to(ids, (GROUP * clips, 2 * clips))
         for block in range(n_cent // 2):
             cols = slice(block * 2 * clips, (block + 1) * 2 * clips)
-            if first and block < 2:
-                copies[block].wait()
+            if first and block == 1:
+                far_copy.wait()
             if block == 0:
                 turned, row_ids = near_turned_ref[0], label_of(near_rows_ref, 0, channels)
             else:
@@ -574,19 +583,16 @@
     dims = head_weight.shape[1]
     here = pl.BlockSpec(memory_space=pltpu.VMEM)
     stored = pl.BlockSpec(memory_space=pltpu.HBM)
-    near_found, far_found = [
-        [pltpu.with_memory_space_constraint(found[0], pltpu.HBM), *found[1:]] for found in (near_found, far_found)
-    ]
+    far_found = [pltpu.with_memory_space_constraint(far_found[0], pltpu.HBM), *far_found[1:]]
     return pl.pallas_call(
         peer_kernel,
         out_shape=jax.ShapeDtypeStruct((n_cent, 4, clips), F32),
-        in_specs=[here, stored, here, here] * 2 + [here] * 2,
+        in_specs=[here] * 5 + [stored] + [here] * 4,
         out_specs=here,
         scratch_shapes=[
-            pltpu.VMEM(near_found[0].shape, BF),
             pltpu.VMEM(far_found[0].shape, BF),
             pltpu.VMEM((8, n_cent * clips), F32),
-            pltpu.SemaphoreType.DMA((2,)),
+            pltpu.SemaphoreType.DMA(()),
         ],
         compiler_params=pltpu.CompilerParams(vmem_limit_bytes=16 << 20),
         cost_estimate=pl.CostEstimate(

time: 104 us -> 103 us (level)
  no operation moved by 1% of the time
where the time goes in v9:
time: 103 us; the launch traced here: 102 us
  Pallas kernels  66 us (64%)
  starting transfers between devices  15.3 us (15%)
  blocking collectives  15.1 us (15%)
  waiting for transfers between devices  4.55 us (4%)
    pallas_call x1, Pallas kernels, embed(): pl.pallas_call(embed_kernel, out_shape=(jax.ShapeDtypeStruct((n_dp, clips...  34.8 us
    pallas_call x2, Pallas kernels, scored(): pl.pallas_call(kernel, out_shape=shapes, in_specs=[here, here] + ([stored...  21.1 us
    all_to_all x1, blocking collectives, local(): lax.all_to_all(pooled, 'dp', split_axis=0, concat_axis=0, tiled=True)  15.1 us
    pallas_call x1, Pallas kernels, peers_of(): pl.pallas_call(peer_kernel, out_shape=jax.ShapeDtypeStruct((n_cent, 4, cl...  8.8 us
    ppermute x3, starting transfers between devices, local(): lax.ppermute(near_rows, 'cent', [((at + 2 * chip) % n_cent, at) for at in...  4.91 us
    all_to_all x1, starting transfers between devices, local(): lax.all_to_all(partial, 'cent', split_axis=0, concat_axis=0, tiled=True)  4.39 us
    all_to_all x1, starting transfers between devices, local(): cols = lax.all_to_all(spread, 'dp', split_axis=0, concat_axis=0, tiled=True)  3.82 us
    all_to_all x1, waiting for transfers between devices, local(): lax.all_to_all(partial, 'cent', split_axis=0, concat_axis=0, tiled=True)  3.65 us
  transfers between devices with their start and end apart: 6, of which 2 were waited for; matrix products, arithmetic and copies ran while one was open for 0% of the time, Pallas kernels for 22%

profile of v9, /device:TPU:1, one launch (start us, length us, event | category | flops | bytes accessed | tf_op | source)
XLA Modules:
  0.0 102.3 jit_solution(15129278370203902385)
XLA Ops:
  0.6 0.0 copy-start
  0.6 34.8 %embed.1 = (bf16[16,8,256]{2,1,0:T(8,128)(2,1)}, bf16[6250,1024]{1,0:T(8,128)(2,1)S(1)}, bf16[192,1024]{1,0:T(8,128)(2,1)S(1)}, bf16[1024,192]{1,0:T(8,128)(2,1)S(1)}) custom-call(bf16[4,16,192,128]{3,2,1,0:T(8,128)(2,1)} %bitcast.12, s32[1,128]{1,0:T(1,128)} %counts_hbm.1, s32[1,128]{1,0:T(1,128)} %send_hbm.1, bf16[2,192,432]{2,1,0:T(8,128)(2,1)} %wide_hbm.1, ...), custom_call_target="tpu_custom_call" | custom-call | tf_op jit(solution)/shard_map/embed/pallas_call | solution.py:275
  35.5 15.1 %all_to_all.15.arrived_ref = bf16[16,8,256]{2,1,0:T(8,128)(2,1)S(1)} all-to-all(bf16[16,8,256]{2,1,0:T(8,128)(2,1)} %get-tuple-element.18), channel_id=1, replica_groups=mesh['dp'=16,'cent'=8] {'dp'}, dimensions={0} | all-to-all | bytes 131072 | tf_op jit(solution)/shard_map/all_to_all | solution.py:621
  50.6 0.0 copy-done
  50.6 0.2 own.1
  50.8 2.2 %collective-permute-start = (bf16[208,128]{1,0:T(8,128)(2,1)S(1)}, bf16[208,128]{1,0:T(8,128)(2,1)S(1)}, u32[]{:S(2)}, u32[]{:S(2)}) collective-permute-start(bf16[208,128]{1,0:T(8,128)(2,1)S(1)} %get-tuple-element.21), channel_id=1, source_target_pairs={{0,1},{1,0},{2,3},{3,2},{4,5},{5,4},{6,7},{7,6},{8,9},{9,8},{10,11... | collective-permute-start | bytes 159752 | tf_op jit(solution)/shard_map/ppermute | solution.py:623
  53.0 0.9 collective-permute-done
  53.9 1.3 %collective-permute-start.3 = (bf16[2,208,128]{2,1,0:T(8,128)(2,1)S(1)}, bf16[2,208,128]{2,1,0:T(8,128)(2,1)S(1)}, u32[]{:S(2)}, u32[]{:S(2)}) collective-permute-start(bf16[2,208,128]{2,1,0:T(8,128)(2,1)S(1)} %pad_maximum_fusion.rows_ref.near_rows_ref), channel_id=1, source_target_pairs={{6,0},{7,1},{0,2},{1,3},{2,4},{3,5},{4,6},{5,7},{14,8},{15,9},{8,1... | collective-permute-start | bytes 319496 | tf_op jit(solution)/shard_map/ppermute | solution.py:627
  55.2 2.4 %collective-permute-start.2 = (bf16[2,208,128]{2,1,0:T(8,128)(2,1)S(1)}, bf16[2,208,128]{2,1,0:T(8,128)(2,1)S(1)}, u32[]{:S(2)}, u32[]{:S(2)}) collective-permute-start(bf16[2,208,128]{2,1,0:T(8,128)(2,1)S(1)} %pad_maximum_fusion.rows_ref.near_rows_ref), channel_id=1, source_target_pairs={{4,0},{5,1},{6,2},{7,3},{0,4},{1,5},{2,6},{3,7},{12,8},{13,9},{14,... | collective-permute-start | bytes 319496 | tf_op jit(solution)/shard_map/ppermute | solution.py:627
  57.6 1.2 %collective-permute-start.1 = (bf16[2,208,128]{2,1,0:T(8,128)(2,1)S(1)}, bf16[2,208,128]{2,1,0:T(8,128)(2,1)S(1)}, u32[]{:S(2)}, u32[]{:S(2)}) collective-permute-start(bf16[2,208,128]{2,1,0:T(8,128)(2,1)S(1)} %pad_maximum_fusion.rows_ref.near_rows_ref), channel_id=1, source_target_pairs={{2,0},{3,1},{4,2},{5,3},{6,4},{7,5},{0,6},{1,7},{10,8},{11,9},{12,... | collective-permute-start | bytes 319496 | tf_op jit(solution)/shard_map/ppermute | solution.py:627
  58.8 4.8 %near.1 = (bf16[1,1024,256]{2,1,0:T(8,128)(2,1)}, f32[1,1,256]{2,1,0:T(1,128)S(1)}, f32[1,1,256]{2,1,0:T(1,128)S(1)}, bf16[16,208,128]{2,1,0:T(8,128)(2,1)}, bf16[8,1024]{1,0:T(8,128)(2,1)S(1)}) custom-call(bf16[2,208,128]{2,1,0:T(8,128)(2,1)S(1)} %pad_maximum_fusion.rows_ref.near_rows_ref, bf16[1024,192]{1,0:T(8,128)(2,1)S(1)} %get-tuple-element.22.flip_ref, ...), custom_call_target="tpu_custom_call" | custom-call | flops 3276800000 | bytes 12800000 | tf_op jit(solution)/shard_map/near/pallas_call | solution.py:501
  63.6 3.8 %all-to-all-start.1 = ((bf16[16,208,128]{2,1,0:T(8,128)(2,1)}), bf16[16,208,128]{2,1,0:T(8,128)(2,1)S(1)}, u32[]{:S(2)}, u32[]{:S(2)}) async-start(bf16[16,208,128]{2,1,0:T(8,128)(2,1)} %get-tuple-element.31), calls=%async_computation.1 | async-start | bytes 1703936 | tf_op jit(solution)/shard_map/all_to_all | solution.py:632
  67.5 0.0 collective-permute-done.1
  67.5 0.0 collective-permute-done.2
  67.5 0.0 collective-permute-done.3
  67.6 0.0 copy-start.1
  67.6 16.3 %far.1 = (bf16[3,1024,256]{2,1,0:T(8,128)(2,1)}, f32[3,1,256]{2,1,0:T(1,128)S(1)}, f32[3,1,256]{2,1,0:T(1,128)S(1)}) custom-call(bf16[6,208,128]{2,1,0:T(8,128)(2,1)S(1)} %constant_dynamic-update-slice_fusion.rows_ref.far_rows_ref, bf16[1024,192]{1,0:T(8,128)(2,1)S(1)} %get-tuple-element.22.flip_ref, bf16[6250,1024]{1,0:T(8,128)(2,1)} %stored_ref.1, ...), custom_call_target="tpu_custom_call" | custom-call | flops 9830400000 | bytes 12800000 | tf_op jit(solution)/shard_map/far/pallas_call | solution.py:501
  83.9 0.0 all-to-all-done.1.cols_ref
  83.9 0.0 copy-done.1
  83.9 8.8 %peers.1 = f32[8,4,128]{2,1,0:T(4,128)} custom-call(bf16[2,208,128]{2,1,0:T(8,128)(2,1)S(1)} %pad_maximum_fusion.rows_ref.near_rows_ref, bf16[1,1024,256]{2,1,0:T(8,128)(2,1)S(1)} %copy-done.1, f32[1,1,256]{2,1,0:T(1,128)S(1)} %get-tuple-element.25.near_best_ref, f32[1,1,256]{2,1,0:T(1,128)S(1)} %get-tuple-element.26.near_own_ref, ...), custom_call_target="tpu_custom_call" | custom-call | flops 4294967296 | bytes 4194304 | tf_op jit(solution)/shard_map/peers/pallas_call | solution.py:587
  92.7 4.4 %all-to-all-start.2 = ((f32[8,4,128]{2,1,0:T(4,128)}), f32[8,4,128]{2,1,0:T(4,128)S(1)}, u32[]{:S(2)}, u32[]{:S(2)}) async-start(f32[8,4,128]{2,1,0:T(4,128)} %peers.1), calls=%async_computation.2 | async-start | bytes 32768 | tf_op jit(solution)/shard_map/all_to_all | solution.py:638
  97.1 1.0 vectors.1
  98.1 3.7 %all-to-all-done.2 = f32[8,4,128]{2,1,0:T(4,128)S(1)} async-done(((f32[8,4,128]{2,1,0:T(4,128)}), f32[8,4,128]{2,1,0:T(4,128)S(1)}, u32[]{:S(2)}, u32[]{:S(2)}) %all-to-all-start.2) | async-done | bytes 16416 | tf_op jit(solution)/shard_map/all_to_all | solution.py:638
  101.8 0.5 slice_bitcast_fusion
  (5 shorter events, 0.1 us)
Async XLA Ops:
  0.6 50.0 %copy-start = (s32[1,128]{1,0:T(1,128)S(1)}, s32[1,128]{1,0:T(1,128)}, u32[]{:S(2)}) copy-start(s32[1,128]{1,0:T(1,128)} %ids_ref.1) | copy-start | bytes 1540
  50.8 3.1 %collective-permute-start = (bf16[208,128]{1,0:T(8,128)(2,1)S(1)}, bf16[208,128]{1,0:T(8,128)(2,1)S(1)}, u32[]{:S(2)}, u32[]{:S(2)}) collective-permute-start(bf16[208,128]{1,0:T(8,128)(2,1)S(1)} %get-tuple-element.21), channel_id=1, source_target_pairs={{0,1},{1,0},{2,3},{3,2},{4,5},{5,4},{6,7},{7,6},{8,9},{9,8},{10,11... | collective-permute-start | bytes 159752 | tf_op jit(solution)/shard_map/ppermute | solution.py:623
  53.9 13.6 %collective-permute-start.3 = (bf16[2,208,128]{2,1,0:T(8,128)(2,1)S(1)}, bf16[2,208,128]{2,1,0:T(8,128)(2,1)S(1)}, u32[]{:S(2)}, u32[]{:S(2)}) collective-permute-start(bf16[2,208,128]{2,1,0:T(8,128)(2,1)S(1)} %pad_maximum_fusion.rows_ref.near_rows_ref), channel_id=1, source_target_pairs={{6,0},{7,1},{0,2},{1,3},{2,4},{3,5},{4,6},{5,7},{14,8},{15,9},{8,1... | collective-permute-start | bytes 319496 | tf_op jit(solution)/shard_map/ppermute | solution.py:627
  55.2 12.3 %collective-permute-start.2 = (bf16[2,208,128]{2,1,0:T(8,128)(2,1)S(1)}, bf16[2,208,128]{2,1,0:T(8,128)(2,1)S(1)}, u32[]{:S(2)}, u32[]{:S(2)}) collective-permute-start(bf16[2,208,128]{2,1,0:T(8,128)(2,1)S(1)} %pad_maximum_fusion.rows_ref.near_rows_ref), channel_id=1, source_target_pairs={{4,0},{5,1},{6,2},{7,3},{0,4},{1,5},{2,6},{3,7},{12,8},{13,9},{14,... | collective-permute-start | bytes 319496 | tf_op jit(solution)/shard_map/ppermute | solution.py:627
  57.6 9.8 %collective-permute-start.1 = (bf16[2,208,128]{2,1,0:T(8,128)(2,1)S(1)}, bf16[2,208,128]{2,1,0:T(8,128)(2,1)S(1)}, u32[]{:S(2)}, u32[]{:S(2)}) collective-permute-start(bf16[2,208,128]{2,1,0:T(8,128)(2,1)S(1)} %pad_maximum_fusion.rows_ref.near_rows_ref), channel_id=1, source_target_pairs={{2,0},{3,1},{4,2},{5,3},{6,4},{7,5},{0,6},{1,7},{10,8},{11,9},{12,... | collective-permute-start | bytes 319496 | tf_op jit(solution)/shard_map/ppermute | solution.py:627
  63.6 20.2 %all-to-all-start.1 = ((bf16[16,208,128]{2,1,0:T(8,128)(2,1)}), bf16[16,208,128]{2,1,0:T(8,128)(2,1)S(1)}, u32[]{:S(2)}, u32[]{:S(2)}) async-start(bf16[16,208,128]{2,1,0:T(8,128)(2,1)} %get-tuple-element.31), calls=%async_computation.1 | async-start | bytes 1703936 | tf_op jit(solution)/shard_map/all_to_all | solution.py:632
  67.6 16.3 %copy-start.1 = (bf16[1,1024,256]{2,1,0:T(8,128)(2,1)S(1)}, bf16[1,1024,256]{2,1,0:T(8,128)(2,1)}, u32[]{:S(2)}) copy-start(bf16[1,1024,256]{2,1,0:T(8,128)(2,1)} %get-tuple-element.24.near_turned_ref) | copy-start | bytes 1572868
  92.7 9.1 %all-to-all-start.2 = ((f32[8,4,128]{2,1,0:T(4,128)}), f32[8,4,128]{2,1,0:T(4,128)S(1)}, u32[]{:S(2)}, u32[]{:S(2)}) async-start(f32[8,4,128]{2,1,0:T(4,128)} %peers.1), calls=%async_computation.2 | async-start | bytes 32768 | tf_op jit(solution)/shard_map/all_to_all | solution.py:638

commit v10 on v9

--- a/solution.py
+++ b/solution.py
@@ -51,14 +51,14 @@
         pltpu.make_async_copy(source, target, ready.at[4 + at])
         for at, (source, target) in enumerate([(head_hbm, head_ref), (panel_hbm, panel_ref)])
     ]
-    for copy in early:
-        copy.start()
+    early[0].start()
+    early[2].start()
     copies = [
         pltpu.make_async_copy(stored_ref.at[frame], clip_ref.at[frame], arrival.at[frame])
         for frame in range(clip_ref.shape[0])
     ]
-    for copy in copies:
-        copy.start()
+    copies[0].start()
+    copies[1].start()
     expanded = wide_ref.shape[2]
     eye = identity(expanded)
     early[0].wait()
@@ -212,6 +212,8 @@
     packed_pool_ref[...] = jnp.zeros_like(packed_pool_ref)
     copies[0].wait()
     copies[1].wait()
+    for copy in (copies[2], copies[3], early[1], early[3]):
+        copy.start()
 
     @pl.loop(0, STEPS)
     def _(step):

time: 103 us -> 103 us (level)
  no operation moved by 1% of the time
where the time goes in v10:
time: 103 us; the launch traced here: 102 us
  Pallas kernels  65.9 us (64%)
  starting transfers between devices  15.4 us (15%)
  blocking collectives  15 us (15%)
  waiting for transfers between devices  4.55 us (4%)
    pallas_call x1, Pallas kernels, embed(): pl.pallas_call(embed_kernel, out_shape=(jax.ShapeDtypeStruct((n_dp, clips...  34.7 us
    pallas_call x2, Pallas kernels, scored(): pl.pallas_call(kernel, out_shape=shapes, in_specs=[here, here] + ([stored...  21.1 us
    all_to_all x1, blocking collectives, local(): lax.all_to_all(pooled, 'dp', split_axis=0, concat_axis=0, tiled=True)  15 us
    pallas_call x1, Pallas kernels, peers_of(): pl.pallas_call(peer_kernel, out_shape=jax.ShapeDtypeStruct((n_cent, 4, cl...  8.8 us
    ppermute x3, starting transfers between devices, local(): lax.ppermute(near_rows, 'cent', [((at + 2 * chip) % n_cent, at) for at in...  4.96 us
    all_to_all x1, starting transfers between devices, local(): lax.all_to_all(partial, 'cent', split_axis=0, concat_axis=0, tiled=True)  4.39 us
    all_to_all x1, starting transfers between devices, local(): cols = lax.all_to_all(spread, 'dp', split_axis=0, concat_axis=0, tiled=True)  3.82 us
    all_to_all x1, waiting for transfers between devices, local(): lax.all_to_all(partial, 'cent', split_axis=0, concat_axis=0, tiled=True)  3.65 us
  transfers between devices with their start and end apart: 6, of which 2 were waited for; matrix products, arithmetic and copies ran while one was open for 0% of the time, Pallas kernels for 22%

profile of v10, /device:TPU:1, one launch (start us, length us, event | category | flops | bytes accessed | tf_op | source)
XLA Modules:
  0.0 102.2 jit_solution(7064547915349632788)
XLA Ops:
  0.6 0.0 copy-start
  0.6 34.7 %embed.1 = (bf16[16,8,256]{2,1,0:T(8,128)(2,1)}, bf16[6250,1024]{1,0:T(8,128)(2,1)S(1)}, bf16[192,1024]{1,0:T(8,128)(2,1)S(1)}, bf16[1024,192]{1,0:T(8,128)(2,1)S(1)}) custom-call(bf16[4,16,192,128]{3,2,1,0:T(8,128)(2,1)} %bitcast.12, s32[1,128]{1,0:T(1,128)} %counts_hbm.1, s32[1,128]{1,0:T(1,128)} %send_hbm.1, bf16[2,192,432]{2,1,0:T(8,128)(2,1)} %wide_hbm.1, ...), custom_call_target="tpu_custom_call" | custom-call | tf_op jit(solution)/shard_map/embed/pallas_call | solution.py:277
  35.4 15.0 %all_to_all.15.arrived_ref = bf16[16,8,256]{2,1,0:T(8,128)(2,1)S(1)} all-to-all(bf16[16,8,256]{2,1,0:T(8,128)(2,1)} %get-tuple-element.18), channel_id=1, replica_groups=mesh['dp'=16,'cent'=8] {'dp'}, dimensions={0} | all-to-all | bytes 131072 | tf_op jit(solution)/shard_map/all_to_all | solution.py:623
  50.4 0.0 copy-done
  50.4 0.2 own.1
  50.6 2.2 %collective-permute-start = (bf16[208,128]{1,0:T(8,128)(2,1)S(1)}, bf16[208,128]{1,0:T(8,128)(2,1)S(1)}, u32[]{:S(2)}, u32[]{:S(2)}) collective-permute-start(bf16[208,128]{1,0:T(8,128)(2,1)S(1)} %get-tuple-element.21), channel_id=1, source_target_pairs={{0,1},{1,0},{2,3},{3,2},{4,5},{5,4},{6,7},{7,6},{8,9},{9,8},{10,11... | collective-permute-start | bytes 159752 | tf_op jit(solution)/shard_map/ppermute | solution.py:625
  52.8 0.9 collective-permute-done
  53.7 1.3 %collective-permute-start.3 = (bf16[2,208,128]{2,1,0:T(8,128)(2,1)S(1)}, bf16[2,208,128]{2,1,0:T(8,128)(2,1)S(1)}, u32[]{:S(2)}, u32[]{:S(2)}) collective-permute-start(bf16[2,208,128]{2,1,0:T(8,128)(2,1)S(1)} %pad_maximum_fusion.rows_ref.near_rows_ref), channel_id=1, source_target_pairs={{6,0},{7,1},{0,2},{1,3},{2,4},{3,5},{4,6},{5,7},{14,8},{15,9},{8,1... | collective-permute-start | bytes 319496 | tf_op jit(solution)/shard_map/ppermute | solution.py:629
  55.1 2.4 %collective-permute-start.2 = (bf16[2,208,128]{2,1,0:T(8,128)(2,1)S(1)}, bf16[2,208,128]{2,1,0:T(8,128)(2,1)S(1)}, u32[]{:S(2)}, u32[]{:S(2)}) collective-permute-start(bf16[2,208,128]{2,1,0:T(8,128)(2,1)S(1)} %pad_maximum_fusion.rows_ref.near_rows_ref), channel_id=1, source_target_pairs={{4,0},{5,1},{6,2},{7,3},{0,4},{1,5},{2,6},{3,7},{12,8},{13,9},{14,... | collective-permute-start | bytes 319496 | tf_op jit(solution)/shard_map/ppermute | solution.py:629
  57.5 1.2 %collective-permute-start.1 = (bf16[2,208,128]{2,1,0:T(8,128)(2,1)S(1)}, bf16[2,208,128]{2,1,0:T(8,128)(2,1)S(1)}, u32[]{:S(2)}, u32[]{:S(2)}) collective-permute-start(bf16[2,208,128]{2,1,0:T(8,128)(2,1)S(1)} %pad_maximum_fusion.rows_ref.near_rows_ref), channel_id=1, source_target_pairs={{2,0},{3,1},{4,2},{5,3},{6,4},{7,5},{0,6},{1,7},{10,8},{11,9},{12,... | collective-permute-start | bytes 319496 | tf_op jit(solution)/shard_map/ppermute | solution.py:629
  58.7 4.8 %near.1 = (bf16[1,1024,256]{2,1,0:T(8,128)(2,1)}, f32[1,1,256]{2,1,0:T(1,128)S(1)}, f32[1,1,256]{2,1,0:T(1,128)S(1)}, bf16[16,208,128]{2,1,0:T(8,128)(2,1)}, bf16[8,1024]{1,0:T(8,128)(2,1)S(1)}) custom-call(bf16[2,208,128]{2,1,0:T(8,128)(2,1)S(1)} %pad_maximum_fusion.rows_ref.near_rows_ref, bf16[1024,192]{1,0:T(8,128)(2,1)S(1)} %get-tuple-element.22.flip_ref, ...), custom_call_target="tpu_custom_call" | custom-call | flops 3276800000 | bytes 12800000 | tf_op jit(solution)/shard_map/near/pallas_call | solution.py:503
  63.5 3.8 %all-to-all-start.1 = ((bf16[16,208,128]{2,1,0:T(8,128)(2,1)}), bf16[16,208,128]{2,1,0:T(8,128)(2,1)S(1)}, u32[]{:S(2)}, u32[]{:S(2)}) async-start(bf16[16,208,128]{2,1,0:T(8,128)(2,1)} %get-tuple-element.31), calls=%async_computation.1 | async-start | bytes 1703936 | tf_op jit(solution)/shard_map/all_to_all | solution.py:634
  67.3 0.0 collective-permute-done.1
  67.4 0.0 collective-permute-done.2
  67.4 0.0 collective-permute-done.3
  67.4 0.0 copy-start.1
  67.4 16.3 %far.1 = (bf16[3,1024,256]{2,1,0:T(8,128)(2,1)}, f32[3,1,256]{2,1,0:T(1,128)S(1)}, f32[3,1,256]{2,1,0:T(1,128)S(1)}) custom-call(bf16[6,208,128]{2,1,0:T(8,128)(2,1)S(1)} %constant_dynamic-update-slice_fusion.rows_ref.far_rows_ref, bf16[1024,192]{1,0:T(8,128)(2,1)S(1)} %get-tuple-element.22.flip_ref, bf16[6250,1024]{1,0:T(8,128)(2,1)} %stored_ref.1, ...), custom_call_target="tpu_custom_call" | custom-call | flops 9830400000 | bytes 12800000 | tf_op jit(solution)/shard_map/far/pallas_call | solution.py:503
  83.7 0.0 all-to-all-done.1.cols_ref
  83.7 0.0 copy-done.1
  83.7 8.8 %peers.1 = f32[8,4,128]{2,1,0:T(4,128)} custom-call(bf16[2,208,128]{2,1,0:T(8,128)(2,1)S(1)} %pad_maximum_fusion.rows_ref.near_rows_ref, bf16[1,1024,256]{2,1,0:T(8,128)(2,1)S(1)} %copy-done.1, f32[1,1,256]{2,1,0:T(1,128)S(1)} %get-tuple-element.25.near_best_ref, f32[1,1,256]{2,1,0:T(1,128)S(1)} %get-tuple-element.26.near_own_ref, ...), custom_call_target="tpu_custom_call" | custom-call | flops 4294967296 | bytes 4194304 | tf_op jit(solution)/shard_map/peers/pallas_call | solution.py:589
  92.6 4.4 %all-to-all-start.2 = ((f32[8,4,128]{2,1,0:T(4,128)}), f32[8,4,128]{2,1,0:T(4,128)S(1)}, u32[]{:S(2)}, u32[]{:S(2)}) async-start(f32[8,4,128]{2,1,0:T(4,128)} %peers.1), calls=%async_computation.2 | async-start | bytes 32768 | tf_op jit(solution)/shard_map/all_to_all | solution.py:640
  96.9 1.0 vectors.1
  98.0 3.7 %all-to-all-done.2 = f32[8,4,128]{2,1,0:T(4,128)S(1)} async-done(((f32[8,4,128]{2,1,0:T(4,128)}), f32[8,4,128]{2,1,0:T(4,128)S(1)}, u32[]{:S(2)}, u32[]{:S(2)}) %all-to-all-start.2) | async-done | bytes 16416 | tf_op jit(solution)/shard_map/all_to_all | solution.py:640
  101.6 0.5 slice_bitcast_fusion
  (5 shorter events, 0.1 us)
Async XLA Ops:
  0.6 49.8 %copy-start = (s32[1,128]{1,0:T(1,128)S(1)}, s32[1,128]{1,0:T(1,128)}, u32[]{:S(2)}) copy-start(s32[1,128]{1,0:T(1,128)} %ids_ref.1) | copy-start | bytes 1540
  50.6 3.1 %collective-permute-start = (bf16[208,128]{1,0:T(8,128)(2,1)S(1)}, bf16[208,128]{1,0:T(8,128)(2,1)S(1)}, u32[]{:S(2)}, u32[]{:S(2)}) collective-permute-start(bf16[208,128]{1,0:T(8,128)(2,1)S(1)} %get-tuple-element.21), channel_id=1, source_target_pairs={{0,1},{1,0},{2,3},{3,2},{4,5},{5,4},{6,7},{7,6},{8,9},{9,8},{10,11... | collective-permute-start | bytes 159752 | tf_op jit(solution)/shard_map/ppermute | solution.py:625
  53.7 13.7 %collective-permute-start.3 = (bf16[2,208,128]{2,1,0:T(8,128)(2,1)S(1)}, bf16[2,208,128]{2,1,0:T(8,128)(2,1)S(1)}, u32[]{:S(2)}, u32[]{:S(2)}) collective-permute-start(bf16[2,208,128]{2,1,0:T(8,128)(2,1)S(1)} %pad_maximum_fusion.rows_ref.near_rows_ref), channel_id=1, source_target_pairs={{6,0},{7,1},{0,2},{1,3},{2,4},{3,5},{4,6},{5,7},{14,8},{15,9},{8,1... | collective-permute-start | bytes 319496 | tf_op jit(solution)/shard_map/ppermute | solution.py:629
  55.1 12.3 %collective-permute-start.2 = (bf16[2,208,128]{2,1,0:T(8,128)(2,1)S(1)}, bf16[2,208,128]{2,1,0:T(8,128)(2,1)S(1)}, u32[]{:S(2)}, u32[]{:S(2)}) collective-permute-start(bf16[2,208,128]{2,1,0:T(8,128)(2,1)S(1)} %pad_maximum_fusion.rows_ref.near_rows_ref), channel_id=1, source_target_pairs={{4,0},{5,1},{6,2},{7,3},{0,4},{1,5},{2,6},{3,7},{12,8},{13,9},{14,... | collective-permute-start | bytes 319496 | tf_op jit(solution)/shard_map/ppermute | solution.py:629
  57.5 9.9 %collective-permute-start.1 = (bf16[2,208,128]{2,1,0:T(8,128)(2,1)S(1)}, bf16[2,208,128]{2,1,0:T(8,128)(2,1)S(1)}, u32[]{:S(2)}, u32[]{:S(2)}) collective-permute-start(bf16[2,208,128]{2,1,0:T(8,128)(2,1)S(1)} %pad_maximum_fusion.rows_ref.near_rows_ref), channel_id=1, source_target_pairs={{2,0},{3,1},{4,2},{5,3},{6,4},{7,5},{0,6},{1,7},{10,8},{11,9},{12,... | collective-permute-start | bytes 319496 | tf_op jit(solution)/shard_map/ppermute | solution.py:629
  63.5 20.2 %all-to-all-start.1 = ((bf16[16,208,128]{2,1,0:T(8,128)(2,1)}), bf16[16,208,128]{2,1,0:T(8,128)(2,1)S(1)}, u32[]{:S(2)}, u32[]{:S(2)}) async-start(bf16[16,208,128]{2,1,0:T(8,128)(2,1)} %get-tuple-element.31), calls=%async_computation.1 | async-start | bytes 1703936 | tf_op jit(solution)/shard_map/all_to_all | solution.py:634
  67.4 16.3 %copy-start.1 = (bf16[1,1024,256]{2,1,0:T(8,128)(2,1)S(1)}, bf16[1,1024,256]{2,1,0:T(8,128)(2,1)}, u32[]{:S(2)}) copy-start(bf16[1,1024,256]{2,1,0:T(8,128)(2,1)} %get-tuple-element.24.near_turned_ref) | copy-start | bytes 1572868
  92.6 9.1 %all-to-all-start.2 = ((f32[8,4,128]{2,1,0:T(4,128)}), f32[8,4,128]{2,1,0:T(4,128)S(1)}, u32[]{:S(2)}, u32[]{:S(2)}) async-start(f32[8,4,128]{2,1,0:T(4,128)} %peers.1), calls=%async_computation.2 | async-start | bytes 32768 | tf_op jit(solution)/shard_map/all_to_all | solution.py:640
